TPU v7x, 32 devices: a whole 2x2x4 slice. The times are simulated.
32 devices in a mesh: groups: 2 (over y), gz: 4 (over x, core), xy: 4 (over z).
Axes of the slice: x: 2, y: 2, z: 4, core: 2. Of those that a mesh axis runs over, the one named last changes fastest.
Arguments:
- features: bfloat16 [16, 32, 32, 128], P(('groups', 'gz'), 'xy'), parts along dimension 0, may hold values from -6 to 6
- species: int32 [16, 32, 32], P(('groups', 'gz'), 'xy'), parts along dimension 0, may hold values from 0 to 7
- sublayer: int32 [16, 32, 32], P(('groups', 'gz'), 'xy'), parts along dimension 0, may hold values from 0 to 1
- offsets: float32 [2, 16, 32, 32], P(None, ('groups', 'gz'), 'xy'), parts along dimension 1, may hold values from 0 to 11
- neighbours: int32 [16, 32, 32, 32], P(('groups', 'gz'), 'xy'), parts along dimension 0, may hold values from 0 to 287
- neighbour_count: int32 [16, 32, 32], P(('groups', 'gz'), 'xy'), parts along dimension 0, may hold values from 16 to 32
- distances: float32 [16, 32, 32, 32], P(('groups', 'gz'), 'xy'), parts along dimension 0, may hold values from 0.8 to 7.8
- species_table: bfloat16 [8, 128], replicated, may hold values from -3 to 3
- charge_weight: bfloat16 [128, 16], replicated, may hold values from -0.5 to 0.5
- radial_in: bfloat16 [8, 64], replicated, may hold values from -2 to 2
- radial_out: bfloat16 [64, 128], replicated, may hold values from -0.75 to 0.75
- update_in: bfloat16 [128, 256], replicated, may hold values from -0.5 to 0.5
- update_out: bfloat16 [256, 128], replicated, may hold values from -0.375 to 0.375
- energy_weight: bfloat16 [128], replicated, may hold values from -0.5 to 0.5
Outputs:
- features_out: bfloat16 [16, 32, 32, 128], P(('groups', 'gz'), 'xy'), parts along dimension 0
- energy: float32 [16, 32, 32], P(('groups', 'gz'), 'xy'), parts along dimension 0
- forces: float32 [2, 16, 32, 32], P(None, ('groups', 'gz'), 'xy'), parts along dimension 1
There are 2 independent parts, one for each index of `groups`. A program takes and returns all parts, laid end to end along the dimension named above; an argument that names none is the same for every part. Nothing has to cross between parts.
Inputs may be any that keep to these rules, and one draw needn't show every extreme that they name: `neighbours`: an entry n names the neighbour at cell offset o = n // 32 (z offset o // 3 - 1, x offset o % 3 - 1) and slot n % 32 of that cell. `neighbour_count`: entries of a list from this count on are padding.
All inputs are finite; a program needn't handle non-finite values.
Results may differ from a plain program's by a relative error of at most 0.0012.
The roundings to bfloat16 on the way count: a program that leaves them out, or rounds other values in their place, can miss the bound.
Values may be sent and summed in bfloat16 or wider, within the bound.
No kernel may reach another device: no remote copies, remote signals or barrier semaphores. Data moves between devices by JAX's collectives and lax.ppermute only.
A program may use at most 64 MiB of HBM per device.

v0:
```python
import math

import jax
import jax.numpy as jnp
from jax import lax
from jax.sharding import PartitionSpec as P

KX = 128
KY = 8


cell_width = 11.0
layer_depth = 5.5
screening = 0.025
smearing = 1.0
coupling = 0.25
cutoff = 8.0
basis_width = 1.0


def carried_in(part, axis, combine, identity, reverse):
    count = lax.axis_size(axis)
    place = lax.axis_index(axis)
    ahead = count - 1 - place if reverse else place
    gathered = jax.tree.map(lambda a: lax.all_gather(a, axis), part)
    state = jax.tree.map(lambda a, e: jnp.zeros_like(a) + jnp.asarray(e, a.dtype), part, identity)

    def one(turn, state):
        source = count - 1 - turn if reverse else turn
        return combine(
            state, jax.tree.map(lambda a: lax.dynamic_index_in_dim(a, source, 0, False), gathered)
        )

    return lax.fori_loop(0, ahead, one, state)


def with_halo(cells, sides, width, closed):
    for axis, dim in sides:
        count = lax.axis_size(axis)
        ends = count if closed else count - 1
        head = lax.slice_in_dim(cells, 0, width, axis=dim)
        tail = lax.slice_in_dim(cells, cells.shape[dim] - width, cells.shape[dim], axis=dim)
        cells = jnp.concatenate(
            [
                lax.ppermute(tail, axis, [(i, (i + 1) % count) for i in range(ends)]),
                cells,
                lax.ppermute(head, axis, [((i + 1) % count, i) for i in range(ends)]),
            ],
            axis=dim,
        )
    return cells


def wave_numbers(wave_index, width_x):
    wave_x = 2.0 * math.pi / width_x * (wave_index // KY - KX // 2).astype(jnp.float32)
    wave_y = 2.0 * math.pi / cell_width * (wave_index % KY - KY // 2).astype(jnp.float32)
    return (wave_x, wave_y)


def wave_factors(wave_x, wave_y, width_x):
    square = wave_x * wave_x + wave_y * wave_y
    screened = jnp.sqrt(square + screening * screening)
    weight = (
        coupling
        * (2.0 * math.pi / (width_x * cell_width))
        * jnp.exp(-0.5 * smearing * smearing * square)
        / screened
    )
    return (screened, weight)


def build_panel(layer_field, wave_x, wave_y, weight):
    cosine = layer_field[:, :, 0] * weight
    sin_part = layer_field[:, :, 1] * weight
    cos_rows = jnp.stack([cosine, wave_x * sin_part, wave_y * sin_part], axis=1)
    sin_rows = jnp.stack([sin_part, -wave_x * cosine, -wave_y * cosine], axis=1)
    field_panel = jnp.stack([cos_rows, sin_rows], axis=3)
    shape = field_panel.shape
    return field_panel.reshape(shape[0], 3 * shape[2], 2, shape[4]).astype(jnp.bfloat16)


def phase_table(coord_x, coord_y, wave_x, wave_y):
    angles = coord_x[..., None] * wave_x + coord_y[..., None] * wave_y
    return jnp.concatenate([jnp.cos(angles), jnp.sin(angles)], axis=-1).astype(jnp.bfloat16)


def combine_sums(earlier, following):
    return (earlier[0] * following[1] + following[0], earlier[1] * following[1])


def layer_panel(moments, first_wave, width_x):
    layers = moments.shape[0]
    wave_count = moments.shape[3]
    wave_index = first_wave + jnp.arange(wave_count, dtype=jnp.int32)
    wave_x, wave_y = wave_numbers(wave_index, width_x)
    screened, weight = wave_factors(wave_x, wave_y, width_x)
    layer_steps = jnp.arange(layers, dtype=jnp.int32)
    layer_gap = jnp.abs(layer_steps[:, None] - layer_steps[None, :]).astype(jnp.float32)
    within = jnp.exp(-screened * layer_depth * layer_gap[:, :, None])
    local_field = jnp.einsum("jmk,mcpk->jcpk", within, moments, precision=lax.Precision.HIGHEST)
    top_sum = local_field[layers - 1]
    bottom_sum = local_field[0]
    span_decay = jnp.exp(-screened * layer_depth * layers)
    identity_pair = (jnp.zeros_like(top_sum), jnp.ones_like(span_decay))
    from_below = carried_in((top_sum, span_decay), "gz", combine_sums, identity_pair, False)[0]
    from_above = carried_in((bottom_sum, span_decay), "gz", combine_sums, identity_pair, True)[0]
    rise_steps = (layer_steps + 1).astype(jnp.float32)
    fall_steps = (layers - layer_steps).astype(jnp.float32)
    rise_factor = jnp.exp(-screened * layer_depth * rise_steps[:, None])[:, None, None, :]
    fall_factor = jnp.exp(-screened * layer_depth * fall_steps[:, None])[:, None, None, :]
    layer_field = local_field + rise_factor * from_below + fall_factor * from_above
    return build_panel(layer_field, wave_x, wave_y, weight)


def edge_messages(gathered, spacing, usable, radial_in, radial_out):
    basis_count = radial_in.shape[0]
    centers = (
        cutoff * jnp.arange(basis_count, dtype=jnp.int32).astype(jnp.float32) / (basis_count - 1)
    )
    radial_basis = jnp.exp(-jnp.square((spacing[..., None] - centers) / basis_width)).astype(
        jnp.bfloat16
    )
    filter_hidden = jax.nn.silu(
        jnp.einsum("xsnb,bh->xsnh", radial_basis, radial_in, preferred_element_type=jnp.float32)
    ).astype(jnp.bfloat16)
    filters = jnp.einsum(
        "xsnh,hf->xsnf", filter_hidden, radial_out, preferred_element_type=jnp.float32
    )
    envelope = jnp.square(1.0 - jnp.square(spacing / cutoff))
    edge_weight = jnp.where(usable, envelope, 0.0)
    return jnp.sum(edge_weight[..., None] * filters * gathered.astype(jnp.float32), axis=2).astype(
        jnp.bfloat16
    )


def shards(
    features,
    species,
    sublayer,
    offsets,
    neighbours,
    neighbour_count,
    distances,
    species_table,
    charge_weight,
    radial_in,
    radial_out,
    update_in,
    update_out,
    energy_weight,
):
    zcells, xcells, slot_count, feature_width = features.shape
    channels = charge_weight.shape[1]
    kind_count = species_table.shape[0]
    atoms_row = xcells * slot_count
    wave_count = KX * KY
    onehot = (species[..., None] == jnp.arange(kind_count, dtype=jnp.int32)).astype(jnp.bfloat16)
    embedded = jnp.einsum(
        "zxsk,kf->zxsf", onehot, species_table, preferred_element_type=jnp.float32
    )
    hidden_start = (features.astype(jnp.float32) + embedded).astype(jnp.bfloat16)
    charges = jnp.einsum(
        "zxsf,fc->zxsc", hidden_start, charge_weight, preferred_element_type=jnp.float32
    ).astype(jnp.bfloat16)
    ghost_rows = with_halo(hidden_start, (("gz", 0),), 1, False)
    extended = with_halo(ghost_rows, (("xy", 1),), 1, True)
    xy_index = lax.axis_index("xy")
    width_x = cell_width * (xcells * lax.axis_size("xy"))
    wave_x, wave_y = wave_numbers(jnp.arange(wave_count, dtype=jnp.int32), width_x)
    cell_x = (xy_index * xcells + jnp.arange(xcells, dtype=jnp.int32)).astype(jnp.float32)
    coord_x = cell_width * cell_x[None, :, None] + offsets[0]
    phases = phase_table(
        coord_x.reshape(zcells, atoms_row), offsets[1].reshape(zcells, atoms_row), wave_x, wave_y
    )
    layer_mask = (sublayer[..., None] == jnp.arange(2, dtype=jnp.int32)).astype(jnp.bfloat16)
    weighted = (layer_mask[..., :, None] * charges[..., None, :]).reshape(
        zcells, atoms_row, 2 * channels
    )
    raw_moments = jnp.einsum("zrp,zrk->zpk", weighted, phases, preferred_element_type=jnp.float32)
    moments = raw_moments.reshape(2 * zcells, channels, 2, wave_count)
    phase_blocks = phases.reshape(zcells, atoms_row, 2, wave_count)
    shared_sums = lax.psum_scatter(moments, "xy", scatter_dimension=3, tiled=True)
    panel_part = layer_panel(shared_sums, xy_index * shared_sums.shape[3], width_x)
    shard_piece = lax.all_gather(panel_part, "xy", axis=3, tiled=True)
    pairs = shard_piece.reshape(zcells, 6 * channels, 2, shard_piece.shape[3])
    evaluated = jnp.einsum(
        "zrpk,zqpk->zrq", phase_blocks, pairs, preferred_element_type=jnp.float32
    )
    evaluated = evaluated.reshape(zcells, xcells, slot_count, 2, 3, channels)
    chosen = jnp.where(
        (sublayer == 0)[..., None, None], evaluated[..., 0, :, :], evaluated[..., 1, :, :]
    )
    charge_values = charges.astype(jnp.float32)
    long_energy = 0.5 * jnp.sum(charge_values * chosen[..., 0, :], axis=-1)
    forces = -jnp.stack(
        [
            jnp.sum(charge_values * chosen[..., 1, :], axis=-1),
            jnp.sum(charge_values * chosen[..., 2, :], axis=-1),
        ]
    )
    region = extended.reshape(-1, feature_width)
    offset_code = neighbours // slot_count
    slot_code = neighbours % slot_count
    z_range = jnp.arange(zcells, dtype=jnp.int32)[:, None, None, None]
    x_range = jnp.arange(xcells, dtype=jnp.int32)[None, :, None, None]
    row_index = (
        (z_range + offset_code // 3) * (xcells + 2) + x_range + offset_code % 3
    ) * slot_count + slot_code
    own_slot = jnp.arange(slot_count, dtype=jnp.int32)[None, None, :, None]
    listed = jnp.arange(neighbours.shape[3], dtype=jnp.int32)
    usable = (listed < neighbour_count[..., None]) & jnp.logical_not(
        (offset_code == 4) & (slot_code == own_slot)
    )
    aggregates = []
    for z_row in range(zcells):
        gathered = jnp.take(region, row_index[z_row].reshape(-1), axis=0).reshape(
            xcells, slot_count, -1, feature_width
        )
        aggregates.append(
            edge_messages(gathered, distances[z_row], usable[z_row], radial_in, radial_out)
        )
    aggregate = jnp.stack(aggregates)
    update_hidden = jax.nn.silu(
        jnp.einsum("zxsf,fh->zxsh", aggregate, update_in, preferred_element_type=jnp.float32)
    ).astype(jnp.bfloat16)
    renewed = hidden_start.astype(jnp.float32) + jnp.einsum(
        "zxsh,hf->zxsf", update_hidden, update_out, preferred_element_type=jnp.float32
    )
    energy = jnp.sum(renewed * energy_weight.astype(jnp.float32), axis=-1) + long_energy
    return (renewed.astype(jnp.bfloat16), energy, forces)


def solution(mesh):
    in_specs = (
        P(("groups", "gz"), "xy", None, None),
        P(("groups", "gz"), "xy", None),
        P(("groups", "gz"), "xy", None),
        P(None, ("groups", "gz"), "xy", None),
        P(("groups", "gz"), "xy", None, None),
        P(("groups", "gz"), "xy", None),
        P(("groups", "gz"), "xy", None, None),
        P(),
        P(),
        P(),
        P(),
        P(),
        P(),
        P(),
    )
    out_specs = (
        P(("groups", "gz"), "xy", None, None),
        P(("groups", "gz"), "xy", None),
        P(None, ("groups", "gz"), "xy", None),
    )
    return jax.shard_map(shards, mesh=mesh, in_specs=in_specs, out_specs=out_specs, check_vma=False)
```

profile of v0, /device:TPU:0, one launch (start us, length us, event | category | flops | bytes accessed | tf_op | source)
XLA Modules:
  0.0 225.5 jit_solution(5195714684004285989)
XLA Ops:
  7.2 0.0 copy-start
  7.2 0.0 all-reduce.3.cloned.1.call-start
  7.3 0.1 add.386
  7.3 0.1 add.387
  7.4 0.7 fusion.110
  8.1 0.1 squeeze.59
  8.2 0.1 mul.572
  8.3 1.2 fusion.15
  9.5 1.0 convolution_convert_fusion
  10.5 0.7 fusion.70
  11.2 0.1 mul.581
  11.3 8.2 %cosine_convert_fusion = (bf16[2,256,1024]{2,1,0:T(8,128)(2,1)S(1)}, bf16[2,256,1024]{2,1,0:T(8,128)(2,1)S(1)}) fusion(f32[1024]{0:T(1024)S(1)} %get-tuple-element.229, f32[2,256]{1,0:T(2,128)S(1)} %mul.572, f32[1024]{0:T(1024)S(1)} %get-tuple-element.228, f32[2,256]{1,0:T(2,128)S(1)} %broadcast_add_fusion), kind=kLoop, calls=%fused_computation.25 | loop fusion | flops 2621440 | bytes 2109440 | tf_op jit(solution)/shard_map/convert.12
  19.6 0.5 fusion.8
  20.0 0.4 reshape.463
  20.5 3.2 %copy.55 = f32[4,16,2,1024]{1,0,2,3:T(4,128)} copy(f32[4,16,2,1024]{3,2,1,0:T(2,128)S(1)} %reshape.463) | data formatting | bytes 1048576 | tf_op jit(solution)/shard_map/reshape | solution.py:180
  23.7 0.0 all-reduce.3.cloned.1.call-update
  23.7 0.0 copy-start.6
  23.7 0.0 copy-start.4
  23.7 0.0 copy-start.7
  23.8 0.0 copy-start.5
  23.8 2.5 %collective-permute-start = (bf16[1,8,32,128]{3,2,1,0:T(8,128)(2,1)S(1)}, bf16[1,8,32,128]{3,2,1,0:T(8,128)(2,1)S(1)}, u32[]{:S(2)}, u32[]{:S(2)}) collective-permute-start(bf16[1,8,32,128]{3,2,1,0:T(8,128)(2,1)S(1)} %get-tuple-element.217), channel_id=1, source_target_pairs={{0,4},{4,8},{8,12},{1,5},{5,9},{9,13},{2,6},{6,10},{10,14},{3,7},{... | collective-permute-start | bytes 196616 | tf_op jit(solution)/shard_map/ppermute | solution.py:45
  26.3 1.3 collective-permute-start.1
  27.7 9.0 %cosine_convert_fusion.1 = (bf16[2,256,1,1024]{3,1,2,0:T(8,128)(2,1)}, bf16[2,256,1,1024]{3,1,2,0:T(8,128)(2,1)}) fusion(f32[1024]{0:T(1024)S(1)} %get-tuple-element.229, f32[2,256]{1,0:T(2,128)S(1)} %mul.572, f32[1024]{0:T(1024)S(1)} %get-tuple-element.228, f32[2,256]{1,0:T(2,128)S(1)} %broadcast_add_fusion), kind=kLoop, calls=%fused_computation.28 | loop fusion | flops 2621440 | bytes 2109440 | tf_op jit(solution)/shard_map/convert.14
  36.7 0.5 fusion.36
  37.3 0.1 reshape_squeeze.6
  37.4 0.1 reshape_squeeze.7
  37.6 0.3 fusion.40
  37.9 0.1 multiply_select_fusion.1
  38.0 0.1 multiply_exponential_fusion.1
  38.1 0.0 collective-permute-done
  38.1 0.0 collective-permute-done.1
  38.1 2.4 %collective-permute-start.2 = (bf16[4,1,32,128]{3,2,1,0:T(8,128)(2,1)S(1)}, bf16[4,1,32,128]{3,2,1,0:T(8,128)(2,1)S(1)}, u32[]{:S(2)}, u32[]{:S(2)}) collective-permute-start(bf16[4,1,32,128]{3,2,1,0:T(8,128)(2,1)S(1)} %get-tuple-element.207), channel_id=1, source_target_pairs={{0,1},{1,2},{2,3},{3,0},{4,5},{5,6},{6,7},{7,4},{8,9},{9,10},{10,1... | collective-permute-start | bytes 98312 | tf_op jit(solution)/shard_map/ppermute | solution.py:45
  40.6 2.1 collective-permute-start.3
  42.7 7.4 %all-gather = f32[4,1,256]{2,1,0:T(1,128)S(1)} all-gather(f32[1,1,256]{2,1,0:T(1,128)S(1)} %exponential_bitcast_fusion), channel_id=1, replica_groups=mesh['groups'=2,'gz'=4,'xy'=4] {'gz'}, dimensions={0}, use_global_device_ids=true | all-gather | bytes 5120 | tf_op jit(solution)/shard_map/all_gather | solution.py:25
  50.1 0.6 dynamic-slice
  51.3 0.0 collective-permute-done.2
  51.3 0.0 collective-permute-done.3
  51.3 0.1 pad_maximum_fusion
  51.4 29.4 %gather_fusion = bf16[8192,128]{1,0:T(8,128)(2,1)} fusion(bf16[1280,128]{1,0:T(8,128)(2,1)S(1)} %bitcast.193, s32[8192]{0:T(1024)S(1)} %fusion.66), kind=kCustom, calls=%fused_computation.clone | custom fusion | bytes 4227072 | tf_op jit(solution)/shard_map/jit(_take)/gather | solution.py:216
  80.8 24.0 %gather_fusion.1 = bf16[8192,128]{1,0:T(8,128)(2,1)S(1)} fusion(bf16[1280,128]{1,0:T(8,128)(2,1)S(1)} %bitcast.194, s32[8192]{0:T(1024)S(1)} %fusion.67), kind=kCustom, calls=%fused_computation.1.clone | custom fusion | bytes 4227072 | tf_op jit(solution)/shard_map/jit(_take)/gather | solution.py:216
  104.9 6.6 %broadcast_select_fusion.1 = bf16[8192,128]{1,0:T(8,128)(2,1)} fusion(bf16[8192,128]{1,0:T(8,128)(2,1)} %gather_fusion, pred[8192]{0:T(1024)(128)(4,1)S(1)} %compare_and_fusion.1), kind=kLoop, calls=%fused_computation.31 | loop fusion | flops 1048576 | bytes 4202496 | tf_op jit(solution)/shard_map/jit(_take)/select_n | solution.py:216
  111.5 5.1 %broadcast_select_fusion = bf16[8192,128]{1,0:T(8,128)(2,1)} fusion(bf16[8192,128]{1,0:T(8,128)(2,1)S(1)} %gather_fusion.1, pred[8192]{0:T(1024)(128)(4,1)S(1)} %compare_and_fusion), kind=kLoop, calls=%fused_computation.30 | loop fusion | flops 1048576 | bytes 4202496 | tf_op jit(solution)/shard_map/jit(_take)/select_n | solution.py:216
  116.6 0.0 copy-done.10
  116.6 3.9 %fusion.3 = bf16[8,32,128]{2,1,0:T(8,128)(2,1)S(1)} fusion(bf16[8,32,32,128]{3,2,1,0:T(8,128)(2,1)} %bitcast.196, f32[8,32,32]{2,1,0:T(8,128)S(1)} %get-tuple-element.199, f32[8]{0:T(128)S(1)} %convert_multiply_fusion.8, f32[8,32,32]{2,1,0:T(8,128)S(1)} %get-tuple-element.203, bf16[64,128]{1,0:T(8,128)(2,1)S(1)} %copy-done.9, bf16[8,64]{1,0:T(8,128)(2,1)S(1)} %copy-done.10), kind=kOutput, calls=%fused_computation.13 | convolution fusion | flops 149651456 | bytes 2245664 | tf_op jit(solution)/shard_map/xsnh,hf->xsnf/dot_general | solution.py:126
  120.5 0.0 copy-start.8
  120.5 2.2 fusion.2
  122.8 1.1 multiply_reduce_fusion
  123.9 59.1 %all-reduce.3.cloned.1.call-done = f32[4,16,2,1024]{1,0,2,3:T(4,128)} async-done(((f32[4,16,2,1024]{1,0,2,3:T(4,128)}), f32[4,16,2,1024]{1,0,2,3:T(4,128)}) %all-reduce.3.cloned.1.call-update) | async-done | bytes 524304
  182.9 3.4 %fusion.16 = f32[256,16,2,4]{1,3,2,0:T(4,128)S(1)} fusion(f32[4,16,2,1024]{1,0,2,3:T(4,128)} %all-reduce.3.cloned.1.call-done, u32[]{:T(128)S(6)} %multiply.24, f32[4,4]{1,0:T(4,128)S(1)} %abs_convert_fusion, f32[256]{0:T(256)S(1)} %negate_multiply_fusion), kind=kOutput, calls=%fused_computation.37 | convolution fusion | flops 1576960 | bytes 1180740 | tf_op jit(solution)/shard_map/jmk,mcpk->jcpk/dot_general | solution.py:100
  186.3 0.4 copy.56
  186.8 5.4 %all_gather.17 = f32[4,16,2,256]{3,1,2,0:T(8,128)S(1)} all-gather(f32[1,16,2,256]{3,1,2,0:T(8,128)S(1)} %get-tuple-element.216), channel_id=1, replica_groups=mesh['groups'=2,'gz'=4,'xy'=4] {'gz'}, dimensions={0}, use_global_device_ids=true | all-gather | bytes 163840 | tf_op jit(solution)/shard_map/all_gather | solution.py:25
  192.2 0.3 while.27
  192.3 0.1 fusion.120
  192.4 0.1 fusion.120
  192.5 0.1 fusion.120
  192.6 5.5 %all_gather.16 = f32[4,16,2,256]{3,1,2,0:T(8,128)S(1)} all-gather(f32[1,16,2,256]{3,1,2,0:T(8,128)S(1)} %get-tuple-element.215), channel_id=1, replica_groups=mesh['groups'=2,'gz'=4,'xy'=4] {'gz'}, dimensions={0}, use_global_device_ids=true | all-gather | bytes 163840 | tf_op jit(solution)/shard_map/all_gather | solution.py:25
  198.3 17.9 %all_gather.18 = bf16[4,48,2,1024]{3,1,0,2:T(8,128)(2,1)S(1)} all-gather(bf16[4,48,2,256]{3,1,0,2:T(8,128)(2,1)S(1)} %pad_maximum_fusion.1), channel_id=1, replica_groups=mesh['groups'=2,'gz'=4,'xy'=4] {'xy'}, dimensions={3}, use_global_device_ids=true | all-gather | bytes 983040 | tf_op jit(solution)/shard_map/all_gather | solution.py:184
  216.2 0.8 fusion.12
  217.0 0.2 reshape.465
  217.2 0.1 fusion.107
  217.3 0.1 fusion.30
  217.4 0.1 fusion.47
  217.5 0.6 maximum_negate_fusion
  218.1 0.6 multiply_add_fusion.3
  (61 shorter events, 0.6 us)
Async XLA Ops:
  7.2 115.6 %copy-start = (bf16[256,128]{1,0:T(8,128)(2,1)S(1)}, bf16[256,128]{1,0:T(8,128)(2,1)}, u32[]{:S(2)}) copy-start(bf16[256,128]{1,0:T(8,128)(2,1)} %param.32) | copy-start | bytes 196612
  7.2 175.8 %all-reduce.3.cloned.1.call-start = ((), (), s32[]{:S(2)}) async-start(), calls=%async_computation | async-start | bytes 8388608
  23.7 13.0 %copy-start.6 = (s32[2,8,32]{2,1,0:T(8,128)S(1)}, s32[2,8,32]{2,1,0:T(8,128)}, u32[]{:S(2)}) copy-start(s32[2,8,32]{2,1,0:T(8,128)} %param.22) | copy-start | bytes 6148
  23.7 13.0 %copy-start.4 = (s32[2,8,32,32]{3,2,1,0:T(8,128)S(1)}, s32[2,8,32,32]{3,2,1,0:T(8,128)}, u32[]{:S(2)}) copy-start(s32[2,8,32,32]{3,2,1,0:T(8,128)} %param.24) | copy-start | bytes 196612
  23.7 13.8 %copy-start.7 = (s32[2,8,32]{2,1,0:T(8,128)S(1)}, s32[2,8,32]{2,1,0:T(8,128)}, u32[]{:S(2)}) copy-start(s32[2,8,32]{2,1,0:T(8,128)} %param.25) | copy-start | bytes 6148
  23.8 14.1 %copy-start.5 = (f32[2,8,32,32]{3,2,1,0:T(8,128)S(1)}, f32[2,8,32,32]{3,2,1,0:T(8,128)}, u32[]{:S(2)}) copy-start(f32[2,8,32,32]{3,2,1,0:T(8,128)} %param.26) | copy-start | bytes 196612
  23.8 14.3 %collective-permute-start = (bf16[1,8,32,128]{3,2,1,0:T(8,128)(2,1)S(1)}, bf16[1,8,32,128]{3,2,1,0:T(8,128)(2,1)S(1)}, u32[]{:S(2)}, u32[]{:S(2)}) collective-permute-start(bf16[1,8,32,128]{3,2,1,0:T(8,128)(2,1)S(1)} %get-tuple-element.217), channel_id=1, source_target_pairs={{0,4},{4,8},{8,12},{1,5},{5,9},{9,13},{2,6},{6,10},{10,14},{3,7},{... | collective-permute-start | bytes 196616 | tf_op jit(solution)/shard_map/ppermute | solution.py:45
  26.3 11.8 %collective-permute-start.1 = (bf16[1,8,32,128]{3,2,1,0:T(8,128)(2,1)S(1)}, bf16[1,8,32,128]{3,2,1,0:T(8,128)(2,1)S(1)}, u32[]{:S(2)}, u32[]{:S(2)}) collective-permute-start(bf16[1,8,32,128]{3,2,1,0:T(8,128)(2,1)S(1)} %get-tuple-element.218), channel_id=1, source_target_pairs={{4,0},{8,4},{12,8},{5,1},{9,5},{13,9},{6,2},{10,6},{14,10},{7,3},{... | collective-permute-start | bytes 196616 | tf_op jit(solution)/shard_map/ppermute | solution.py:47
  36.7 13.4 %copy-start.11 = (bf16[128]{0:T(256)(128)(2,1)S(1)}, bf16[128]{0:T(256)(128)(2,1)}, u32[]{:S(2)}) copy-start(bf16[128]{0:T(256)(128)(2,1)} %param.33) | copy-start | bytes 772
  36.7 13.4 %copy-start.12 = (u32[32]{0:T(128)S(1)}, u32[32]{0:T(128)}, u32[]{:S(2)}) copy-start(u32[32]{0:T(128)} %constant.222) | copy-start | bytes 388
  38.1 13.2 %collective-permute-start.2 = (bf16[4,1,32,128]{3,2,1,0:T(8,128)(2,1)S(1)}, bf16[4,1,32,128]{3,2,1,0:T(8,128)(2,1)S(1)}, u32[]{:S(2)}, u32[]{:S(2)}) collective-permute-start(bf16[4,1,32,128]{3,2,1,0:T(8,128)(2,1)S(1)} %get-tuple-element.207), channel_id=1, source_target_pairs={{0,1},{1,2},{2,3},{3,0},{4,5},{5,6},{6,7},{7,4},{8,9},{9,10},{10,1... | collective-permute-start | bytes 98312 | tf_op jit(solution)/shard_map/ppermute | solution.py:45
  40.6 10.7 %collective-permute-start.3 = (bf16[4,1,32,128]{3,2,1,0:T(8,128)(2,1)S(1)}, bf16[4,1,32,128]{3,2,1,0:T(8,128)(2,1)S(1)}, u32[]{:S(2)}, u32[]{:S(2)}) collective-permute-start(bf16[4,1,32,128]{3,2,1,0:T(8,128)(2,1)S(1)} %get-tuple-element.208), channel_id=1, source_target_pairs={{1,0},{2,1},{3,2},{0,3},{5,4},{6,5},{7,6},{4,7},{9,8},{10,9},{11,1... | collective-permute-start | bytes 98312 | tf_op jit(solution)/shard_map/ppermute | solution.py:47
  111.5 5.1 %copy-start.9 = (bf16[64,128]{1,0:T(8,128)(2,1)S(1)}, bf16[64,128]{1,0:T(8,128)(2,1)}, u32[]{:S(2)}) copy-start(bf16[64,128]{1,0:T(8,128)(2,1)} %param.30) | copy-start | bytes 49156
  111.5 5.1 %copy-start.10 = (bf16[8,64]{1,0:T(8,128)(2,1)S(1)}, bf16[8,64]{1,0:T(8,128)(2,1)}, u32[]{:S(2)}) copy-start(bf16[8,64]{1,0:T(8,128)(2,1)} %param.29) | copy-start | bytes 3076
  116.6 4.0 %copy-start.1 = (bf16[8192,128]{1,0:T(8,128)(2,1)S(1)}, bf16[8192,128]{1,0:T(8,128)(2,1)}, u32[]{:S(2)}) copy-start(bf16[8192,128]{1,0:T(8,128)(2,1)} %broadcast_select_fusion) | copy-start | bytes 6291460
  120.5 2.3 %copy-start.8 = (bf16[128,256]{1,0:T(8,128)(2,1)S(1)}, bf16[128,256]{1,0:T(8,128)(2,1)}, u32[]{:S(2)}) copy-start(bf16[128,256]{1,0:T(8,128)(2,1)} %param.31) | copy-start | bytes 196612
  192.5 23.6 %copy-start.2 = (bf16[2,256,1,1024]{3,1,2,0:T(8,128)(2,1)S(1)}, bf16[2,256,1,1024]{3,1,2,0:T(8,128)(2,1)}, u32[]{:S(2)}) copy-start(bf16[2,256,1,1024]{3,1,2,0:T(8,128)(2,1)} %get-tuple-element.223) | copy-start | bytes 3145732
  192.5 23.6 %copy-start.3 = (bf16[2,256,1,1024]{3,1,2,0:T(8,128)(2,1)S(1)}, bf16[2,256,1,1024]{3,1,2,0:T(8,128)(2,1)}, u32[]{:S(2)}) copy-start(bf16[2,256,1,1024]{3,1,2,0:T(8,128)(2,1)} %get-tuple-element.224) | copy-start | bytes 3145732
Sparse Core Ops, SparseCore 0:
  23.8 159.0 all-reduce.2
where the time goes:
time: 226 us
  local copies, waits for them, and re-layouts  60 us (27%)
  waiting for transfers between devices  59.1 us (26%)
  blocking collectives  36.2 us (16%)
  other arithmetic  32.5 us (14%)
  between operations  15.2 us (7%)
  matrix products  14 us (6%)
  starting transfers between devices  8.4 us (4%)
    unnamed x2, waiting for transfers between devices  59.1 us
    gather x2, local copies, waits for them, and re-layouts, shards(): jnp.take(region, row_index[z_row].reshape(-1), axis=0)  53.5 us
    all_gather x3, blocking collectives, carried_in(): gathered = jax.tree.map(lambda a: lax.all_gather(a, axis), part)  18.4 us
    all_gather x1, blocking collectives, shards(): shard_piece = lax.all_gather(panel_part, 'xy', axis=3, tiled=True)  17.9 us
    another operation x4, other arithmetic  17.2 us
    select_n x2, other arithmetic, shards(): jnp.take(region, row_index[z_row].reshape(-1), axis=0)  11.7 us
    dot_general x2, matrix products, edge_messages(): jnp.einsum('xsnh,hf->xsnf', filter_hidden, radial_out, preferred_element_...  6.18 us
    ppermute x2, starting transfers between devices, with_halo(): lax.ppermute(tail, axis, [(i, (i + 1) % count) for i in range(ends)])  4.98 us
  transfers between devices with their start and end apart: 5, of which 1 were waited for; matrix products, arithmetic and copies ran while one was open for 37% of the time, Pallas kernels for 0%

commit v1 on v0

v1 whole, which is shorter than its diff:
```python
import math

import jax
import jax.numpy as jnp
from jax import lax
from jax.experimental import pallas as pl
from jax.experimental.pallas import tpu as pltpu
from jax.sharding import PartitionSpec as P

KX = 128
KY = 8

cell_width = 11.0
layer_depth = 5.5
screening = 0.025
smearing = 1.0
coupling = 0.25
cutoff = 8.0
basis_width = 1.0

HALF_X = KX // 2
HALF_Y = KY // 2
WAVES = 640

f32 = jnp.float32
bf16 = jnp.bfloat16

SIN_TERMS = (9.99999996e-01, -1.66666580e-01, 8.33305062e-03, -1.98090464e-04, 2.60516628e-06)
COS_TERMS = (9.99999953e-01, -4.99999051e-01, 4.16635789e-02, -1.38536669e-03, 2.31531742e-05)


def nt_dot(a, b):
    return lax.dot_general(a, b, (((1,), (1,)), ((), ())), preferred_element_type=f32)


def nn_dot(a, b):
    return lax.dot_general(a, b, (((1,), (0,)), ((), ())), preferred_element_type=f32)


def tn_dot(a, b):
    return lax.dot_general(a, b, (((0,), (0,)), ((), ())), preferred_element_type=f32)


def polynomial(z, terms):
    value = jnp.full_like(z, terms[-1])
    for term in terms[-2::-1]:
        value = value * z + term
    return value


def cos_sin(angle):
    turns = jnp.floor(angle * (1.0 / (2.0 * math.pi)) + 0.5)
    head = 6.28125
    rest = (angle - turns * head) - turns * (2.0 * math.pi - head)
    half = rest * 0.5
    z = half * half
    s = half * polynomial(z, SIN_TERMS)
    c = polynomial(z, COS_TERMS)
    return 1.0 - 2.0 * (s * s), 2.0 * (s * c)


def wave_row(width_x):
    lane = lax.broadcasted_iota(jnp.int32, (1, WAVES), 1)
    block = lane // HALF_X
    place = lane % HALF_X
    edge = block == 2 * HALF_Y + 1
    minus = (block > 0) & (block % 2 == 0)
    step_x = jnp.where(
        edge, jnp.where(place <= HALF_Y, HALF_X, -HALF_X), jnp.where(minus, -place, place)
    )
    step_y = jnp.where(
        edge, jnp.where(place <= HALF_Y, place, place - HALF_Y), (block + 1) // 2
    )
    inner = (place > 0) | ((block > 0) & (step_y < HALF_Y))
    twice = inner & ((step_y < HALF_Y))
    plain = jnp.where(minus & (place == 0), 0, jnp.where(twice, 2, 1))
    count = jnp.where(edge, jnp.where(place < 2 * HALF_Y, 1, 0), plain).astype(f32)
    wave_x = 2.0 * math.pi / width_x * step_x.astype(f32)
    wave_y = 2.0 * math.pi / cell_width * step_y.astype(f32)
    square = wave_x * wave_x + wave_y * wave_y
    screened = jnp.sqrt(square + screening * screening)
    weight = (
        coupling
        * (2.0 * math.pi / (width_x * cell_width))
        * jnp.exp(-0.5 * smearing * smearing * square)
        / screened
    )
    return wave_x, wave_y, screened, weight * count


def twin(row):
    return jnp.concatenate([row, row], axis=1)


def store_phases(out_ref, lanes, coord_x, coord_y, width_x):
    count = coord_x.shape[1]
    step_x = lax.broadcasted_iota(jnp.int32, (HALF_X + 8, count), 0).astype(f32)
    cos_x, sin_x = cos_sin((2.0 * math.pi / width_x * step_x) * coord_x)
    row = lax.broadcasted_iota(jnp.int32, (2 * HALF_Y, count), 0)
    step_y = jnp.where(row <= HALF_Y, row, row - HALF_Y).astype(f32)
    cos_y, sin_y = cos_sin((2.0 * math.pi / cell_width * step_y) * coord_y)
    main_c, main_s = cos_x[:HALF_X], sin_x[:HALF_X]

    def put(block, cosine, sine):
        rows = cosine.shape[0]
        out_ref[block * HALF_X : block * HALF_X + rows, lanes] = cosine.astype(bf16)
        out_ref[WAVES + block * HALF_X : WAVES + block * HALF_X + rows, lanes] = sine.astype(bf16)

    put(0, main_c, main_s)
    for b in range(1, HALF_Y + 1):
        cb, sb = cos_y[b : b + 1], sin_y[b : b + 1]
        cc, ss, sc, cs = main_c * cb, main_s * sb, main_s * cb, main_c * sb
        put(2 * b - 1, cc - ss, sc + cs)
        put(2 * b, cc + ss, cs - sc)
    edge_c = cos_x[HALF_X : HALF_X + 1]
    edge_s = jnp.where(row <= HALF_Y, sin_x[HALF_X : HALF_X + 1], -sin_x[HALF_X : HALF_X + 1])
    blank = jnp.zeros((HALF_X - 2 * HALF_Y, count), f32)
    put(
        2 * HALF_Y + 1,
        jnp.concatenate([edge_c * cos_y - edge_s * sin_y, blank], axis=0),
        jnp.concatenate([edge_s * cos_y + edge_c * sin_y, blank], axis=0),
    )


def layer_charges(charges, sub):
    return jnp.concatenate(
        [
            jnp.where(sub == 0.0, charges, 0.0).astype(bf16),
            jnp.where(sub == 1.0, charges, 0.0).astype(bf16),
        ],
        axis=0,
    )


def lane_rows(read, cells, slots):
    per = 128 // slots
    cat = jnp.concatenate(
        [read(pl.ds(j, cells // per, stride=per)) for j in range(per)], axis=1
    )
    return jnp.concatenate([cat[q : q + 1] for q in range(cells // per)], axis=1)


def three_parts(value):
    head = value.astype(bf16).astype(f32)
    middle = (value - head).astype(bf16).astype(f32)
    return [head, middle, (value - head) - middle]


def start_kernel(zcells, xcells, slots, place_ref, feat_ref, spec_ref, sub_ref, off_ref, table_ref,
                 cw_ref, hid_ref, msg_ref, right_ref, left_ref):
    cells = zcells * xcells
    atoms = cells * slots
    kinds = table_ref.shape[0]
    spec = lane_rows(lambda rows: spec_ref[rows, :], cells, slots)
    onehot = (lax.broadcasted_iota(jnp.int32, (kinds, atoms), 0) == spec).astype(f32)
    embedded = tn_dot(onehot, table_ref[...].astype(f32))
    hidden = (feat_ref[...].astype(f32) + embedded).astype(bf16)
    hid_ref[...] = hidden
    weight_t = cw_ref[...].astype(f32).T.astype(bf16)
    charges = nt_dot(weight_t, hidden).astype(bf16)
    channels = charges.shape[0]
    sub = lane_rows(lambda rows: sub_ref[rows, :], cells, slots).astype(f32)
    lane_cell = lax.broadcasted_iota(jnp.int32, (1, atoms), 1) // slots % xcells
    cell_x = (place_ref[0] * xcells + lane_cell).astype(f32)
    coord_x = cell_width * cell_x + lane_rows(lambda rows: off_ref[0, rows, :], cells, slots)
    coord_y = lane_rows(lambda rows: off_ref[1, rows, :], cells, slots)
    extra = jnp.concatenate(
        three_parts(coord_x)
        + three_parts(coord_y)
        + [sub, jnp.zeros((16 - 7, atoms), f32)],
        axis=0,
    ).astype(bf16)
    msg_ref[0:channels, :] = charges
    msg_ref[channels : channels + 16, :] = extra
    for ref, column in ((right_ref, xcells - 1), (left_ref, 0)):
        ref[0:channels, :] = charges
        ref[channels : channels + 16, :] = extra
        for z in range(zcells):
            for h in range(slots // 16):
                begin = (z * xcells + column) * slots + 16 * h
                lane = (z * (slots // 16) + h) * 128
                ref[channels + 16 : channels + 32, lane : lane + 128] = hid_ref[
                    begin : begin + 16, :
                ]


def read_atoms(msg_ref, channels, lanes):
    charges = msg_ref[0:channels, lanes].astype(f32)
    extra = msg_ref[channels : channels + 16, lanes].astype(f32)
    coord_x = (extra[0:1] + extra[1:2]) + extra[2:3]
    coord_y = (extra[3:4] + extra[4:5]) + extra[5:6]
    return charges, coord_x, coord_y, extra[6:7]


def own_kernel(zcells, channels, width_x, msg_ref, phase_ref, moment_ref):
    row_atoms = msg_ref.shape[1] // zcells
    for z in range(zcells):
        lanes = slice(z * row_atoms, (z + 1) * row_atoms)
        charges, coord_x, coord_y, sub = read_atoms(msg_ref, channels, lanes)
        store_phases(phase_ref, lanes, coord_x, coord_y, width_x)
        moment_ref[z] = nt_dot(layer_charges(charges, sub), phase_ref[:, lanes])


def slab_kernel(zcells, channels, width_x, slabs, others, place_ref, own_ref, *refs):
    msg_refs = refs[:others]
    moment_ref = refs[others]
    send_refs = refs[others + 1 : others + slabs]
    scratch = refs[others + slabs]
    row_atoms = msg_refs[0].shape[1] // zcells
    for z in range(zcells):
        total = own_ref[z]
        for ref in msg_refs:
            lanes = slice(z * row_atoms, (z + 1) * row_atoms)
            charges, coord_x, coord_y, sub = read_atoms(ref, channels, lanes)
            store_phases(scratch, slice(0, row_atoms), coord_x, coord_y, width_x)
            total = total + nt_dot(layer_charges(charges, sub), scratch[...])
        moment_ref[z] = total
    screened = wave_row(width_x)[2]
    decay = twin(jnp.exp(-screened * layer_depth))
    layers = [
        moment_ref[z, l * channels : (l + 1) * channels, :] for z in range(zcells) for l in range(2)
    ]
    top = layers[0]
    for layer in layers[1:]:
        top = decay * top + layer
    bottom = decay * layers[-1]
    for layer in layers[-2::-1]:
        bottom = decay * (bottom + layer)
    for shift, ref in enumerate(send_refs, start=1):
        ref[...] = jnp.where(place_ref[1] + shift < slabs, top, bottom)


def edge_kernel(zcells, xcells, slots, channels, hid_ref, below_ref, above_ref, left_ref,
                right_ref, near_ref, dist_ref, count_ref, rin_ref, rout_ref, uin_ref, uout_ref,
                ew_ref, out_ref, energy_ref, ext_ref):
    features = hid_ref.shape[1]
    wide = (xcells + 2) * slots
    listed = near_ref.shape[2]
    ext_ref[0] = below_ref[...]
    ext_ref[zcells + 1] = above_ref[...]
    for z in range(zcells):
        ext_ref[z + 1, slots : slots + xcells * slots, :] = hid_ref[
            z * xcells * slots : (z + 1) * xcells * slots, :
        ]
        for h in range(slots // 16):
            lane = (z * (slots // 16) + h) * 128
            ext_ref[z + 1, 16 * h : 16 * h + 16, :] = left_ref[
                channels + 16 : channels + 32, lane : lane + 128
            ]
            ext_ref[z + 1, wide - slots + 16 * h : wide - slots + 16 * h + 16, :] = right_ref[
                channels + 16 : channels + 32, lane : lane + 128
            ]
    rin_t = rin_ref[...].astype(f32).T.astype(bf16)
    rout_t = rout_ref[...].astype(f32).T.astype(bf16)
    uin_t = uin_ref[...].astype(f32).T.astype(bf16)
    basis = rin_ref.shape[0]
    lane_groups = 128 // slots
    chunk_rows = listed // lane_groups
    region = 9 * slots // 2
    centre = (
        cutoff * lax.broadcasted_iota(jnp.int32, (basis, 256), 0).astype(f32) / (basis - 1)
    )
    row_id = lax.broadcasted_iota(jnp.int32, (region, 256), 0)
    lane8 = lax.broadcasted_iota(jnp.int32, (chunk_rows, 128), 1)
    sub8 = lax.broadcasted_iota(jnp.int32, (chunk_rows, 128), 0)
    slot8 = lane8 % slots
    listed8 = (lane8 // slots) * chunk_rows + sub8
    group_lane = lax.broadcasted_iota(jnp.int32, (features, 128), 1) // slots

    def edge_rows(block):
        turned = block.T
        return jnp.concatenate(
            [turned[g * chunk_rows : (g + 1) * chunk_rows] for g in range(lane_groups)], axis=1
        )

    def one_cell(cell):
        z = cell // xcells
        x = cell % xcells
        begin = pl.multiple_of(x * slots, slots)
        rows = jnp.concatenate(
            [ext_ref[z + dz, pl.ds(begin, 3 * slots), :] for dz in range(3)], axis=0
        )
        rows_t = jnp.concatenate(
            [rows[:region].astype(f32).T, rows[region:].astype(f32).T], axis=0
        ).astype(bf16)
        near = edge_rows(near_ref[cell].astype(f32)).astype(jnp.int32)
        dist = edge_rows(dist_ref[cell])
        count = count_ref[pl.ds(cell, 1), :]
        count = jnp.concatenate([count] * lane_groups, axis=1)
        itself = near == 4 * slots + slot8
        usable = (listed8 < count) & jnp.logical_not(itself)
        part = 1.0 - jnp.square(dist * (1.0 / cutoff))
        weight = jnp.where(usable, part * part, 0.0)
        upper = jnp.where(near >= region, 1.0, 0.0)
        index = jnp.where(near >= region, near - region, near)
        total = jnp.zeros((features, 128), f32)
        for q in range(0, chunk_rows, 2):
            def pair(table):
                return jnp.concatenate([table[q : q + 1], table[q + 1 : q + 2]], axis=1)

            onehot = jnp.where(row_id == pair(index), 1.0, 0.0).astype(bf16)
            both = nn_dot(rows_t, onehot)
            gap = (pair(dist) - centre) / basis_width
            radial = jnp.exp(-(gap * gap)).astype(bf16)
            half = 0.5 * nn_dot(rin_t, radial)
            hidden = (half + half * jnp.tanh(half)).astype(bf16)
            filters = nn_dot(rout_t, hidden)
            picked = jnp.where(pair(upper) > 0.5, both[features:], both[:features])
            product = (pair(weight) * filters) * picked
            total = total + (product[:, :128] + product[:, 128:])
        shift = 64
        while shift >= slots:
            total = total + pltpu.roll(total, shift, 1)
            shift //= 2
        return total

    def four_cells(step, carry):
        merged = one_cell(step * lane_groups)
        for g in range(1, lane_groups):
            merged = jnp.where(group_lane == g, one_cell(step * lane_groups + g), merged)
        aggregate = merged.astype(bf16)
        half = 0.5 * nn_dot(uin_t, aggregate)
        hidden = (half + half * jnp.tanh(half)).astype(bf16)
        begin = pl.multiple_of(step * 128, 128)
        renewed = hid_ref[pl.ds(begin, 128), :].astype(f32) + nn_dot(
            hidden.astype(f32).T.astype(bf16), uout_ref[...]
        )
        out_ref[pl.ds(begin, 128), :] = renewed.astype(bf16)
        weighted = renewed * ew_ref[...].astype(f32)
        energy_ref[pl.ds(step, 1), :] = jnp.sum(weighted.T, axis=0, keepdims=True)
        return carry

    lax.fori_loop(0, zcells * xcells // lane_groups, four_cells, 0)


def field_kernel(zcells, xcells, slots, channels, width_x, slabs, place_ref, msg_ref, phase_ref,
                 moment_ref, short_ref, *refs):
    sums = refs[: slabs - 1]
    energy_ref, force_ref = refs[slabs - 1 :]
    wave_x, wave_y, screened, weight = wave_row(width_x)
    decay = twin(jnp.exp(-screened * layer_depth))
    span = decay
    for _ in range(2 * zcells - 1):
        span = span * decay
    place = place_ref[1]
    below = jnp.zeros_like(sums[0][...])
    above = jnp.zeros_like(below)
    for shift in range(slabs - 1, 0, -1):
        below = jnp.where(place >= shift, below * span + sums[shift - 1][...], below)
    for shift in range(1, slabs):
        above = jnp.where(place < shift, above * span + sums[shift - 1][...], above)
    layers = [
        moment_ref[z, l * channels : (l + 1) * channels, :] for z in range(zcells) for l in range(2)
    ]
    down = []
    for layer in layers:
        below = decay * below + layer
        down.append(below)
    up = [above]
    for layer in layers[:0:-1]:
        above = decay * (above + layer)
        up.append(above)
    up = up[::-1]
    row_atoms = xcells * slots
    for z in range(zcells):
        lanes = slice(z * row_atoms, (z + 1) * row_atoms)
        rows = []
        for l in range(2):
            field = down[2 * z + l] + up[2 * z + l]
            cosine = field[:, :WAVES] * weight
            sine = field[:, WAVES:] * weight
            rows.append(jnp.concatenate([cosine, sine], axis=1))
            rows.append(jnp.concatenate([wave_x * sine, -wave_x * cosine], axis=1))
            rows.append(jnp.concatenate([wave_y * sine, -wave_y * cosine], axis=1))
        panel = jnp.concatenate([row.astype(bf16) for row in rows], axis=0)
        evaluated = nn_dot(panel, phase_ref[:, lanes])
        sub = msg_ref[channels : channels + 16, lanes].astype(f32)[6:7]
        chosen = jnp.where(sub == 0.0, evaluated[: 3 * channels], evaluated[3 * channels :])
        charges = msg_ref[0:channels, lanes].astype(f32)
        long_energy = 0.5 * jnp.sum(charges * chosen[:channels], axis=0, keepdims=True)
        force_x = -jnp.sum(charges * chosen[channels : 2 * channels], axis=0, keepdims=True)
        force_y = -jnp.sum(charges * chosen[2 * channels :], axis=0, keepdims=True)
        per = row_atoms // 128
        short = jnp.concatenate(
            [short_ref[z * per + j : z * per + j + 1, :] for j in range(per)], axis=1
        )
        energy = short + long_energy
        for x in range(xcells):
            cell = z * xcells + x
            piece = slice(x * slots, (x + 1) * slots)
            energy_ref[cell : cell + 1, :] = energy[:, piece]
            force_ref[0, cell : cell + 1, :] = force_x[:, piece]
            force_ref[1, cell : cell + 1, :] = force_y[:, piece]


def vmem():
    return pl.BlockSpec(memory_space=pltpu.VMEM)


def smem():
    return pl.BlockSpec(memory_space=pltpu.SMEM)


def shards(
    features,
    species,
    sublayer,
    offsets,
    neighbours,
    neighbour_count,
    distances,
    species_table,
    charge_weight,
    radial_in,
    radial_out,
    update_in,
    update_out,
    energy_weight,
):
    zcells, xcells, slots, width = features.shape
    channels = charge_weight.shape[1]
    listed = neighbours.shape[3]
    cells = zcells * xcells
    atoms = cells * slots
    strips = lax.axis_size("xy")
    slabs = lax.axis_size("gz")
    width_x = cell_width * (xcells * strips)
    place = jnp.stack([lax.axis_index("xy"), lax.axis_index("gz")]).astype(jnp.int32)

    def shape(dims, kind):
        return jax.ShapeDtypeStruct(dims, kind)

    def partial(body, *static):
        def kernel(*refs):
            body(*static, *refs)

        kernel.__name__ = body.__name__
        return kernel

    def cost(flops, data):
        return pl.CostEstimate(flops=flops, bytes_accessed=data, transcendentals=0)

    hidden, message, to_right, to_left = pl.pallas_call(
        partial(start_kernel, zcells, xcells, slots),
        out_shape=(
            shape((atoms, width), bf16),
            shape((channels + 16, atoms), bf16),
            shape((channels + 32, atoms), bf16),
            shape((channels + 32, atoms), bf16),
        ),
        in_specs=[smem()] + [vmem()] * 6,
        out_specs=(vmem(),) * 4,
    )(
        place,
        features.reshape(atoms, width),
        species.reshape(cells, slots),
        sublayer.reshape(cells, slots),
        offsets.reshape(2, cells, slots),
        species_table,
        charge_weight,
    )

    def ring(count, shift):
        return [(i, (i + shift) % count) for i in range(count)]

    from_left = lax.ppermute(to_right, "xy", ring(strips, 1))
    from_right = lax.ppermute(to_left, "xy", ring(strips, strips - 1))
    messages = [from_left, from_right] + [
        lax.ppermute(message, "xy", ring(strips, shift)) for shift in range(2, strips - 1)
    ]

    phases, own_moments = pl.pallas_call(
        partial(own_kernel, zcells, channels, width_x),
        out_shape=(
            shape((2 * WAVES, atoms), bf16),
            shape((zcells, 2 * channels, 2 * WAVES), f32),
        ),
        in_specs=[vmem()],
        out_specs=(vmem(), vmem()),
        cost_estimate=cost(4_000_000_000, 2_000_000),
    )(message)

    slab = pl.pallas_call(
        partial(slab_kernel, zcells, channels, width_x, slabs, len(messages)),
        out_shape=(shape((zcells, 2 * channels, 2 * WAVES), f32),)
        + (shape((channels, 2 * WAVES), f32),) * (slabs - 1),
        in_specs=[smem()] + [vmem()] * (1 + len(messages)),
        out_specs=(vmem(),) * slabs,
        scratch_shapes=[pltpu.VMEM((2 * WAVES, atoms // zcells), bf16)],
        cost_estimate=cost(8_000_000_000, 2_000_000),
    )(place, own_moments, *messages)
    moments = slab[0]

    def column(received, z):
        rows = received[channels + 16 :].reshape(16, -1, width)
        first = z * (slots // 16)
        return jnp.concatenate([rows[:, first + h] for h in range(slots // 16)], axis=0)

    row_atoms = xcells * slots

    def extended(z):
        return jnp.concatenate(
            [
                column(from_left, z),
                hidden[z * row_atoms : (z + 1) * row_atoms],
                column(from_right, z),
            ],
            axis=0,
        )

    below = lax.ppermute(extended(zcells - 1), "gz", [(i, i + 1) for i in range(slabs - 1)])
    above = lax.ppermute(extended(0), "gz", [(i + 1, i) for i in range(slabs - 1)])
    sums = [
        lax.ppermute(slab[shift], "gz", ring(slabs, shift)) for shift in range(1, slabs)
    ]

    features_out, short_energy = pl.pallas_call(
        partial(edge_kernel, zcells, xcells, slots, channels),
        out_shape=(shape((atoms, width), bf16), shape((atoms // 128, 128), f32)),
        in_specs=[vmem()] * 13,
        out_specs=(vmem(), vmem()),
        scratch_shapes=[pltpu.VMEM((zcells + 2, (xcells + 2) * slots, width), bf16)],
        cost_estimate=cost(12_000_000_000, 4_000_000),
    )(
        hidden,
        below,
        above,
        from_left,
        from_right,
        neighbours.reshape(cells, slots, listed),
        distances.reshape(cells, slots, listed),
        neighbour_count.reshape(cells, slots),
        radial_in,
        radial_out,
        update_in,
        update_out,
        energy_weight.reshape(1, width),
    )

    energy, forces = pl.pallas_call(
        partial(field_kernel, zcells, xcells, slots, channels, width_x, slabs),
        out_shape=(shape((cells, slots), f32), shape((2, cells, slots), f32)),
        in_specs=[smem()] + [vmem()] * (4 + len(sums)),
        out_specs=(vmem(), vmem()),
        cost_estimate=cost(3_000_000_000, 3_000_000),
    )(place, message, phases, moments, short_energy, *sums)

    return (
        features_out.reshape(features.shape),
        energy.reshape(species.shape),
        forces.reshape(offsets.shape),
    )


def solution(mesh):
    in_specs = (
        P(("groups", "gz"), "xy", None, None),
        P(("groups", "gz"), "xy", None),
        P(("groups", "gz"), "xy", None),
        P(None, ("groups", "gz"), "xy", None),
        P(("groups", "gz"), "xy", None, None),
        P(("groups", "gz"), "xy", None),
        P(("groups", "gz"), "xy", None, None),
        P(),
        P(),
        P(),
        P(),
        P(),
        P(),
        P(),
    )
    out_specs = (
        P(("groups", "gz"), "xy", None, None),
        P(("groups", "gz"), "xy", None),
        P(None, ("groups", "gz"), "xy", None),
    )
    return jax.shard_map(shards, mesh=mesh, in_specs=in_specs, out_specs=out_specs, check_vma=False)
```

time: 226 us -> 46.5 us (0.21)
  waiting for transfers between devices: 59.1 us -> 0.1 us
  local copies, waits for them, and re-layouts: 60 us -> 3.51 us
  blocking collectives: 36.2 us -> 0 us
  other arithmetic: 32.5 us -> 0.58 us
  Pallas kernels: 0 us -> 24.7 us
  between operations: 15.2 us -> 0.81 us
  matrix products: 14 us -> 0 us
  starting transfers between devices: 8.4 us -> 16.4 us
    unnamed x2 -> x0, waiting for transfers between devices: 59.1 us -> none
    gather x2 -> x0, local copies, waits for them, and re-layouts: 53.5 us -> none  [shards(): jnp.take(region, row_index[z_row].reshape(-1), axis=0)]
    all_gather x4 -> x0, blocking collectives: 36.2 us -> none  [the longest x3 18.4 us: carried_in(): gathered = jax.tree.map(lambda a: lax.all_gather(a, axis), part)]
    pallas_call x0 -> x5, Pallas kernels: none -> 24.7 us  [the longest x1 14.2 us: shards(): pl.pallas_call(partial(edge_kernel, zcells, xcells, slots, channels), out...]
    another operation x7 -> x1, other arithmetic: 17.3 us -> 0.58 us  [shards(): jnp.stack([lax.axis_index('xy'), lax.axis_index('gz')]).astype(jnp.int32)]
    dot_general x8 -> x0, matrix products: 14 us -> none  [the longest x2 6.18 us: edge_messages(): jnp.einsum('xsnh,hf->xsnf', filter_hidden, radial_out, preferred_element_...]
    select_n x4 -> x0, other arithmetic: 11.9 us -> none  [the longest x2 11.7 us: shards(): jnp.take(region, row_index[z_row].reshape(-1), axis=0)]
    ppermute x4 -> x8, starting transfers between devices: 8.36 us -> 16.4 us  [the longest x3 5.93 us: shards(): lax.ppermute(slab[shift], 'gz', ring(slabs, shift))]
  transfers between devices with their start and end apart: 5 -> 8, of which waited for: 1 -> 1; matrix products, arithmetic and copies ran while one was open for 37% -> 0% of each run, Pallas kernels for 0% -> 43%
where the time goes in v1:
time: 46.5 us; the launch traced here: 46.1 us
  Pallas kernels  24.7 us (53%)
  starting transfers between devices  16.4 us (35%)
  local copies, waits for them, and re-layouts  3.51 us (8%)
  between operations  0.81 us (2%)
  other arithmetic  0.58 us (1%)
    pallas_call x1, Pallas kernels, shards(): pl.pallas_call(partial(edge_kernel, zcells, xcells, slots, channels), out...  14.2 us
    ppermute x3, starting transfers between devices, shards(): lax.ppermute(slab[shift], 'gz', ring(slabs, shift))  5.93 us
    ppermute x1, starting transfers between devices, shards(): lax.ppermute(message, 'xy', ring(strips, shift))  4.06 us
    unnamed x25, local copies, waits for them, and re-layouts  3.4 us
    pallas_call x1, Pallas kernels, shards(): pl.pallas_call(partial(slab_kernel, zcells, channels, width_x, slabs, len...  3.37 us
    pallas_call x1, Pallas kernels, shards(): pl.pallas_call(partial(field_kernel, zcells, xcells, slots, channels, wid...  2.61 us
    pallas_call x1, Pallas kernels, shards(): pl.pallas_call(partial(own_kernel, zcells, channels, width_x), out_shape=...  2.44 us
    ppermute x1, starting transfers between devices, shards(): from_right = lax.ppermute(to_left, 'xy', ring(strips, strips - 1))  2.25 us
  transfers between devices with their start and end apart: 8, of which 1 were waited for; matrix products, arithmetic and copies ran while one was open for 0% of the time, Pallas kernels for 43%

profile of v1, /device:TPU:0, one launch (start us, length us, event | category | flops | bytes accessed | tf_op | source)
XLA Modules:
  0.0 46.1 jit_solution(4413064214890500856)
XLA Ops:
  0.6 1.4 %copy.17.refs_6_ = bf16[128,16]{1,0:T(8,128)(2,1)} copy(bf16[128,16]{0,1:T(8,128)(2,1)} %param.22) | data formatting | bytes 8192 | tf_op args[8]
  2.0 0.6 %pad_add_fusion.refs_0_ = s32[2]{0:T(128)} fusion(s32[1]{0:T(128)} %bitcast.1, s32[1]{0:T(128)} %bitcast), kind=kLoop, calls=%fused_computation.18 | loop fusion | flops 2 | bytes 16 | tf_op jit(solution)/shard_map/stack | solution.py:428
  2.6 2.1 %shard_map.157 = (bf16[512,128]{1,0:T(8,128)(2,1)}, bf16[32,512]{1,0:T(8,128)(2,1)}, bf16[48,512]{1,0:T(8,128)(2,1)}, bf16[48,512]{1,0:T(8,128)(2,1)}) custom-call(s32[2]{0:T(128)} %pad_add_fusion.refs_0_, bf16[512,128]{1,0:T(8,128)(2,1)} %bitcast.45, s32[16,32]{1,0:T(8,128)} %bitcast.47, s32[16,32]{1,0:T(8,128)} %bitcast.48, f32[2,16,32]{2,1,0:T(8,128)} %bitcast.46, ...), custom_call_target="tpu_custom_call" | custom-call | tf_op jit(solution)/shard_map/pallas_call | solution.py:443
  4.7 4.1 %collective-permute-start.4 = (bf16[32,512]{1,0:T(8,128)(2,1)}, bf16[32,512]{1,0:T(8,128)(2,1)S(1)}, u32[]{:S(2)}, u32[]{:S(2)}) collective-permute-start(bf16[32,512]{1,0:T(8,128)(2,1)} %get-tuple-element.21.refs_0_.refs_1_), channel_id=1, source_target_pairs={{0,2},{1,3},{2,0},{3,1},{4,6},{5,7},{6,4},{7,5},{8,10},{9,11},{10,... | collective-permute-start | bytes 98312 | tf_op jit(solution)/shard_map/ppermute | solution.py:469
  8.8 1.6 %collective-permute-start = (bf16[48,512]{1,0:T(8,128)(2,1)}, bf16[48,512]{1,0:T(8,128)(2,1)S(1)}, u32[]{:S(2)}, u32[]{:S(2)}) collective-permute-start(bf16[48,512]{1,0:T(8,128)(2,1)} %get-tuple-element.18), channel_id=1, source_target_pairs={{0,1},{1,2},{2,3},{3,0},{4,5},{5,6},{6,7},{7,4},{8,9},{9,10},{10,1... | collective-permute-start | bytes 147464 | tf_op jit(solution)/shard_map/ppermute | solution.py:466
  10.3 0.0 copy-start
  10.3 2.2 %collective-permute-start.1 = (bf16[48,512]{1,0:T(8,128)(2,1)}, bf16[48,512]{1,0:T(8,128)(2,1)S(1)}, u32[]{:S(2)}, u32[]{:S(2)}) collective-permute-start(bf16[48,512]{1,0:T(8,128)(2,1)} %get-tuple-element.19), channel_id=1, source_target_pairs={{0,3},{1,0},{2,1},{3,2},{4,7},{5,4},{6,5},{7,6},{8,11},{9,8},{10,9... | collective-permute-start | bytes 147464 | tf_op jit(solution)/shard_map/ppermute | solution.py:467
  12.6 2.4 %shard_map.159 = (bf16[1280,512]{1,0:T(8,128)(2,1)}, f32[2,32,1280]{2,1,0:T(8,128)}) custom-call(bf16[32,512]{1,0:T(8,128)(2,1)} %get-tuple-element.21.refs_0_.refs_1_), custom_call_target="tpu_custom_call" | custom-call | flops 4000000000 | bytes 2000000 | tf_op jit(solution)/shard_map/pallas_call | solution.py:472
  15.0 0.0 collective-permute-done.refs_3_.refs_2_
  15.0 0.0 copy-start.1
  15.1 0.1 collective-permute-done.1.refs_4_.refs_3_
  15.2 0.0 copy-start.2
  15.3 0.0 copy-done
  15.3 1.3 %collective-permute-start.2 = (bf16[320,128]{1,0:T(8,128)(2,1)S(1)}, bf16[320,128]{1,0:T(8,128)(2,1)S(1)}, u32[]{:S(2)}, u32[]{:S(2)}) collective-permute-start(bf16[320,128]{1,0:T(8,128)(2,1)S(1)} %constant_dynamic-update-slice_fusion), channel_id=1, source_target_pairs={{0,4},{4,8},{8,12},{1,5},{5,9},{9,13},{2,6},{6,10},{10,14},{3,7},{... | collective-permute-start | bytes 245768 | tf_op jit(solution)/shard_map/ppermute | solution.py:511
  16.7 1.3 %collective-permute-start.3 = (bf16[320,128]{1,0:T(8,128)(2,1)S(1)}, bf16[320,128]{1,0:T(8,128)(2,1)S(1)}, u32[]{:S(2)}, u32[]{:S(2)}) collective-permute-start(bf16[320,128]{1,0:T(8,128)(2,1)S(1)} %constant_dynamic-update-slice_fusion.4), channel_id=1, source_target_pairs={{4,0},{8,4},{12,8},{5,1},{9,5},{13,9},{6,2},{10,6},{14,10},{7,3},{... | collective-permute-start | bytes 245768 | tf_op jit(solution)/shard_map/ppermute | solution.py:512
  18.0 0.0 collective-permute-done.4.refs_4_
  18.0 0.0 copy-start.8
  18.0 0.0 copy-done.1
  18.0 0.0 copy-done.2
  18.0 0.6 %copy-done.8 = bf16[32,512]{1,0:T(8,128)(2,1)} copy-done((bf16[32,512]{1,0:T(8,128)(2,1)}, bf16[32,512]{1,0:T(8,128)(2,1)S(1)}, u32[]{:S(2)}) %copy-start.8) | copy-done | bytes 32792
  18.6 3.4 %shard_map.160 = (f32[2,32,1280]{2,1,0:T(8,128)}, f32[16,1280]{1,0:T(8,128)}, f32[16,1280]{1,0:T(8,128)}, f32[16,1280]{1,0:T(8,128)}) custom-call(s32[2]{0:T(128)} %pad_add_fusion.refs_0_, f32[2,32,1280]{2,1,0:T(8,128)} %get-tuple-element.23.refs_1_, bf16[48,512]{1,0:T(8,128)(2,1)} %copy-done.1, bf16[48,512]{1,0:T(8,128)(2,1)} %copy-done.2, ...), custom_call_target="tpu_custom_call" | custom-call | flops 8000000000 | bytes 2000000 | tf_op jit(solution)/shard_map/pallas_call | solution.py:483
  22.0 2.8 %collective-permute-start.5 = (f32[16,1280]{1,0:T(8,128)}, f32[16,1280]{1,0:T(8,128)S(1)}, u32[]{:S(2)}, u32[]{:S(2)}) collective-permute-start(f32[16,1280]{1,0:T(8,128)} %get-tuple-element.26), channel_id=1, source_target_pairs={{0,4},{4,8},{8,12},{12,0},{1,5},{5,9},{9,13},{13,1},{2,6},{6,10},{... | collective-permute-start | bytes 245768 | tf_op jit(solution)/shard_map/ppermute | solution.py:514
  24.8 1.6 %collective-permute-start.6 = (f32[16,1280]{1,0:T(8,128)}, f32[16,1280]{1,0:T(8,128)S(1)}, u32[]{:S(2)}, u32[]{:S(2)}) collective-permute-start(f32[16,1280]{1,0:T(8,128)} %get-tuple-element.27), channel_id=1, source_target_pairs={{0,8},{4,12},{8,0},{12,4},{1,9},{5,13},{9,1},{13,5},{2,10},{6,14},... | collective-permute-start | bytes 245768 | tf_op jit(solution)/shard_map/ppermute | solution.py:514
  26.4 1.5 %collective-permute-start.7 = (f32[16,1280]{1,0:T(8,128)}, f32[16,1280]{1,0:T(8,128)S(1)}, u32[]{:S(2)}, u32[]{:S(2)}) collective-permute-start(f32[16,1280]{1,0:T(8,128)} %get-tuple-element.28), channel_id=1, source_target_pairs={{0,12},{4,0},{8,4},{12,8},{1,13},{5,1},{9,5},{13,9},{2,14},{6,2},{... | collective-permute-start | bytes 245768 | tf_op jit(solution)/shard_map/ppermute | solution.py:514
  27.9 0.0 collective-permute-done.2.refs_1_
  27.9 0.0 copy-start.3
  27.9 0.0 collective-permute-done.3.refs_2_
  27.9 0.0 copy-start.7
  27.9 0.6 %copy-done.3 = bf16[320,128]{1,0:T(8,128)(2,1)} copy-done((bf16[320,128]{1,0:T(8,128)(2,1)}, bf16[320,128]{1,0:T(8,128)(2,1)S(1)}, u32[]{:S(2)}) %copy-start.3) | copy-done | bytes 81944
  28.5 0.0 copy-done.7
  28.6 14.2 %shard_map.158 = (bf16[512,128]{1,0:T(8,128)(2,1)}, f32[4,128]{1,0:T(4,128)}) custom-call(bf16[512,128]{1,0:T(8,128)(2,1)} %get-tuple-element.17.refs_0_, bf16[320,128]{1,0:T(8,128)(2,1)} %copy-done.3, bf16[320,128]{1,0:T(8,128)(2,1)} %copy-done.7, bf16[48,512]{1,0:T(8,128)(2,1)} %copy-done.1, bf16[48,512]{1,0:T(8,128)(2,1)} %copy-done.2, ...), custom_call_target="tpu_custom_call" | custom-call | flops 12000000000 | bytes 4000000 | tf_op jit(solution)/shard_map/pallas_call | solution.py:517
  42.8 0.0 collective-permute-done.5.refs_5_
  42.8 0.0 copy-start.4
  42.8 0.0 collective-permute-done.6.refs_6_
  42.8 0.0 copy-start.5
  42.8 0.0 collective-permute-done.7.refs_7_
  42.8 0.0 copy-start.6
  42.8 0.6 %copy-done.4 = f32[16,1280]{1,0:T(8,128)} copy-done((f32[16,1280]{1,0:T(8,128)}, f32[16,1280]{1,0:T(8,128)S(1)}, u32[]{:S(2)}) %copy-start.4) | copy-done | bytes 81944
  43.4 0.0 copy-done.5
  43.5 0.1 copy-done.6
  43.5 2.6 %shard_map.161 = (f32[16,32]{1,0:T(8,128)}, f32[2,16,32]{2,1,0:T(8,128)}) custom-call(s32[2]{0:T(128)} %pad_add_fusion.refs_0_, bf16[32,512]{1,0:T(8,128)(2,1)} %get-tuple-element.21.refs_0_.refs_1_, bf16[1280,512]{1,0:T(8,128)(2,1)} %get-tuple-element.22.refs_2_, f32[2,32,1280]{2,1,0:T(8,128)} %get-tuple-element.24.refs_3_, ...), custom_call_target="tpu_custom_call" | custom-call | flops 3000000000 | bytes 3000000 | tf_op jit(solution)/shard_map/pallas_call | solution.py:540
  (14 shorter events, 0.2 us)
Async XLA Ops:
  4.7 13.3 %collective-permute-start.4 = (bf16[32,512]{1,0:T(8,128)(2,1)}, bf16[32,512]{1,0:T(8,128)(2,1)S(1)}, u32[]{:S(2)}, u32[]{:S(2)}) collective-permute-start(bf16[32,512]{1,0:T(8,128)(2,1)} %get-tuple-element.21.refs_0_.refs_1_), channel_id=1, source_target_pairs={{0,2},{1,3},{2,0},{3,1},{4,6},{5,7},{6,4},{7,5},{8,10},{9,11},{10,... | collective-permute-start | bytes 98312 | tf_op jit(solution)/shard_map/ppermute | solution.py:469
  8.8 6.3 %collective-permute-start = (bf16[48,512]{1,0:T(8,128)(2,1)}, bf16[48,512]{1,0:T(8,128)(2,1)S(1)}, u32[]{:S(2)}, u32[]{:S(2)}) collective-permute-start(bf16[48,512]{1,0:T(8,128)(2,1)} %get-tuple-element.18), channel_id=1, source_target_pairs={{0,1},{1,2},{2,3},{3,0},{4,5},{5,6},{6,7},{7,4},{8,9},{9,10},{10,1... | collective-permute-start | bytes 147464 | tf_op jit(solution)/shard_map/ppermute | solution.py:466
  10.3 4.9 %copy-start = (bf16[512,128]{1,0:T(8,128)(2,1)S(1)}, bf16[512,128]{1,0:T(8,128)(2,1)}, u32[]{:S(2)}) copy-start(bf16[512,128]{1,0:T(8,128)(2,1)} %get-tuple-element.17.refs_0_) | copy-start | bytes 393220
  10.3 4.8 %collective-permute-start.1 = (bf16[48,512]{1,0:T(8,128)(2,1)}, bf16[48,512]{1,0:T(8,128)(2,1)S(1)}, u32[]{:S(2)}, u32[]{:S(2)}) collective-permute-start(bf16[48,512]{1,0:T(8,128)(2,1)} %get-tuple-element.19), channel_id=1, source_target_pairs={{0,3},{1,0},{2,1},{3,2},{4,7},{5,4},{6,5},{7,6},{8,11},{9,8},{10,9... | collective-permute-start | bytes 147464 | tf_op jit(solution)/shard_map/ppermute | solution.py:467
  15.0 2.9 %copy-start.1 = (bf16[48,512]{1,0:T(8,128)(2,1)}, bf16[48,512]{1,0:T(8,128)(2,1)S(1)}, u32[]{:S(2)}) copy-start(bf16[48,512]{1,0:T(8,128)(2,1)S(1)} %collective-permute-done.refs_3_.refs_2_) | copy-start | bytes 147460
  15.2 2.8 %copy-start.2 = (bf16[48,512]{1,0:T(8,128)(2,1)}, bf16[48,512]{1,0:T(8,128)(2,1)S(1)}, u32[]{:S(2)}) copy-start(bf16[48,512]{1,0:T(8,128)(2,1)S(1)} %collective-permute-done.1.refs_4_.refs_3_) | copy-start | bytes 147460
  15.3 12.6 %collective-permute-start.2 = (bf16[320,128]{1,0:T(8,128)(2,1)S(1)}, bf16[320,128]{1,0:T(8,128)(2,1)S(1)}, u32[]{:S(2)}, u32[]{:S(2)}) collective-permute-start(bf16[320,128]{1,0:T(8,128)(2,1)S(1)} %constant_dynamic-update-slice_fusion), channel_id=1, source_target_pairs={{0,4},{4,8},{8,12},{1,5},{5,9},{9,13},{2,6},{6,10},{10,14},{3,7},{... | collective-permute-start | bytes 245768 | tf_op jit(solution)/shard_map/ppermute | solution.py:511
  16.7 11.2 %collective-permute-start.3 = (bf16[320,128]{1,0:T(8,128)(2,1)S(1)}, bf16[320,128]{1,0:T(8,128)(2,1)S(1)}, u32[]{:S(2)}, u32[]{:S(2)}) collective-permute-start(bf16[320,128]{1,0:T(8,128)(2,1)S(1)} %constant_dynamic-update-slice_fusion.4), channel_id=1, source_target_pairs={{4,0},{8,4},{12,8},{5,1},{9,5},{13,9},{6,2},{10,6},{14,10},{7,3},{... | collective-permute-start | bytes 245768 | tf_op jit(solution)/shard_map/ppermute | solution.py:512
  18.0 0.6 %copy-start.8 = (bf16[32,512]{1,0:T(8,128)(2,1)}, bf16[32,512]{1,0:T(8,128)(2,1)S(1)}, u32[]{:S(2)}) copy-start(bf16[32,512]{1,0:T(8,128)(2,1)S(1)} %collective-permute-done.4.refs_4_) | copy-start | bytes 98308
  22.0 20.8 %collective-permute-start.5 = (f32[16,1280]{1,0:T(8,128)}, f32[16,1280]{1,0:T(8,128)S(1)}, u32[]{:S(2)}, u32[]{:S(2)}) collective-permute-start(f32[16,1280]{1,0:T(8,128)} %get-tuple-element.26), channel_id=1, source_target_pairs={{0,4},{4,8},{8,12},{12,0},{1,5},{5,9},{9,13},{13,1},{2,6},{6,10},{... | collective-permute-start | bytes 245768 | tf_op jit(solution)/shard_map/ppermute | solution.py:514
  24.8 18.0 %collective-permute-start.6 = (f32[16,1280]{1,0:T(8,128)}, f32[16,1280]{1,0:T(8,128)S(1)}, u32[]{:S(2)}, u32[]{:S(2)}) collective-permute-start(f32[16,1280]{1,0:T(8,128)} %get-tuple-element.27), channel_id=1, source_target_pairs={{0,8},{4,12},{8,0},{12,4},{1,9},{5,13},{9,1},{13,5},{2,10},{6,14},... | collective-permute-start | bytes 245768 | tf_op jit(solution)/shard_map/ppermute | solution.py:514
  26.4 16.4 %collective-permute-start.7 = (f32[16,1280]{1,0:T(8,128)}, f32[16,1280]{1,0:T(8,128)S(1)}, u32[]{:S(2)}, u32[]{:S(2)}) collective-permute-start(f32[16,1280]{1,0:T(8,128)} %get-tuple-element.28), channel_id=1, source_target_pairs={{0,12},{4,0},{8,4},{12,8},{1,13},{5,1},{9,5},{13,9},{2,14},{6,2},{... | collective-permute-start | bytes 245768 | tf_op jit(solution)/shard_map/ppermute | solution.py:514
  27.9 0.6 %copy-start.3 = (bf16[320,128]{1,0:T(8,128)(2,1)}, bf16[320,128]{1,0:T(8,128)(2,1)S(1)}, u32[]{:S(2)}) copy-start(bf16[320,128]{1,0:T(8,128)(2,1)S(1)} %collective-permute-done.2.refs_1_) | copy-start | bytes 245764
  27.9 0.7 %copy-start.7 = (bf16[320,128]{1,0:T(8,128)(2,1)}, bf16[320,128]{1,0:T(8,128)(2,1)S(1)}, u32[]{:S(2)}) copy-start(bf16[320,128]{1,0:T(8,128)(2,1)S(1)} %collective-permute-done.3.refs_2_) | copy-start | bytes 245764
  42.8 0.6 %copy-start.4 = (f32[16,1280]{1,0:T(8,128)}, f32[16,1280]{1,0:T(8,128)S(1)}, u32[]{:S(2)}) copy-start(f32[16,1280]{1,0:T(8,128)S(1)} %collective-permute-done.5.refs_5_) | copy-start | bytes 245764
  42.8 0.7 %copy-start.5 = (f32[16,1280]{1,0:T(8,128)}, f32[16,1280]{1,0:T(8,128)S(1)}, u32[]{:S(2)}) copy-start(f32[16,1280]{1,0:T(8,128)S(1)} %collective-permute-done.6.refs_6_) | copy-start | bytes 245764
  42.8 0.7 %copy-start.6 = (f32[16,1280]{1,0:T(8,128)}, f32[16,1280]{1,0:T(8,128)S(1)}, u32[]{:S(2)}) copy-start(f32[16,1280]{1,0:T(8,128)S(1)} %collective-permute-done.7.refs_7_) | copy-start | bytes 245764

commit v2 on v1

--- a/solution.py
+++ b/solution.py
@@ -146,7 +146,7 @@
     return [head, middle, (value - head) - middle]
 
 
-def start_kernel(zcells, xcells, slots, place_ref, feat_ref, spec_ref, sub_ref, off_ref, table_ref,
+def start_kernel(zcells, xcells, slots, feat_ref, spec_ref, sub_ref, off_ref, table_ref,
                  cw_ref, hid_ref, msg_ref, right_ref, left_ref):
     cells = zcells * xcells
     atoms = cells * slots
@@ -156,12 +156,11 @@
     embedded = tn_dot(onehot, table_ref[...].astype(f32))
     hidden = (feat_ref[...].astype(f32) + embedded).astype(bf16)
     hid_ref[...] = hidden
-    weight_t = cw_ref[...].astype(f32).T.astype(bf16)
-    charges = nt_dot(weight_t, hidden).astype(bf16)
+    charges = nt_dot(cw_ref[...], hidden).astype(bf16)
     channels = charges.shape[0]
     sub = lane_rows(lambda rows: sub_ref[rows, :], cells, slots).astype(f32)
     lane_cell = lax.broadcasted_iota(jnp.int32, (1, atoms), 1) // slots % xcells
-    cell_x = (place_ref[0] * xcells + lane_cell).astype(f32)
+    cell_x = (lax.axis_index("xy") * xcells + lane_cell).astype(f32)
     coord_x = cell_width * cell_x + lane_rows(lambda rows: off_ref[0, rows, :], cells, slots)
     coord_y = lane_rows(lambda rows: off_ref[1, rows, :], cells, slots)
     extra = jnp.concatenate(
@@ -201,7 +200,7 @@
         moment_ref[z] = nt_dot(layer_charges(charges, sub), phase_ref[:, lanes])
 
 
-def slab_kernel(zcells, channels, width_x, slabs, others, place_ref, own_ref, *refs):
+def slab_kernel(zcells, channels, width_x, slabs, others, own_ref, *refs):
     msg_refs = refs[:others]
     moment_ref = refs[others]
     send_refs = refs[others + 1 : others + slabs]
@@ -227,17 +226,71 @@
     for layer in layers[-2::-1]:
         bottom = decay * (bottom + layer)
     for shift, ref in enumerate(send_refs, start=1):
-        ref[...] = jnp.where(place_ref[1] + shift < slabs, top, bottom)
-
-
-def edge_kernel(zcells, xcells, slots, channels, hid_ref, below_ref, above_ref, left_ref,
-                right_ref, near_ref, dist_ref, count_ref, rin_ref, rout_ref, uin_ref, uout_ref,
-                ew_ref, out_ref, energy_ref, ext_ref):
+        ref[...] = jnp.where(lax.axis_index("gz") + shift < slabs, top, bottom)
+
+
+def prepare_kernel(slots, near_ref, dist_ref, count_ref, rin_ref, table_ref, weight_ref, filter_ref):
+    cells, _, listed = near_ref.shape
+    basis = rin_ref.shape[0]
+    groups = 128 // slots
+    rows = listed // groups
+    rin_t = (0.5 * rin_ref[...].astype(f32)).T.astype(bf16)
+    centre = (
+        cutoff * lax.broadcasted_iota(jnp.int32, (basis, 256), 0).astype(f32) / (basis - 1)
+    )
+    lane8 = lax.broadcasted_iota(jnp.int32, (rows, 128), 1)
+    slot8 = lane8 % slots
+    listed8 = (lane8 // slots) * rows + lax.broadcasted_iota(jnp.int32, (rows, 128), 0)
+
+    def edge_rows(block):
+        turned = block.T
+        return jnp.concatenate(
+            [turned[g * rows : (g + 1) * rows] for g in range(groups)], axis=1
+        )
+
+    def one_cell(cell, carry):
+        near = edge_rows(near_ref[cell].astype(f32)).astype(jnp.int32)
+        dist = edge_rows(dist_ref[cell])
+        count = jnp.concatenate([count_ref[pl.ds(cell, 1), :]] * groups, axis=1)
+        usable = (listed8 < count) & jnp.logical_not(near == 4 * slots + slot8)
+        part = 1.0 - jnp.square(dist * (1.0 / cutoff))
+        table_ref[cell] = near
+        weight_ref[cell] = jnp.where(usable, part * part, 0.0)
+        for q in range(0, rows, 2):
+            gap = jnp.concatenate([dist[q : q + 1], dist[q + 1 : q + 2]], axis=1) - centre
+            gap = gap / basis_width
+            radial = jnp.exp(-(gap * gap)).astype(bf16)
+            half = nn_dot(rin_t, radial)
+            filter_ref[cell, :, 128 * q : 128 * q + 256] = (half + half * jnp.tanh(half)).astype(
+                bf16
+            )
+        return carry
+
+    lax.fori_loop(0, cells, one_cell, 0, unroll=4)
+
+
+def extend_kernel(zcells, xcells, slots, channels, hid_ref, left_ref, right_ref, top_ref, bottom_ref):
+    count = xcells * slots
+    for ref, z in ((top_ref, zcells - 1), (bottom_ref, 0)):
+        ref[slots : slots + count, :] = hid_ref[z * count : (z + 1) * count, :]
+        for h in range(slots // 16):
+            lane = (z * (slots // 16) + h) * 128
+            rows = slice(channels + 16, channels + 32)
+            ref[16 * h : 16 * h + 16, :] = left_ref[rows, lane : lane + 128]
+            begin = slots + count + 16 * h
+            ref[begin : begin + 16, :] = right_ref[rows, lane : lane + 128]
+
+
+def edge_kernel(zcells, xcells, slots, channels, slabs, hid_ref, below_ref, above_ref, left_ref,
+                right_ref, table_ref, weight_ref, filter_ref, rout_ref, uin_ref, uout_ref, ew_ref,
+                out_ref, energy_ref, ext_ref, rows_a, rows_b, hot_a, hot_b, both_a, both_b, wide_a,
+                wide_b, agg_ref):
     features = hid_ref.shape[1]
     wide = (xcells + 2) * slots
-    listed = near_ref.shape[2]
-    ext_ref[0] = below_ref[...]
-    ext_ref[zcells + 1] = above_ref[...]
+    cells = zcells * xcells
+    place = lax.axis_index("gz")
+    ext_ref[0] = jnp.where(place > 0, below_ref[...], jnp.zeros_like(below_ref))
+    ext_ref[zcells + 1] = jnp.where(place < slabs - 1, above_ref[...], jnp.zeros_like(above_ref))
     for z in range(zcells):
         ext_ref[z + 1, slots : slots + xcells * slots, :] = hid_ref[
             z * xcells * slots : (z + 1) * xcells * slots, :
@@ -250,91 +303,82 @@
             ext_ref[z + 1, wide - slots + 16 * h : wide - slots + 16 * h + 16, :] = right_ref[
                 channels + 16 : channels + 32, lane : lane + 128
             ]
-    rin_t = rin_ref[...].astype(f32).T.astype(bf16)
     rout_t = rout_ref[...].astype(f32).T.astype(bf16)
-    uin_t = uin_ref[...].astype(f32).T.astype(bf16)
-    basis = rin_ref.shape[0]
-    lane_groups = 128 // slots
-    chunk_rows = listed // lane_groups
+    uin_t = (0.5 * uin_ref[...].astype(f32)).T.astype(bf16)
+    groups = 128 // slots
+    chunks = table_ref.shape[1] // 2
     region = 9 * slots // 2
-    centre = (
-        cutoff * lax.broadcasted_iota(jnp.int32, (basis, 256), 0).astype(f32) / (basis - 1)
-    )
-    row_id = lax.broadcasted_iota(jnp.int32, (region, 256), 0)
-    lane8 = lax.broadcasted_iota(jnp.int32, (chunk_rows, 128), 1)
-    sub8 = lax.broadcasted_iota(jnp.int32, (chunk_rows, 128), 0)
-    slot8 = lane8 % slots
-    listed8 = (lane8 // slots) * chunk_rows + sub8
+    row_id = lax.broadcasted_iota(jnp.int32, (16, 256), 0).astype(jnp.int16)
+    one, zero = jnp.ones((16, 256), bf16), jnp.zeros((16, 256), bf16)
     group_lane = lax.broadcasted_iota(jnp.int32, (features, 128), 1) // slots
 
-    def edge_rows(block):
-        turned = block.T
-        return jnp.concatenate(
-            [turned[g * chunk_rows : (g + 1) * chunk_rows] for g in range(lane_groups)], axis=1
-        )
-
-    def one_cell(cell):
+    def pair(table, q):
+        return jnp.concatenate([table[2 * q : 2 * q + 1], table[2 * q + 1 : 2 * q + 2]], axis=1)
+
+    def make_hot(cell, hot_ref, rows_ref):
+        near = table_ref[cell]
+        index = jnp.where(near >= region, near - region, near)
+        for q in range(chunks):
+            column = jnp.broadcast_to(pair(index, q), (16, 256)).astype(jnp.int16)
+            for r in range(0, region, 16):
+                hot_ref[q, r : r + 16, :] = jnp.where(column == row_id + r, one, zero)
         z = cell // xcells
-        x = cell % xcells
-        begin = pl.multiple_of(x * slots, slots)
+        begin = pl.multiple_of(cell % xcells * slots, slots)
         rows = jnp.concatenate(
             [ext_ref[z + dz, pl.ds(begin, 3 * slots), :] for dz in range(3)], axis=0
         )
-        rows_t = jnp.concatenate(
-            [rows[:region].astype(f32).T, rows[region:].astype(f32).T], axis=0
-        ).astype(bf16)
-        near = edge_rows(near_ref[cell].astype(f32)).astype(jnp.int32)
-        dist = edge_rows(dist_ref[cell])
-        count = count_ref[pl.ds(cell, 1), :]
-        count = jnp.concatenate([count] * lane_groups, axis=1)
-        itself = near == 4 * slots + slot8
-        usable = (listed8 < count) & jnp.logical_not(itself)
-        part = 1.0 - jnp.square(dist * (1.0 / cutoff))
-        weight = jnp.where(usable, part * part, 0.0)
-        upper = jnp.where(near >= region, 1.0, 0.0)
-        index = jnp.where(near >= region, near - region, near)
+        rows_ref[:features] = rows[:region].astype(f32).T.astype(bf16)
+        rows_ref[features:] = rows[region:].astype(f32).T.astype(bf16)
+
+    def multiply(cell, hot_ref, rows_ref, both_ref, wide_ref):
+        rows_t = rows_ref[...]
+        for q in range(chunks):
+            both_ref[q] = nn_dot(rows_t, hot_ref[q])
+            wide_ref[q] = nn_dot(rout_t, filter_ref[cell, :, 256 * q : 256 * q + 256])
+
+    def gather_up(cell, both_ref, wide_ref):
+        near = table_ref[cell]
+        weight = weight_ref[cell]
         total = jnp.zeros((features, 128), f32)
-        for q in range(0, chunk_rows, 2):
-            def pair(table):
-                return jnp.concatenate([table[q : q + 1], table[q + 1 : q + 2]], axis=1)
-
-            onehot = jnp.where(row_id == pair(index), 1.0, 0.0).astype(bf16)
-            both = nn_dot(rows_t, onehot)
-            gap = (pair(dist) - centre) / basis_width
-            radial = jnp.exp(-(gap * gap)).astype(bf16)
-            half = 0.5 * nn_dot(rin_t, radial)
-            hidden = (half + half * jnp.tanh(half)).astype(bf16)
-            filters = nn_dot(rout_t, hidden)
-            picked = jnp.where(pair(upper) > 0.5, both[features:], both[:features])
-            product = (pair(weight) * filters) * picked
+        for q in range(chunks):
+            upper = pair(near, q) >= region
+            picked = jnp.where(upper, both_ref[q, features:], both_ref[q, :features])
+            product = (pair(weight, q) * wide_ref[q]) * picked
             total = total + (product[:, :128] + product[:, 128:])
         shift = 64
         while shift >= slots:
             total = total + pltpu.roll(total, shift, 1)
             shift //= 2
-        return total
-
-    def four_cells(step, carry):
-        merged = one_cell(step * lane_groups)
-        for g in range(1, lane_groups):
-            merged = jnp.where(group_lane == g, one_cell(step * lane_groups + g), merged)
-        aggregate = merged.astype(bf16)
-        half = 0.5 * nn_dot(uin_t, aggregate)
-        hidden = (half + half * jnp.tanh(half)).astype(bf16)
-        begin = pl.multiple_of(step * 128, 128)
-        renewed = hid_ref[pl.ds(begin, 128), :].astype(f32) + nn_dot(
-            hidden.astype(f32).T.astype(bf16), uout_ref[...]
-        )
-        out_ref[pl.ds(begin, 128), :] = renewed.astype(bf16)
+        step = cell // groups
+        agg_ref[step] = jnp.where(group_lane == cell % groups, total, agg_ref[step])
+
+    make_hot(0, hot_a, rows_a)
+
+    def two_cells(turn, carry):
+        cell = 2 * turn
+        multiply(cell, hot_a, rows_a, both_a, wide_a)
+        make_hot(cell + 1, hot_b, rows_b)
+        gather_up(jnp.maximum(cell - 1, 0), both_b, wide_b)
+        multiply(cell + 1, hot_b, rows_b, both_b, wide_b)
+        make_hot(jnp.minimum(cell + 2, cells - 1), hot_a, rows_a)
+        gather_up(cell, both_a, wide_a)
+        return carry
+
+    lax.fori_loop(0, cells // 2, two_cells, 0)
+    gather_up(cells - 1, both_b, wide_b)
+
+    for step in range(cells // groups):
+        half = nn_dot(uin_t, agg_ref[step].astype(bf16))
+        hidden = (half + half * jnp.tanh(half)).T.astype(bf16)
+        begin = step * 128
+        renewed = hid_ref[begin : begin + 128, :].astype(f32) + nn_dot(hidden, uout_ref[...])
+        out_ref[begin : begin + 128, :] = renewed.astype(bf16)
         weighted = renewed * ew_ref[...].astype(f32)
-        energy_ref[pl.ds(step, 1), :] = jnp.sum(weighted.T, axis=0, keepdims=True)
-        return carry
-
-    lax.fori_loop(0, zcells * xcells // lane_groups, four_cells, 0)
-
-
-def field_kernel(zcells, xcells, slots, channels, width_x, slabs, place_ref, msg_ref, phase_ref,
-                 moment_ref, short_ref, *refs):
+        energy_ref[step : step + 1, :] = jnp.sum(weighted.T, axis=0, keepdims=True)
+
+
+def field_kernel(zcells, xcells, slots, channels, width_x, slabs, msg_ref, phase_ref, moment_ref,
+                 short_ref, *refs):
     sums = refs[: slabs - 1]
     energy_ref, force_ref = refs[slabs - 1 :]
     wave_x, wave_y, screened, weight = wave_row(width_x)
@@ -342,7 +386,7 @@
     span = decay
     for _ in range(2 * zcells - 1):
         span = span * decay
-    place = place_ref[1]
+    place = lax.axis_index("gz")
     below = jnp.zeros_like(sums[0][...])
     above = jnp.zeros_like(below)
     for shift in range(slabs - 1, 0, -1):
@@ -397,8 +441,34 @@
     return pl.BlockSpec(memory_space=pltpu.VMEM)
 
 
-def smem():
-    return pl.BlockSpec(memory_space=pltpu.SMEM)
+def hbm():
+    return pl.BlockSpec(memory_space=pltpu.HBM)
+
+
+def fetching(body, count):
+    def kernel(*refs):
+        copies, sems = refs[-count - 1 : -1], refs[-1]
+        moves = [
+            pltpu.make_async_copy(refs[i], copies[i], sems.at[i]) for i in range(count)
+        ]
+        for move in moves:
+            move.start()
+        for move in moves:
+            move.wait()
+        body(*copies, *refs[count : -count - 1])
+
+    kernel.__name__ = body.__name__
+    return kernel
+
+
+def held(arrays):
+    return [pltpu.with_memory_space_constraint(a, pltpu.HBM) for a in arrays]
+
+
+def fetch_scratch(arrays):
+    return [pltpu.VMEM(a.shape, a.dtype) for a in arrays] + [
+        pltpu.SemaphoreType.DMA((len(arrays),))
+    ]
 
 
 def shards(
@@ -425,7 +495,6 @@
     strips = lax.axis_size("xy")
     slabs = lax.axis_size("gz")
     width_x = cell_width * (xcells * strips)
-    place = jnp.stack([lax.axis_index("xy"), lax.axis_index("gz")]).astype(jnp.int32)
 
     def shape(dims, kind):
         return jax.ShapeDtypeStruct(dims, kind)
@@ -437,28 +506,33 @@
         kernel.__name__ = body.__name__
         return kernel
 
+    def grant(mebibytes):
+        return pltpu.CompilerParams(vmem_limit_bytes=mebibytes * 1024 * 1024)
+
     def cost(flops, data):
         return pl.CostEstimate(flops=flops, bytes_accessed=data, transcendentals=0)
 
+    inputs = (
+        features.reshape(atoms, width),
+        species.reshape(cells, slots),
+        sublayer.reshape(cells, slots),
+        offsets.reshape(2, cells, slots),
+        species_table,
+        charge_weight.T,
+    )
     hidden, message, to_right, to_left = pl.pallas_call(
-        partial(start_kernel, zcells, xcells, slots),
+        fetching(partial(start_kernel, zcells, xcells, slots), len(inputs)),
         out_shape=(
             shape((atoms, width), bf16),
             shape((channels + 16, atoms), bf16),
             shape((channels + 32, atoms), bf16),
             shape((channels + 32, atoms), bf16),
         ),
-        in_specs=[smem()] + [vmem()] * 6,
+        in_specs=[hbm()] * len(inputs),
         out_specs=(vmem(),) * 4,
-    )(
-        place,
-        features.reshape(atoms, width),
-        species.reshape(cells, slots),
-        sublayer.reshape(cells, slots),
-        offsets.reshape(2, cells, slots),
-        species_table,
-        charge_weight,
-    )
+        scratch_shapes=fetch_scratch(inputs),
+        compiler_params=grant(6),
+    )(*held(inputs))
 
     def ring(count, shift):
         return [(i, (i + shift) % count) for i in range(count)]
@@ -477,49 +551,76 @@
         ),
         in_specs=[vmem()],
         out_specs=(vmem(), vmem()),
+        compiler_params=grant(8),
         cost_estimate=cost(4_000_000_000, 2_000_000),
     )(message)
+
+    rows = listed * slots // 128
+    chunks = rows // 2
+    inputs = (
+        neighbours.reshape(cells, slots, listed),
+        distances.reshape(cells, slots, listed),
+        neighbour_count.reshape(cells, slots),
+        radial_in,
+    )
+    table, weight, filters = pl.pallas_call(
+        fetching(partial(prepare_kernel, slots), len(inputs)),
+        out_shape=(
+            shape((cells, rows, 128), jnp.int32),
+            shape((cells, rows, 128), f32),
+            shape((cells, radial_in.shape[1], rows * 128), bf16),
+        ),
+        in_specs=[hbm()] * len(inputs),
+        out_specs=(vmem(),) * 3,
+        scratch_shapes=fetch_scratch(inputs),
+        compiler_params=grant(10),
+        cost_estimate=cost(6_000_000_000, 4_000_000),
+    )(*held(inputs))
 
     slab = pl.pallas_call(
         partial(slab_kernel, zcells, channels, width_x, slabs, len(messages)),
         out_shape=(shape((zcells, 2 * channels, 2 * WAVES), f32),)
         + (shape((channels, 2 * WAVES), f32),) * (slabs - 1),
-        in_specs=[smem()] + [vmem()] * (1 + len(messages)),
+        in_specs=[vmem()] * (1 + len(messages)),
         out_specs=(vmem(),) * slabs,
         scratch_shapes=[pltpu.VMEM((2 * WAVES, atoms // zcells), bf16)],
+        compiler_params=grant(8),
         cost_estimate=cost(8_000_000_000, 2_000_000),
-    )(place, own_moments, *messages)
+    )(own_moments, *messages)
     moments = slab[0]
 
-    def column(received, z):
-        rows = received[channels + 16 :].reshape(16, -1, width)
-        first = z * (slots // 16)
-        return jnp.concatenate([rows[:, first + h] for h in range(slots // 16)], axis=0)
-
-    row_atoms = xcells * slots
-
-    def extended(z):
-        return jnp.concatenate(
-            [
-                column(from_left, z),
-                hidden[z * row_atoms : (z + 1) * row_atoms],
-                column(from_right, z),
-            ],
-            axis=0,
-        )
-
-    below = lax.ppermute(extended(zcells - 1), "gz", [(i, i + 1) for i in range(slabs - 1)])
-    above = lax.ppermute(extended(0), "gz", [(i + 1, i) for i in range(slabs - 1)])
+    wide = ((xcells + 2) * slots, width)
+    top, bottom = pl.pallas_call(
+        partial(extend_kernel, zcells, xcells, slots, channels),
+        out_shape=(shape(wide, bf16), shape(wide, bf16)),
+        in_specs=[vmem()] * 3,
+        out_specs=(vmem(), vmem()),
+        compiler_params=grant(4),
+    )(hidden, from_left, from_right)
+    below = lax.ppermute(top, "gz", ring(slabs, 1))
+    above = lax.ppermute(bottom, "gz", ring(slabs, slabs - 1))
     sums = [
         lax.ppermute(slab[shift], "gz", ring(slabs, shift)) for shift in range(1, slabs)
     ]
 
     features_out, short_energy = pl.pallas_call(
-        partial(edge_kernel, zcells, xcells, slots, channels),
+        partial(edge_kernel, zcells, xcells, slots, channels, slabs),
         out_shape=(shape((atoms, width), bf16), shape((atoms // 128, 128), f32)),
-        in_specs=[vmem()] * 13,
+        in_specs=[vmem()] * 12,
         out_specs=(vmem(), vmem()),
-        scratch_shapes=[pltpu.VMEM((zcells + 2, (xcells + 2) * slots, width), bf16)],
+        scratch_shapes=[
+            pltpu.VMEM((zcells + 2, (xcells + 2) * slots, width), bf16),
+            pltpu.VMEM((2 * width, 9 * slots // 2), bf16),
+            pltpu.VMEM((2 * width, 9 * slots // 2), bf16),
+            pltpu.VMEM((chunks, 9 * slots // 2, 256), bf16),
+            pltpu.VMEM((chunks, 9 * slots // 2, 256), bf16),
+            pltpu.VMEM((chunks, 2 * width, 256), f32),
+            pltpu.VMEM((chunks, 2 * width, 256), f32),
+            pltpu.VMEM((chunks, width, 256), f32),
+            pltpu.VMEM((chunks, width, 256), f32),
+            pltpu.VMEM((atoms // 128, width, 128), f32),
+        ],
+        compiler_params=grant(16),
         cost_estimate=cost(12_000_000_000, 4_000_000),
     )(
         hidden,
@@ -527,10 +628,9 @@
         above,
         from_left,
         from_right,
-        neighbours.reshape(cells, slots, listed),
-        distances.reshape(cells, slots, listed),
-        neighbour_count.reshape(cells, slots),
-        radial_in,
+        table,
+        weight,
+        filters,
         radial_out,
         update_in,
         update_out,
@@ -540,10 +640,11 @@
     energy, forces = pl.pallas_call(
         partial(field_kernel, zcells, xcells, slots, channels, width_x, slabs),
         out_shape=(shape((cells, slots), f32), shape((2, cells, slots), f32)),
-        in_specs=[smem()] + [vmem()] * (4 + len(sums)),
+        in_specs=[vmem()] * (4 + len(sums)),
         out_specs=(vmem(), vmem()),
+        compiler_params=grant(8),
         cost_estimate=cost(3_000_000_000, 3_000_000),
-    )(place, message, phases, moments, short_energy, *sums)
+    )(message, phases, moments, short_energy, *sums)
 
     return (
         features_out.reshape(features.shape),

time: 46.5 us -> 26.7 us (0.57)
  Pallas kernels: 24.7 us -> 14.8 us
  starting transfers between devices: 16.4 us -> 10.9 us
  local copies, waits for them, and re-layouts: 3.51 us -> 0.02 us
  other arithmetic: 0.58 us -> 0 us
    pallas_call x2 -> x4, Pallas kernels: 16.3 us -> 11.5 us  [the longest x1 6.23 us: shards(): pl.pallas_call(partial(edge_kernel, zcells, xcells, slots, channels, slab...]
    unnamed x25 -> x8, local copies, waits for them, and re-layouts: 3.4 us -> 0.02 us
    ppermute x1, starting transfers between devices: 4.06 us -> 0.95 us  [shards(): lax.ppermute(message, 'xy', ring(strips, shift))]
    ppermute x3, starting transfers between devices: 5.93 us -> 3.01 us  [shards(): lax.ppermute(slab[shift], 'gz', ring(slabs, shift))]
    pallas_call x1, Pallas kernels: 3.37 us -> 1.53 us  [shards(): pl.pallas_call(partial(slab_kernel, zcells, channels, width_x, slabs, len...]
    pallas_call x1, Pallas kernels: 2.44 us -> 0.68 us  [shards(): pl.pallas_call(partial(own_kernel, zcells, channels, width_x), out_shape=...]
    ppermute x1, starting transfers between devices: 1.58 us -> 3.1 us  [shards(): from_left = lax.ppermute(to_right, 'xy', ring(strips, 1))]
    pallas_call x1, Pallas kernels: 2.61 us -> 1.15 us  [shards(): pl.pallas_call(partial(field_kernel, zcells, xcells, slots, channels, wid...]
  transfers between devices with their start and end apart: 8 -> 8, of which waited for: 1 -> 0; matrix products, arithmetic and copies ran while one was open for 0% -> 0% of each run, Pallas kernels for 43% -> 46%
where the time goes in v2:
time: 26.7 us; the launch traced here: 26.6 us
  Pallas kernels  14.8 us (55%)
  starting transfers between devices  10.9 us (41%)
  between operations  0.75 us (3%)
    pallas_call x1, Pallas kernels, shards(): pl.pallas_call(partial(edge_kernel, zcells, xcells, slots, channels, slab...  6.23 us
    pallas_call x1, Pallas kernels, shards(): pl.pallas_call(fetching(partial(prepare_kernel, slots), len(inputs)), out...  3.77 us
    ppermute x1, starting transfers between devices, shards(): from_left = lax.ppermute(to_right, 'xy', ring(strips, 1))  3.1 us
    ppermute x3, starting transfers between devices, shards(): lax.ppermute(slab[shift], 'gz', ring(slabs, shift))  3.01 us
    ppermute x1, starting transfers between devices, shards(): from_right = lax.ppermute(to_left, 'xy', ring(strips, strips - 1))  2.09 us
    ppermute x1, starting transfers between devices, shards(): above = lax.ppermute(bottom, 'gz', ring(slabs, slabs - 1))  1.73 us
    pallas_call x1, Pallas kernels, shards(): pl.pallas_call(partial(slab_kernel, zcells, channels, width_x, slabs, len...  1.53 us
    pallas_call x1, Pallas kernels, shards(): pl.pallas_call(fetching(partial(start_kernel, zcells, xcells, slots), len...  1.45 us
  transfers between devices with their start and end apart: 8, of which 0 were waited for; matrix products, arithmetic and copies ran while one was open for 0% of the time, Pallas kernels for 46%

profile of v2, /device:TPU:0, one launch (start us, length us, event | category | flops | bytes accessed | tf_op | source)
XLA Modules:
  0.0 26.6 jit_solution(200705017768918944)
XLA Ops:
  0.6 1.4 %shard_map.157 = (bf16[512,128]{1,0:T(8,128)(2,1)S(1)}, bf16[32,512]{1,0:T(8,128)(2,1)S(1)}, bf16[48,512]{1,0:T(8,128)(2,1)S(1)}, bf16[48,512]{1,0:T(8,128)(2,1)S(1)}) custom-call(bf16[512,128]{1,0:T(8,128)(2,1)} %bitcast.13, s32[16,32]{1,0:T(8,128)} %bitcast.15, s32[16,32]{1,0:T(8,128)} %bitcast.16, f32[2,16,32]{2,1,0:T(8,128)} %bitcast.14, ...), custom_call_target="tpu_custom_call" | custom-call | tf_op jit(solution)/shard_map/pallas_call | solution.py:523
  2.1 3.1 %collective-permute-start = (bf16[48,512]{1,0:T(8,128)(2,1)S(1)}, bf16[48,512]{1,0:T(8,128)(2,1)S(1)}, u32[]{:S(2)}, u32[]{:S(2)}) collective-permute-start(bf16[48,512]{1,0:T(8,128)(2,1)S(1)} %get-tuple-element.23), channel_id=1, source_target_pairs={{0,1},{1,2},{2,3},{3,0},{4,5},{5,6},{6,7},{7,4},{8,9},{9,10},{10,1... | collective-permute-start | bytes 147464 | tf_op jit(solution)/shard_map/ppermute | solution.py:540
  5.2 2.1 %collective-permute-start.1 = (bf16[48,512]{1,0:T(8,128)(2,1)S(1)}, bf16[48,512]{1,0:T(8,128)(2,1)S(1)}, u32[]{:S(2)}, u32[]{:S(2)}) collective-permute-start(bf16[48,512]{1,0:T(8,128)(2,1)S(1)} %get-tuple-element.24), channel_id=1, source_target_pairs={{0,3},{1,0},{2,1},{3,2},{4,7},{5,4},{6,5},{7,6},{8,11},{9,8},{10,9... | collective-permute-start | bytes 147464 | tf_op jit(solution)/shard_map/ppermute | solution.py:541
  7.3 0.9 %collective-permute-start.4 = (bf16[32,512]{1,0:T(8,128)(2,1)S(1)}, bf16[32,512]{1,0:T(8,128)(2,1)S(1)}, u32[]{:S(2)}, u32[]{:S(2)}) collective-permute-start(bf16[32,512]{1,0:T(8,128)(2,1)S(1)} %get-tuple-element.31.refs_0_), channel_id=1, source_target_pairs={{0,2},{1,3},{2,0},{3,1},{4,6},{5,7},{6,4},{7,5},{8,10},{9,11},{10,... | collective-permute-start | bytes 98312 | tf_op jit(solution)/shard_map/ppermute | solution.py:543
  8.2 3.8 %shard_map.159 = (s32[16,8,128]{2,1,0:T(8,128)S(1)}, f32[16,8,128]{2,1,0:T(8,128)S(1)}, bf16[16,64,1024]{2,1,0:T(8,128)(2,1)S(1)}) custom-call(s32[16,32,32]{2,1,0:T(8,128)} %bitcast.18, f32[16,32,32]{2,1,0:T(8,128)} %bitcast.19, s32[16,32]{1,0:T(8,128)} %bitcast.20, bf16[8,64]{1,0:T(8,128)(2,1)} %refs_3_.1), custom_call_target="tpu_custom_call" | custom-call | flops 6000000000 | bytes 4000000 | tf_op jit(solution)/shard_map/pallas_call | solution.py:566
  12.0 0.7 %shard_map.161 = (bf16[1280,512]{1,0:T(8,128)(2,1)S(1)}, f32[2,32,1280]{2,1,0:T(8,128)S(1)}) custom-call(bf16[32,512]{1,0:T(8,128)(2,1)S(1)} %get-tuple-element.31.refs_0_), custom_call_target="tpu_custom_call" | custom-call | flops 4000000000 | bytes 2000000 | tf_op jit(solution)/shard_map/pallas_call | solution.py:546
  12.7 0.0 collective-permute-done.refs_1_.refs_3_
  12.7 0.0 collective-permute-done.1.refs_2_.refs_4_
  12.7 0.1 collective-permute-start.2
  12.8 1.7 %collective-permute-start.3 = (bf16[320,128]{1,0:T(8,128)(2,1)S(1)}, bf16[320,128]{1,0:T(8,128)(2,1)S(1)}, u32[]{:S(2)}, u32[]{:S(2)}) collective-permute-start(bf16[320,128]{1,0:T(8,128)(2,1)S(1)} %get-tuple-element.26), channel_id=1, source_target_pairs={{0,12},{4,0},{8,4},{12,8},{1,13},{5,1},{9,5},{13,9},{2,14},{6,2},{... | collective-permute-start | bytes 245768 | tf_op jit(solution)/shard_map/ppermute | solution.py:601
  14.5 0.0 collective-permute-done.4.refs_3_
  14.5 0.0 copy-start
  14.5 0.0 copy-start.1
  14.5 0.0 copy-start.2
  14.6 0.0 copy-start.3
  14.6 1.5 %shard_map.162 = (f32[2,32,1280]{2,1,0:T(8,128)S(1)}, f32[16,1280]{1,0:T(8,128)S(1)}, f32[16,1280]{1,0:T(8,128)S(1)}, f32[16,1280]{1,0:T(8,128)S(1)}) custom-call(f32[2,32,1280]{2,1,0:T(8,128)S(1)} %get-tuple-element.33.refs_0_, bf16[48,512]{1,0:T(8,128)(2,1)S(1)} %collective-permute-done.refs_1_.refs_3_, ...), custom_call_target="tpu_custom_call" | custom-call | flops 8000000000 | bytes 2000000 | tf_op jit(solution)/shard_map/pallas_call | solution.py:580
  16.1 0.1 collective-permute-start.5
  16.2 1.6 %collective-permute-start.6 = (f32[16,1280]{1,0:T(8,128)S(1)}, f32[16,1280]{1,0:T(8,128)S(1)}, u32[]{:S(2)}, u32[]{:S(2)}) collective-permute-start(f32[16,1280]{1,0:T(8,128)S(1)} %get-tuple-element.37), channel_id=1, source_target_pairs={{0,8},{4,12},{8,0},{12,4},{1,9},{5,13},{9,1},{13,5},{2,10},{6,14},... | collective-permute-start | bytes 245768 | tf_op jit(solution)/shard_map/ppermute | solution.py:603
  17.7 1.4 %collective-permute-start.7 = (f32[16,1280]{1,0:T(8,128)S(1)}, f32[16,1280]{1,0:T(8,128)S(1)}, u32[]{:S(2)}, u32[]{:S(2)}) collective-permute-start(f32[16,1280]{1,0:T(8,128)S(1)} %get-tuple-element.38), channel_id=1, source_target_pairs={{0,12},{4,0},{8,4},{12,8},{1,13},{5,1},{9,5},{13,9},{2,14},{6,2},{... | collective-permute-start | bytes 245768 | tf_op jit(solution)/shard_map/ppermute | solution.py:603
  19.1 0.0 collective-permute-done.2.refs_1_
  19.1 0.0 collective-permute-done.3.refs_2_
  19.1 0.0 copy-done
  19.1 0.0 copy-done.1
  19.1 0.0 copy-done.2
  19.2 0.0 copy-done.3
  19.2 6.2 %shard_map.160 = (bf16[512,128]{1,0:T(8,128)(2,1)}, f32[4,128]{1,0:T(4,128)S(1)}) custom-call(bf16[512,128]{1,0:T(8,128)(2,1)S(1)} %get-tuple-element.22.refs_0_, bf16[320,128]{1,0:T(8,128)(2,1)S(1)} %collective-permute-done.2.refs_1_, bf16[320,128]{1,0:T(8,128)(2,1)S(1)} %collective-permute-done.3.refs_2_, ...), custom_call_target="tpu_custom_call" | custom-call | flops 12000000000 | bytes 4000000 | tf_op jit(solution)/shard_map/pallas_call | solution.py:606
  25.4 0.0 collective-permute-done.5.refs_4_
  25.4 0.0 collective-permute-done.6.refs_5_
  25.4 0.0 collective-permute-done.7.refs_6_
  25.4 1.2 %shard_map.163 = (f32[16,32]{1,0:T(8,128)}, f32[2,16,32]{2,1,0:T(8,128)}) custom-call(bf16[32,512]{1,0:T(8,128)(2,1)S(1)} %get-tuple-element.31.refs_0_, bf16[1280,512]{1,0:T(8,128)(2,1)S(1)} %get-tuple-element.32.refs_1_, f32[2,32,1280]{2,1,0:T(8,128)S(1)} %get-tuple-element.34.refs_2_, f32[4,128]{1,0:T(4,128)S(1)} %get-tuple-element.35.refs_3_, ...), custom_call_target="tpu_custom_call" | custom-call | flops 3000000000 | bytes 3000000 | tf_op jit(solution)/shard_map/pallas_call | solution.py:640
  (1 shorter events, 0.0 us)
Async XLA Ops:
  2.1 10.6 %collective-permute-start = (bf16[48,512]{1,0:T(8,128)(2,1)S(1)}, bf16[48,512]{1,0:T(8,128)(2,1)S(1)}, u32[]{:S(2)}, u32[]{:S(2)}) collective-permute-start(bf16[48,512]{1,0:T(8,128)(2,1)S(1)} %get-tuple-element.23), channel_id=1, source_target_pairs={{0,1},{1,2},{2,3},{3,0},{4,5},{5,6},{6,7},{7,4},{8,9},{9,10},{10,1... | collective-permute-start | bytes 147464 | tf_op jit(solution)/shard_map/ppermute | solution.py:540
  5.2 7.5 %collective-permute-start.1 = (bf16[48,512]{1,0:T(8,128)(2,1)S(1)}, bf16[48,512]{1,0:T(8,128)(2,1)S(1)}, u32[]{:S(2)}, u32[]{:S(2)}) collective-permute-start(bf16[48,512]{1,0:T(8,128)(2,1)S(1)} %get-tuple-element.24), channel_id=1, source_target_pairs={{0,3},{1,0},{2,1},{3,2},{4,7},{5,4},{6,5},{7,6},{8,11},{9,8},{10,9... | collective-permute-start | bytes 147464 | tf_op jit(solution)/shard_map/ppermute | solution.py:541
  7.3 7.3 %collective-permute-start.4 = (bf16[32,512]{1,0:T(8,128)(2,1)S(1)}, bf16[32,512]{1,0:T(8,128)(2,1)S(1)}, u32[]{:S(2)}, u32[]{:S(2)}) collective-permute-start(bf16[32,512]{1,0:T(8,128)(2,1)S(1)} %get-tuple-element.31.refs_0_), channel_id=1, source_target_pairs={{0,2},{1,3},{2,0},{3,1},{4,6},{5,7},{6,4},{7,5},{8,10},{9,11},{10,... | collective-permute-start | bytes 98312 | tf_op jit(solution)/shard_map/ppermute | solution.py:543
  12.7 6.4 %collective-permute-start.2 = (bf16[320,128]{1,0:T(8,128)(2,1)S(1)}, bf16[320,128]{1,0:T(8,128)(2,1)S(1)}, u32[]{:S(2)}, u32[]{:S(2)}) collective-permute-start(bf16[320,128]{1,0:T(8,128)(2,1)S(1)} %get-tuple-element.25), channel_id=1, source_target_pairs={{0,4},{4,8},{8,12},{12,0},{1,5},{5,9},{9,13},{13,1},{2,6},{6,10},{... | collective-permute-start | bytes 245768 | tf_op jit(solution)/shard_map/ppermute | solution.py:600
  12.8 6.3 %collective-permute-start.3 = (bf16[320,128]{1,0:T(8,128)(2,1)S(1)}, bf16[320,128]{1,0:T(8,128)(2,1)S(1)}, u32[]{:S(2)}, u32[]{:S(2)}) collective-permute-start(bf16[320,128]{1,0:T(8,128)(2,1)S(1)} %get-tuple-element.26), channel_id=1, source_target_pairs={{0,12},{4,0},{8,4},{12,8},{1,13},{5,1},{9,5},{13,9},{2,14},{6,2},{... | collective-permute-start | bytes 245768 | tf_op jit(solution)/shard_map/ppermute | solution.py:601
  14.5 4.6 %copy-start = (bf16[128,256]{1,0:T(8,128)(2,1)S(1)}, bf16[128,256]{1,0:T(8,128)(2,1)}, u32[]{:S(2)}) copy-start(bf16[128,256]{1,0:T(8,128)(2,1)} %refs_9_.1) | copy-start | bytes 196612
  14.5 4.6 %copy-start.1 = (bf16[256,128]{1,0:T(8,128)(2,1)S(1)}, bf16[256,128]{1,0:T(8,128)(2,1)}, u32[]{:S(2)}) copy-start(bf16[256,128]{1,0:T(8,128)(2,1)} %refs_10_.1) | copy-start | bytes 196612
  14.5 4.6 %copy-start.2 = (bf16[64,128]{1,0:T(8,128)(2,1)S(1)}, bf16[64,128]{1,0:T(8,128)(2,1)}, u32[]{:S(2)}) copy-start(bf16[64,128]{1,0:T(8,128)(2,1)} %refs_8_.1) | copy-start | bytes 49156
  14.6 4.6 %copy-start.3 = (bf16[128]{0:T(256)(128)(2,1)S(1)}, bf16[128]{0:T(256)(128)(2,1)}, u32[]{:S(2)}) copy-start(bf16[128]{0:T(256)(128)(2,1)} %param.27) | copy-start | bytes 772
  16.1 9.3 %collective-permute-start.5 = (f32[16,1280]{1,0:T(8,128)S(1)}, f32[16,1280]{1,0:T(8,128)S(1)}, u32[]{:S(2)}, u32[]{:S(2)}) collective-permute-start(f32[16,1280]{1,0:T(8,128)S(1)} %get-tuple-element.36), channel_id=1, source_target_pairs={{0,4},{4,8},{8,12},{12,0},{1,5},{5,9},{9,13},{13,1},{2,6},{6,10},{... | collective-permute-start | bytes 245768 | tf_op jit(solution)/shard_map/ppermute | solution.py:603
  16.2 9.2 %collective-permute-start.6 = (f32[16,1280]{1,0:T(8,128)S(1)}, f32[16,1280]{1,0:T(8,128)S(1)}, u32[]{:S(2)}, u32[]{:S(2)}) collective-permute-start(f32[16,1280]{1,0:T(8,128)S(1)} %get-tuple-element.37), channel_id=1, source_target_pairs={{0,8},{4,12},{8,0},{12,4},{1,9},{5,13},{9,1},{13,5},{2,10},{6,14},... | collective-permute-start | bytes 245768 | tf_op jit(solution)/shard_map/ppermute | solution.py:603
  17.7 7.7 %collective-permute-start.7 = (f32[16,1280]{1,0:T(8,128)S(1)}, f32[16,1280]{1,0:T(8,128)S(1)}, u32[]{:S(2)}, u32[]{:S(2)}) collective-permute-start(f32[16,1280]{1,0:T(8,128)S(1)} %get-tuple-element.38), channel_id=1, source_target_pairs={{0,12},{4,0},{8,4},{12,8},{1,13},{5,1},{9,5},{13,9},{2,14},{6,2},{... | collective-permute-start | bytes 245768 | tf_op jit(solution)/shard_map/ppermute | solution.py:603

commit v3 on v2

--- a/solution.py
+++ b/solution.py
@@ -94,12 +94,30 @@
 
 def store_phases(out_ref, lanes, coord_x, coord_y, width_x):
     count = coord_x.shape[1]
-    step_x = lax.broadcasted_iota(jnp.int32, (HALF_X + 8, count), 0).astype(f32)
-    cos_x, sin_x = cos_sin((2.0 * math.pi / width_x * step_x) * coord_x)
-    row = lax.broadcasted_iota(jnp.int32, (2 * HALF_Y, count), 0)
+    row = lax.broadcasted_iota(jnp.int32, (8, count), 0)
     step_y = jnp.where(row <= HALF_Y, row, row - HALF_Y).astype(f32)
-    cos_y, sin_y = cos_sin((2.0 * math.pi / cell_width * step_y) * coord_y)
-    main_c, main_s = cos_x[:HALF_X], sin_x[:HALF_X]
+    unit_x = 2.0 * math.pi / width_x * row.astype(f32)
+    cosine, sine = cos_sin(
+        jnp.concatenate(
+            [
+                unit_x * coord_x,
+                (8.0 * unit_x) * coord_x,
+                (2.0 * math.pi / cell_width * step_y) * coord_y,
+            ],
+            axis=0,
+        )
+    )
+    fine_c, fine_s = cosine[:8], sine[:8]
+    cos_y, sin_y = cosine[16:], sine[16:]
+    main_c, main_s = [fine_c], [fine_s]
+    for h in range(1, HALF_X // 8):
+        hc, hs = cosine[8 + h : 9 + h], sine[8 + h : 9 + h]
+        main_c.append(hc * fine_c - hs * fine_s)
+        main_s.append(hs * fine_c + hc * fine_s)
+    last_c, last_s = cosine[7 + HALF_X // 8 : 8 + HALF_X // 8], sine[7 + HALF_X // 8 : 8 + HALF_X // 8]
+    edge_c = last_c * cosine[9:10] - last_s * sine[9:10]
+    edge_s = last_s * cosine[9:10] + last_c * sine[9:10]
+    main_c, main_s = jnp.concatenate(main_c, axis=0), jnp.concatenate(main_s, axis=0)
 
     def put(block, cosine, sine):
         rows = cosine.shape[0]
@@ -112,8 +130,7 @@
         cc, ss, sc, cs = main_c * cb, main_s * sb, main_s * cb, main_c * sb
         put(2 * b - 1, cc - ss, sc + cs)
         put(2 * b, cc + ss, cs - sc)
-    edge_c = cos_x[HALF_X : HALF_X + 1]
-    edge_s = jnp.where(row <= HALF_Y, sin_x[HALF_X : HALF_X + 1], -sin_x[HALF_X : HALF_X + 1])
+    edge_s = jnp.where(row <= HALF_Y, edge_s, -edge_s)
     blank = jnp.zeros((HALF_X - 2 * HALF_Y, count), f32)
     put(
         2 * HALF_Y + 1,
@@ -147,7 +164,7 @@
 
 
 def start_kernel(zcells, xcells, slots, feat_ref, spec_ref, sub_ref, off_ref, table_ref,
-                 cw_ref, hid_ref, msg_ref, right_ref, left_ref):
+                 cw_ref, hid_ref, msg_ref, even_ref, odd_ref):
     cells = zcells * xcells
     atoms = cells * slots
     kinds = table_ref.shape[0]
@@ -171,15 +188,17 @@
     ).astype(bf16)
     msg_ref[0:channels, :] = charges
     msg_ref[channels : channels + 16, :] = extra
-    for ref, column in ((right_ref, xcells - 1), (left_ref, 0)):
+    even = lax.axis_index("xy") % 2 == 0
+    right = xcells - 1
+    for ref, column in ((even_ref, jnp.where(even, right, 0)), (odd_ref, jnp.where(even, 0, right))):
         ref[0:channels, :] = charges
         ref[channels : channels + 16, :] = extra
         for z in range(zcells):
             for h in range(slots // 16):
-                begin = (z * xcells + column) * slots + 16 * h
+                begin = pl.multiple_of((z * xcells + column) * slots + 16 * h, 16)
                 lane = (z * (slots // 16) + h) * 128
                 ref[channels + 16 : channels + 32, lane : lane + 128] = hid_ref[
-                    begin : begin + 16, :
+                    pl.ds(begin, 16), :
                 ]
 
 
@@ -191,13 +210,96 @@
     return charges, coord_x, coord_y, extra[6:7]
 
 
-def own_kernel(zcells, channels, width_x, msg_ref, phase_ref, moment_ref):
+def own_kernel(zcells, channels, width_x, slots, near_hbm, dist_hbm, count_hbm, rin_hbm, msg_ref,
+               phase_ref, moment_ref, table_ref, weight_ref, filter_ref, near_ref, dist_ref,
+               count_ref, rin_ref, rad_a, rad_b, sems):
+    moves = [
+        pltpu.make_async_copy(source, target, sems.at[i])
+        for i, (source, target) in enumerate(
+            (
+                (near_hbm, near_ref),
+                (dist_hbm, dist_ref),
+                (count_hbm, count_ref),
+                (rin_hbm, rin_ref),
+            )
+        )
+    ]
+    for move in moves:
+        move.start()
     row_atoms = msg_ref.shape[1] // zcells
     for z in range(zcells):
         lanes = slice(z * row_atoms, (z + 1) * row_atoms)
         charges, coord_x, coord_y, sub = read_atoms(msg_ref, channels, lanes)
         store_phases(phase_ref, lanes, coord_x, coord_y, width_x)
         moment_ref[z] = nt_dot(layer_charges(charges, sub), phase_ref[:, lanes])
+    for move in moves:
+        move.wait()
+
+    cells, _, listed = near_ref.shape
+    basis = rin_ref.shape[0]
+    groups = 128 // slots
+    rows = listed // groups
+    rin_t = (0.5 * rin_ref[...].astype(f32)).T.astype(bf16)
+    centre = (
+        cutoff * lax.broadcasted_iota(jnp.int32, (basis, 128), 0).astype(f32) / (basis - 1)
+    )
+    lane8 = lax.broadcasted_iota(jnp.int32, (rows, 128), 1)
+    slot8 = lane8 % slots
+    listed8 = (lane8 // slots) * rows + lax.broadcasted_iota(jnp.int32, (rows, 128), 0)
+
+    def edge_rows(block):
+        turned = block.T
+        return jnp.concatenate(
+            [turned[g * rows : (g + 1) * rows] for g in range(groups)], axis=1
+        )
+
+    def spread(cell, rad_ref, slot):
+        near = edge_rows(near_ref[cell].astype(f32)).astype(jnp.int32)
+        dist = edge_rows(dist_ref[cell])
+        count = jnp.concatenate([count_ref[pl.ds(cell, 1), :]] * groups, axis=1)
+        usable = (listed8 < count) & jnp.logical_not(near == 4 * slots + slot8)
+        part = 1.0 - jnp.square(dist * (1.0 / cutoff))
+        table_ref[cell] = near
+        weight_ref[cell] = jnp.where(usable, part * part, 0.0)
+        for q in range(rows):
+            gap = (dist[q : q + 1] - centre) / basis_width
+            rad_ref[slot, :, 128 * q : 128 * q + 128] = jnp.exp(-(gap * gap)).astype(bf16)
+
+    def filtered(cell, rad_ref, slot):
+        for q in range(0, rows * 128, 256):
+            half = nn_dot(rin_t, rad_ref[slot, :, q : q + 256])
+            filter_ref[cell, :, q : q + 256] = (half + half * jnp.tanh(half)).astype(bf16)
+
+    for slot in range(2):
+        spread(slot, rad_a, slot)
+
+    def four_cells(turn, carry):
+        cell = 4 * turn
+        for slot in range(2):
+            filtered(cell + slot, rad_a, slot)
+            spread(cell + 2 + slot, rad_b, slot)
+        for slot in range(2):
+            filtered(cell + 2 + slot, rad_b, slot)
+            spread(jnp.minimum(cell + 4 + slot, cells - 1), rad_a, slot)
+        return carry
+
+    lax.fori_loop(0, cells // 4, four_cells, 0)
+
+
+def targets(place, count):
+    even = place % 2 == 0
+    above, below = (place + 1) % count, (place + count - 1) % count
+    return [jnp.where(even, above, below), jnp.where(even, below, above)] + [
+        (place + shift) % count for shift in range(2, count - 1)
+    ]
+
+
+def routes(count):
+    even = [(i, i + 1 if i % 2 == 0 else i - 1) for i in range(count)]
+    odd = [(i, (i + 1) % count if i % 2 == 1 else (i - 1) % count) for i in range(count)]
+    return [even, odd] + [
+        [(i, (i + shift) % count) for i in range(count)] for shift in range(2, count - 1)
+    ]
 
 
 def slab_kernel(zcells, channels, width_x, slabs, others, own_ref, *refs):
@@ -225,86 +327,52 @@
     bottom = decay * layers[-1]
     for layer in layers[-2::-1]:
         bottom = decay * (bottom + layer)
-    for shift, ref in enumerate(send_refs, start=1):
-        ref[...] = jnp.where(lax.axis_index("gz") + shift < slabs, top, bottom)
-
-
-def prepare_kernel(slots, near_ref, dist_ref, count_ref, rin_ref, table_ref, weight_ref, filter_ref):
-    cells, _, listed = near_ref.shape
-    basis = rin_ref.shape[0]
-    groups = 128 // slots
-    rows = listed // groups
-    rin_t = (0.5 * rin_ref[...].astype(f32)).T.astype(bf16)
-    centre = (
-        cutoff * lax.broadcasted_iota(jnp.int32, (basis, 256), 0).astype(f32) / (basis - 1)
-    )
-    lane8 = lax.broadcasted_iota(jnp.int32, (rows, 128), 1)
-    slot8 = lane8 % slots
-    listed8 = (lane8 // slots) * rows + lax.broadcasted_iota(jnp.int32, (rows, 128), 0)
-
-    def edge_rows(block):
-        turned = block.T
-        return jnp.concatenate(
-            [turned[g * rows : (g + 1) * rows] for g in range(groups)], axis=1
+    place = lax.axis_index("gz")
+    for target, ref in zip(targets(place, slabs), send_refs):
+        ref[...] = jnp.where(target > place, top, bottom)
+
+
+def sides(even_ref, odd_ref, rows, lanes):
+    first, second = even_ref[rows, lanes], odd_ref[rows, lanes]
+    even = lax.axis_index("xy") % 2 == 0
+    return jnp.where(even, second, first), jnp.where(even, first, second)
+
+
+def fill_row(ref, z, xcells, slots, channels, hid_ref, even_ref, odd_ref):
+    count = xcells * slots
+    ref[slots : slots + count, :] = hid_ref[z * count : (z + 1) * count, :]
+    for h in range(slots // 16):
+        lane = (z * (slots // 16) + h) * 128
+        left, right = sides(
+            even_ref, odd_ref, slice(channels + 16, channels + 32), slice(lane, lane + 128)
         )
-
-    def one_cell(cell, carry):
-        near = edge_rows(near_ref[cell].astype(f32)).astype(jnp.int32)
-        dist = edge_rows(dist_ref[cell])
-        count = jnp.concatenate([count_ref[pl.ds(cell, 1), :]] * groups, axis=1)
-        usable = (listed8 < count) & jnp.logical_not(near == 4 * slots + slot8)
-        part = 1.0 - jnp.square(dist * (1.0 / cutoff))
-        table_ref[cell] = near
-        weight_ref[cell] = jnp.where(usable, part * part, 0.0)
-        for q in range(0, rows, 2):
-            gap = jnp.concatenate([dist[q : q + 1], dist[q + 1 : q + 2]], axis=1) - centre
-            gap = gap / basis_width
-            radial = jnp.exp(-(gap * gap)).astype(bf16)
-            half = nn_dot(rin_t, radial)
-            filter_ref[cell, :, 128 * q : 128 * q + 256] = (half + half * jnp.tanh(half)).astype(
-                bf16
-            )
-        return carry
-
-    lax.fori_loop(0, cells, one_cell, 0, unroll=4)
-
-
-def extend_kernel(zcells, xcells, slots, channels, hid_ref, left_ref, right_ref, top_ref, bottom_ref):
-    count = xcells * slots
-    for ref, z in ((top_ref, zcells - 1), (bottom_ref, 0)):
-        ref[slots : slots + count, :] = hid_ref[z * count : (z + 1) * count, :]
-        for h in range(slots // 16):
-            lane = (z * (slots // 16) + h) * 128
-            rows = slice(channels + 16, channels + 32)
-            ref[16 * h : 16 * h + 16, :] = left_ref[rows, lane : lane + 128]
-            begin = slots + count + 16 * h
-            ref[begin : begin + 16, :] = right_ref[rows, lane : lane + 128]
-
-
-def edge_kernel(zcells, xcells, slots, channels, slabs, hid_ref, below_ref, above_ref, left_ref,
-                right_ref, table_ref, weight_ref, filter_ref, rout_ref, uin_ref, uout_ref, ew_ref,
-                out_ref, energy_ref, ext_ref, rows_a, rows_b, hot_a, hot_b, both_a, both_b, wide_a,
-                wide_b, agg_ref):
-    features = hid_ref.shape[1]
-    wide = (xcells + 2) * slots
+        ref[16 * h : 16 * h + 16, :] = left
+        begin = slots + count + 16 * h
+        ref[begin : begin + 16, :] = right
+
+
+def extend_kernel(zcells, xcells, slots, channels, hid_ref, even_ref, odd_ref, first_ref,
+                  second_ref, ext_ref):
+    for z in range(zcells):
+        fill_row(ext_ref.at[z], z, xcells, slots, channels, hid_ref, even_ref, odd_ref)
+    even = lax.axis_index("gz") % 2 == 0
+    first_ref[...] = ext_ref[jnp.where(even, zcells - 1, 0)]
+    second_ref[...] = ext_ref[jnp.where(even, 0, zcells - 1)]
+
+
+def edge_kernel(zcells, xcells, slots, slabs, first_ref, second_ref, own_ref, table_ref, weight_ref,
+                filter_ref, rout_ref, agg_ref, ext_ref, rows_a, rows_b, hot_a, hot_b, both_a,
+                both_b, wide_a, wide_b):
+    features = own_ref.shape[2]
     cells = zcells * xcells
     place = lax.axis_index("gz")
-    ext_ref[0] = jnp.where(place > 0, below_ref[...], jnp.zeros_like(below_ref))
-    ext_ref[zcells + 1] = jnp.where(place < slabs - 1, above_ref[...], jnp.zeros_like(above_ref))
-    for z in range(zcells):
-        ext_ref[z + 1, slots : slots + xcells * slots, :] = hid_ref[
-            z * xcells * slots : (z + 1) * xcells * slots, :
-        ]
-        for h in range(slots // 16):
-            lane = (z * (slots // 16) + h) * 128
-            ext_ref[z + 1, 16 * h : 16 * h + 16, :] = left_ref[
-                channels + 16 : channels + 32, lane : lane + 128
-            ]
-            ext_ref[z + 1, wide - slots + 16 * h : wide - slots + 16 * h + 16, :] = right_ref[
-                channels + 16 : channels + 32, lane : lane + 128
-            ]
+    even = place % 2 == 0
+    first, second = first_ref[...], second_ref[...]
+    blank = jnp.zeros_like(first)
+    ext_ref[0] = jnp.where(place > 0, jnp.where(even, second, first), blank)
+    ext_ref[zcells + 1] = jnp.where(place < slabs - 1, jnp.where(even, first, second), blank)
+    ext_ref[1 : zcells + 1] = own_ref[...]
     rout_t = rout_ref[...].astype(f32).T.astype(bf16)
-    uin_t = (0.5 * uin_ref[...].astype(f32)).T.astype(bf16)
     groups = 128 // slots
     chunks = table_ref.shape[1] // 2
     region = 9 * slots // 2
@@ -354,45 +422,61 @@
 
     make_hot(0, hot_a, rows_a)
 
-    def two_cells(turn, carry):
-        cell = 2 * turn
-        multiply(cell, hot_a, rows_a, both_a, wide_a)
-        make_hot(cell + 1, hot_b, rows_b)
-        gather_up(jnp.maximum(cell - 1, 0), both_b, wide_b)
-        multiply(cell + 1, hot_b, rows_b, both_b, wide_b)
-        make_hot(jnp.minimum(cell + 2, cells - 1), hot_a, rows_a)
-        gather_up(cell, both_a, wide_a)
+    def four_cells(turn, carry):
+        for cell in (4 * turn, 4 * turn + 2):
+            multiply(cell, hot_a, rows_a, both_a, wide_a)
+            make_hot(cell + 1, hot_b, rows_b)
+            gather_up(jnp.maximum(cell - 1, 0), both_b, wide_b)
+            multiply(cell + 1, hot_b, rows_b, both_b, wide_b)
+            make_hot(jnp.minimum(cell + 2, cells - 1), hot_a, rows_a)
+            gather_up(cell, both_a, wide_a)
         return carry
 
-    lax.fori_loop(0, cells // 2, two_cells, 0)
+    lax.fori_loop(0, cells // 4, four_cells, 0)
     gather_up(cells - 1, both_b, wide_b)
 
-    for step in range(cells // groups):
-        half = nn_dot(uin_t, agg_ref[step].astype(bf16))
-        hidden = (half + half * jnp.tanh(half)).T.astype(bf16)
-        begin = step * 128
-        renewed = hid_ref[begin : begin + 128, :].astype(f32) + nn_dot(hidden, uout_ref[...])
-        out_ref[begin : begin + 128, :] = renewed.astype(bf16)
-        weighted = renewed * ew_ref[...].astype(f32)
-        energy_ref[step : step + 1, :] = jnp.sum(weighted.T, axis=0, keepdims=True)
-
 
 def field_kernel(zcells, xcells, slots, channels, width_x, slabs, msg_ref, phase_ref, moment_ref,
-                 short_ref, *refs):
-    sums = refs[: slabs - 1]
-    energy_ref, force_ref = refs[slabs - 1 :]
+                 hid_ref, agg_ref, uin_ref, uout_ref, ew_ref, *refs):
+    sums = [ref[...] for ref in refs[: slabs - 1]]
+    out_ref, energy_ref, force_ref = refs[slabs - 1 :]
+
+    aggregate = jnp.concatenate(
+        [agg_ref[step].astype(bf16) for step in range(agg_ref.shape[0])], axis=1
+    )
+    uin_t = (0.5 * uin_ref[...].astype(f32)).T.astype(bf16)
+    uout_t = uout_ref[...].astype(f32).T.astype(bf16)
+    half = nn_dot(uin_t, aggregate)
+    update = nn_dot(uout_t, (half + half * jnp.tanh(half)).astype(bf16))
+    readout = ew_ref[...]
+    energy_column = jnp.broadcast_to(readout.astype(f32), (8, readout.shape[1])).T[:, :1]
+    short = jnp.sum(update * energy_column, axis=0, keepdims=True) + nt_dot(
+        jnp.broadcast_to(readout, (16, readout.shape[1])), hid_ref[...]
+    )[:1]
+    out_ref[...] = (hid_ref[...].astype(f32) + update.T).astype(bf16)
+
     wave_x, wave_y, screened, weight = wave_row(width_x)
     decay = twin(jnp.exp(-screened * layer_depth))
     span = decay
     for _ in range(2 * zcells - 1):
         span = span * decay
+    spans = [jnp.ones_like(span)]
+    for _ in range(slabs - 2):
+        spans.append(spans[-1] * span)
     place = lax.axis_index("gz")
-    below = jnp.zeros_like(sums[0][...])
-    above = jnp.zeros_like(below)
-    for shift in range(slabs - 1, 0, -1):
-        below = jnp.where(place >= shift, below * span + sums[shift - 1][...], below)
-    for shift in range(1, slabs):
-        above = jnp.where(place < shift, above * span + sums[shift - 1][...], above)
+    even = place % 2 == 0
+    inner = jnp.where(even, place > 0, place < slabs - 1)
+    near, other = sums[0], sums[1]
+    other = jnp.where(inner, other, other * spans[-1])
+    other_below = jnp.where(even, place > 0, place == slabs - 1)
+    zero = jnp.zeros_like(near)
+    below = jnp.where(even, zero, near) + jnp.where(other_below, other, zero)
+    above = jnp.where(even, near, zero) + jnp.where(other_below, zero, other)
+    for shift, value in enumerate(sums[2:], start=2):
+        under = place >= shift
+        value = value * jnp.where(under, spans[shift - 1], spans[slabs - shift - 1])
+        below = below + jnp.where(under, value, zero)
+        above = above + jnp.where(under, zero, value)
     layers = [
         moment_ref[z, l * channels : (l + 1) * channels, :] for z in range(zcells) for l in range(2)
     ]
@@ -424,11 +508,7 @@
         long_energy = 0.5 * jnp.sum(charges * chosen[:channels], axis=0, keepdims=True)
         force_x = -jnp.sum(charges * chosen[channels : 2 * channels], axis=0, keepdims=True)
         force_y = -jnp.sum(charges * chosen[2 * channels :], axis=0, keepdims=True)
-        per = row_atoms // 128
-        short = jnp.concatenate(
-            [short_ref[z * per + j : z * per + j + 1, :] for j in range(per)], axis=1
-        )
-        energy = short + long_energy
+        energy = short[:, lanes] + long_energy
         for x in range(xcells):
             cell = z * xcells + x
             piece = slice(x * slots, (x + 1) * slots)
@@ -520,7 +600,7 @@
         species_table,
         charge_weight.T,
     )
-    hidden, message, to_right, to_left = pl.pallas_call(
+    hidden, message, even_message, odd_message = pl.pallas_call(
         fetching(partial(start_kernel, zcells, xcells, slots), len(inputs)),
         out_shape=(
             shape((atoms, width), bf16),
@@ -534,48 +614,51 @@
         compiler_params=grant(6),
     )(*held(inputs))
 
-    def ring(count, shift):
-        return [(i, (i + shift) % count) for i in range(count)]
-
-    from_left = lax.ppermute(to_right, "xy", ring(strips, 1))
-    from_right = lax.ppermute(to_left, "xy", ring(strips, strips - 1))
-    messages = [from_left, from_right] + [
-        lax.ppermute(message, "xy", ring(strips, shift)) for shift in range(2, strips - 1)
-    ]
-
-    phases, own_moments = pl.pallas_call(
-        partial(own_kernel, zcells, channels, width_x),
-        out_shape=(
-            shape((2 * WAVES, atoms), bf16),
-            shape((zcells, 2 * channels, 2 * WAVES), f32),
-        ),
-        in_specs=[vmem()],
-        out_specs=(vmem(), vmem()),
-        compiler_params=grant(8),
-        cost_estimate=cost(4_000_000_000, 2_000_000),
-    )(message)
+    paths = routes(strips)
+    payloads = [even_message, odd_message] + [message] * (len(paths) - 2)
+    messages = [lax.ppermute(p, "xy", path) for p, path in zip(payloads, paths)]
 
     rows = listed * slots // 128
     chunks = rows // 2
+    basis, hidden_width = radial_in.shape
     inputs = (
         neighbours.reshape(cells, slots, listed),
         distances.reshape(cells, slots, listed),
         neighbour_count.reshape(cells, slots),
         radial_in,
     )
-    table, weight, filters = pl.pallas_call(
-        fetching(partial(prepare_kernel, slots), len(inputs)),
+    phases, own_moments, table, weight, filters = pl.pallas_call(
+        partial(own_kernel, zcells, channels, width_x, slots),
         out_shape=(
+            shape((2 * WAVES, atoms), bf16),
+            shape((zcells, 2 * channels, 2 * WAVES), f32),
             shape((cells, rows, 128), jnp.int32),
             shape((cells, rows, 128), f32),
-            shape((cells, radial_in.shape[1], rows * 128), bf16),
+            shape((cells, hidden_width, rows * 128), bf16),
         ),
-        in_specs=[hbm()] * len(inputs),
-        out_specs=(vmem(),) * 3,
-        scratch_shapes=fetch_scratch(inputs),
+        in_specs=[hbm()] * len(inputs) + [vmem()],
+        out_specs=(vmem(),) * 5,
+        scratch_shapes=[pltpu.VMEM(a.shape, a.dtype) for a in inputs]
+        + [
+            pltpu.VMEM((2, basis, rows * 128), bf16),
+            pltpu.VMEM((2, basis, rows * 128), bf16),
+            pltpu.SemaphoreType.DMA((len(inputs),)),
+        ],
         compiler_params=grant(10),
         cost_estimate=cost(6_000_000_000, 4_000_000),
-    )(*held(inputs))
+    )(*held(inputs), message)
+
+    wide = ((xcells + 2) * slots, width)
+    first, second, own_rows = pl.pallas_call(
+        partial(extend_kernel, zcells, xcells, slots, channels),
+        out_shape=(shape(wide, bf16), shape(wide, bf16), shape((zcells,) + wide, bf16)),
+        in_specs=[vmem()] * 3,
+        out_specs=(vmem(),) * 3,
+        compiler_params=grant(4),
+    )(hidden, messages[0], messages[1])
+    paths = routes(slabs)
+    first = lax.ppermute(first, "gz", paths[0])
+    second = lax.ppermute(second, "gz", paths[1])
 
     slab = pl.pallas_call(
         partial(slab_kernel, zcells, channels, width_x, slabs, len(messages)),
@@ -587,64 +670,45 @@
         compiler_params=grant(8),
         cost_estimate=cost(8_000_000_000, 2_000_000),
     )(own_moments, *messages)
-    moments = slab[0]
-
-    wide = ((xcells + 2) * slots, width)
-    top, bottom = pl.pallas_call(
-        partial(extend_kernel, zcells, xcells, slots, channels),
-        out_shape=(shape(wide, bf16), shape(wide, bf16)),
-        in_specs=[vmem()] * 3,
-        out_specs=(vmem(), vmem()),
-        compiler_params=grant(4),
-    )(hidden, from_left, from_right)
-    below = lax.ppermute(top, "gz", ring(slabs, 1))
-    above = lax.ppermute(bottom, "gz", ring(slabs, slabs - 1))
-    sums = [
-        lax.ppermute(slab[shift], "gz", ring(slabs, shift)) for shift in range(1, slabs)
-    ]
-
-    features_out, short_energy = pl.pallas_call(
-        partial(edge_kernel, zcells, xcells, slots, channels, slabs),
-        out_shape=(shape((atoms, width), bf16), shape((atoms // 128, 128), f32)),
-        in_specs=[vmem()] * 12,
-        out_specs=(vmem(), vmem()),
-        scratch_shapes=[
-            pltpu.VMEM((zcells + 2, (xcells + 2) * slots, width), bf16),
-            pltpu.VMEM((2 * width, 9 * slots // 2), bf16),
-            pltpu.VMEM((2 * width, 9 * slots // 2), bf16),
-            pltpu.VMEM((chunks, 9 * slots // 2, 256), bf16),
-            pltpu.VMEM((chunks, 9 * slots // 2, 256), bf16),
-            pltpu.VMEM((chunks, 2 * width, 256), f32),
-            pltpu.VMEM((chunks, 2 * width, 256), f32),
-            pltpu.VMEM((chunks, width, 256), f32),
-            pltpu.VMEM((chunks, width, 256), f32),
-            pltpu.VMEM((atoms // 128, width, 128), f32),
-        ],
-        compiler_params=grant(16),
+    sums = [lax.ppermute(part, "gz", path) for part, path in zip(slab[1:], paths)]
+
+    region = 9 * slots // 2
+    aggregate = pl.pallas_call(
+        partial(edge_kernel, zcells, xcells, slots, slabs),
+        out_shape=shape((atoms // 128, width, 128), f32),
+        in_specs=[vmem()] * 7,
+        out_specs=vmem(),
+        scratch_shapes=[pltpu.VMEM((zcells + 2,) + wide, bf16)]
+        + [pltpu.VMEM((2 * width, region), bf16)] * 2
+        + [pltpu.VMEM((chunks, region, 256), bf16)] * 2
+        + [pltpu.VMEM((chunks, 2 * width, 256), f32)] * 2
+        + [pltpu.VMEM((chunks, width, 256), f32)] * 2,
+        compiler_params=grant(12),
         cost_estimate=cost(12_000_000_000, 4_000_000),
+    )(first, second, own_rows, table, weight, filters, radial_out)
+
+    features_out, energy, forces = pl.pallas_call(
+        partial(field_kernel, zcells, xcells, slots, channels, width_x, slabs),
+        out_shape=(
+            shape((atoms, width), bf16),
+            shape((cells, slots), f32),
+            shape((2, cells, slots), f32),
+        ),
+        in_specs=[vmem()] * (8 + len(sums)),
+        out_specs=(vmem(),) * 3,
+        compiler_params=grant(8),
+        cost_estimate=cost(3_000_000_000, 3_000_000),
     )(
+        message,
+        phases,
+        slab[0],
         hidden,
-        below,
-        above,
-        from_left,
-        from_right,
-        table,
-        weight,
-        filters,
-        radial_out,
+        aggregate,
         update_in,
         update_out,
         energy_weight.reshape(1, width),
-    )
-
-    energy, forces = pl.pallas_call(
-        partial(field_kernel, zcells, xcells, slots, channels, width_x, slabs),
-        out_shape=(shape((cells, slots), f32), shape((2, cells, slots), f32)),
-        in_specs=[vmem()] * (4 + len(sums)),
-        out_specs=(vmem(), vmem()),
-        compiler_params=grant(8),
-        cost_estimate=cost(3_000_000_000, 3_000_000),
-    )(message, phases, moments, short_energy, *sums)
+        *sums,
+    )
 
     return (
         features_out.reshape(features.shape),

time: 26.7 us -> 23.2 us (0.87)
  Pallas kernels: 14.8 us -> 12.1 us
  starting transfers between devices: 10.9 us -> 9.58 us
  waiting for transfers between devices: 0.02 us -> 0.59 us
    pallas_call x3 -> x2, Pallas kernels: 10.7 us -> 7.8 us  [the longest x1 4.65 us: shards(): pl.pallas_call(partial(edge_kernel, zcells, xcells, slots, slabs), out_sh...]
    ppermute x8, starting transfers between devices: 10.9 us -> 9.58 us  [the longest x3 5.71 us: shards(): messages = [lax.ppermute(p, 'xy', path) for p, path in zip(payloads, paths)]]
    ppermute x8, waiting for transfers between devices: 0.02 us -> 0.59 us  [the longest x3 0.58 us: shards(): messages = [lax.ppermute(p, 'xy', path) for p, path in zip(payloads, paths)]]
    pallas_call x1, Pallas kernels: 1.15 us -> 1.51 us  [shards(): pl.pallas_call(partial(field_kernel, zcells, xcells, slots, channels, wid...]
  transfers between devices with their start and end apart: 8 -> 8, of which waited for: 0 -> 1; matrix products, arithmetic and copies ran while one was open for 0% -> 0% of each run, Pallas kernels for 46% -> 40%
where the time goes in v3:
time: 23.2 us; the launch traced here: 23 us
  Pallas kernels  12.1 us (52%)
  starting transfers between devices  9.58 us (41%)
  between operations  0.75 us (3%)
  waiting for transfers between devices  0.59 us (3%)
    ppermute x3, starting transfers between devices, shards(): messages = [lax.ppermute(p, 'xy', path) for p, path in zip(payloads, paths)]  5.71 us
    pallas_call x1, Pallas kernels, shards(): pl.pallas_call(partial(edge_kernel, zcells, xcells, slots, slabs), out_sh...  4.65 us
    pallas_call x1, Pallas kernels, shards(): pl.pallas_call(partial(own_kernel, zcells, channels, width_x, slots), out...  3.15 us
    ppermute x3, starting transfers between devices, shards(): lax.ppermute(part, 'gz', path)  2.21 us
    ppermute x1, starting transfers between devices, shards(): second = lax.ppermute(second, 'gz', paths[1])  1.59 us
    pallas_call x1, Pallas kernels, shards(): pl.pallas_call(partial(field_kernel, zcells, xcells, slots, channels, wid...  1.51 us
    pallas_call x1, Pallas kernels, shards(): pl.pallas_call(fetching(partial(start_kernel, zcells, xcells, slots), len...  1.44 us
    pallas_call x1, Pallas kernels, shards(): pl.pallas_call(partial(slab_kernel, zcells, channels, width_x, slabs, len...  1.3 us
  transfers between devices with their start and end apart: 8, of which 1 were waited for; matrix products, arithmetic and copies ran while one was open for 0% of the time, Pallas kernels for 40%

profile of v3, /device:TPU:0, one launch (start us, length us, event | category | flops | bytes accessed | tf_op | source)
XLA Modules:
  0.0 23.0 jit_solution(2827769080244476372)
XLA Ops:
  0.6 1.4 %shard_map.157 = (bf16[512,128]{1,0:T(8,128)(2,1)S(1)}, bf16[32,512]{1,0:T(8,128)(2,1)S(1)}, bf16[48,512]{1,0:T(8,128)(2,1)S(1)}, bf16[48,512]{1,0:T(8,128)(2,1)S(1)}) custom-call(bf16[512,128]{1,0:T(8,128)(2,1)} %bitcast.13, s32[16,32]{1,0:T(8,128)} %bitcast.15, s32[16,32]{1,0:T(8,128)} %bitcast.16, f32[2,16,32]{2,1,0:T(8,128)} %bitcast.14, ...), custom_call_target="tpu_custom_call" | custom-call | tf_op jit(solution)/shard_map/pallas_call | solution.py:603
  2.1 3.1 %collective-permute-start = (bf16[48,512]{1,0:T(8,128)(2,1)S(1)}, bf16[48,512]{1,0:T(8,128)(2,1)S(1)}, u32[]{:S(2)}, u32[]{:S(2)}) collective-permute-start(bf16[48,512]{1,0:T(8,128)(2,1)S(1)} %get-tuple-element.25), channel_id=1, source_target_pairs={{0,1},{1,0},{2,3},{3,2},{4,5},{5,4},{6,7},{7,6},{8,9},{9,8},{10,11... | collective-permute-start | bytes 147464 | tf_op jit(solution)/shard_map/ppermute | solution.py:619
  5.2 2.5 %collective-permute-start.1 = (bf16[48,512]{1,0:T(8,128)(2,1)S(1)}, bf16[48,512]{1,0:T(8,128)(2,1)S(1)}, u32[]{:S(2)}, u32[]{:S(2)}) collective-permute-start(bf16[48,512]{1,0:T(8,128)(2,1)S(1)} %get-tuple-element.26), channel_id=1, source_target_pairs={{0,3},{1,2},{2,1},{3,0},{4,7},{5,6},{6,5},{7,4},{8,11},{9,10},{10,... | collective-permute-start | bytes 147464 | tf_op jit(solution)/shard_map/ppermute | solution.py:619
  7.7 0.1 collective-permute-start.2
  7.8 3.1 %shard_map.158 = (bf16[1280,512]{1,0:T(8,128)(2,1)S(1)}, f32[2,32,1280]{2,1,0:T(8,128)S(1)}, s32[16,8,128]{2,1,0:T(8,128)S(1)}, f32[16,8,128]{2,1,0:T(8,128)S(1)}, bf16[16,64,1024]{2,1,0:T(8,128)(2,1)S(1)}) custom-call(s32[16,32,32]{2,1,0:T(8,128)} %bitcast.18, f32[16,32,32]{2,1,0:T(8,128)} %bitcast.19, s32[16,32]{1,0:T(8,128)} %bitcast.20, ...), custom_call_target="tpu_custom_call" | custom-call | flops 6000000000 | bytes 4000000 | tf_op jit(solution)/shard_map/pallas_call | solution.py:630
  10.9 0.0 collective-permute-done.refs_1_
  11.0 0.6 %collective-permute-done.1.refs_2_ = bf16[48,512]{1,0:T(8,128)(2,1)S(1)} collective-permute-done((bf16[48,512]{1,0:T(8,128)(2,1)S(1)}, bf16[48,512]{1,0:T(8,128)(2,1)S(1)}, u32[]{:S(2)}, u32[]{:S(2)}) %collective-permute-start.1) | collective-permute-done | bytes 49184 | tf_op jit(solution)/shard_map/ppermute | solution.py:619
  11.6 0.1 collective-permute-start.3
  11.7 1.6 %collective-permute-start.4 = (bf16[320,128]{1,0:T(8,128)(2,1)S(1)}, bf16[320,128]{1,0:T(8,128)(2,1)S(1)}, u32[]{:S(2)}, u32[]{:S(2)}) collective-permute-start(bf16[320,128]{1,0:T(8,128)(2,1)S(1)} %get-tuple-element.30), channel_id=1, source_target_pairs={{0,12},{4,8},{8,4},{12,0},{1,13},{5,9},{9,5},{13,1},{2,14},{6,10},... | collective-permute-start | bytes 245768 | tf_op jit(solution)/shard_map/ppermute | solution.py:661
  13.2 0.0 collective-permute-done.2.refs_3_
  13.2 0.0 copy-start.2
  13.2 1.3 %shard_map.159 = (f32[2,32,1280]{2,1,0:T(8,128)S(1)}, f32[16,1280]{1,0:T(8,128)S(1)}, f32[16,1280]{1,0:T(8,128)S(1)}, f32[16,1280]{1,0:T(8,128)S(1)}) custom-call(f32[2,32,1280]{2,1,0:T(8,128)S(1)} %get-tuple-element.24.refs_0_, bf16[48,512]{1,0:T(8,128)(2,1)S(1)} %collective-permute-done.refs_1_, bf16[48,512]{1,0:T(8,128)(2,1)S(1)} %collective-permute-done.1.refs_2_, ...), custom_call_target="tpu_custom_call" | custom-call | flops 8000000000 | bytes 2000000 | tf_op jit(solution)/shard_map/pallas_call | solution.py:663
  14.6 0.1 collective-permute-start.5
  14.7 1.1 %collective-permute-start.6 = (f32[16,1280]{1,0:T(8,128)S(1)}, f32[16,1280]{1,0:T(8,128)S(1)}, u32[]{:S(2)}, u32[]{:S(2)}) collective-permute-start(f32[16,1280]{1,0:T(8,128)S(1)} %get-tuple-element.36), channel_id=1, source_target_pairs={{0,12},{4,8},{8,4},{12,0},{1,13},{5,9},{9,5},{13,1},{2,14},{6,10},... | collective-permute-start | bytes 245768 | tf_op jit(solution)/shard_map/ppermute | solution.py:673
  15.8 0.9 %collective-permute-start.7 = (f32[16,1280]{1,0:T(8,128)S(1)}, f32[16,1280]{1,0:T(8,128)S(1)}, u32[]{:S(2)}, u32[]{:S(2)}) collective-permute-start(f32[16,1280]{1,0:T(8,128)S(1)} %get-tuple-element.37), channel_id=1, source_target_pairs={{0,8},{4,12},{8,0},{12,4},{1,9},{5,13},{9,1},{13,5},{2,10},{6,14},... | collective-permute-start | bytes 245768 | tf_op jit(solution)/shard_map/ppermute | solution.py:673
  16.8 0.0 collective-permute-done.3.refs_0_
  16.8 0.0 collective-permute-done.4.refs_1_
  16.8 0.0 copy-done.2
  16.8 0.0 copy-start
  16.8 0.0 copy-start.1
  16.8 0.0 copy-start.3
  16.8 4.7 %shard_map.161.refs_4_ = f32[4,128,128]{2,1,0:T(8,128)S(1)} custom-call(bf16[320,128]{1,0:T(8,128)(2,1)S(1)} %collective-permute-done.3.refs_0_, bf16[320,128]{1,0:T(8,128)(2,1)S(1)} %collective-permute-done.4.refs_1_, bf16[2,320,128]{2,1,0:T(8,128)(2,1)S(1)} %get-tuple-element.31.refs_2_, s32[16,8,128]{2,1,0:T(8,128)S(1)} %get-tuple-element.32.refs_3_, ...), custom_call_target="tpu_custom_call" | custom-call | flops 12000000000 | bytes 4000000 | tf_op jit(solution)/shard_map/pallas_call | solution.py:676
  21.5 0.0 collective-permute-done.5.refs_8_
  21.5 0.0 collective-permute-done.6.refs_9_
  21.5 0.0 collective-permute-done.7.refs_10_
  21.5 0.0 copy-done
  21.5 0.0 copy-done.1
  21.5 0.0 copy-done.3
  21.5 1.5 %shard_map.162 = (bf16[512,128]{1,0:T(8,128)(2,1)}, f32[16,32]{1,0:T(8,128)}, f32[2,16,32]{2,1,0:T(8,128)}) custom-call(bf16[32,512]{1,0:T(8,128)(2,1)S(1)} %get-tuple-element.22.refs_4_.refs_0_, bf16[1280,512]{1,0:T(8,128)(2,1)S(1)} %get-tuple-element.23.refs_1_, f32[2,32,1280]{2,1,0:T(8,128)S(1)} %get-tuple-element.27.refs_2_, ...), custom_call_target="tpu_custom_call" | custom-call | flops 3000000000 | bytes 3000000 | tf_op jit(solution)/shard_map/pallas_call | solution.py:690
  (1 shorter events, 0.0 us)
Async XLA Ops:
  2.1 8.9 %collective-permute-start = (bf16[48,512]{1,0:T(8,128)(2,1)S(1)}, bf16[48,512]{1,0:T(8,128)(2,1)S(1)}, u32[]{:S(2)}, u32[]{:S(2)}) collective-permute-start(bf16[48,512]{1,0:T(8,128)(2,1)S(1)} %get-tuple-element.25), channel_id=1, source_target_pairs={{0,1},{1,0},{2,3},{3,2},{4,5},{5,4},{6,7},{7,6},{8,9},{9,8},{10,11... | collective-permute-start | bytes 147464 | tf_op jit(solution)/shard_map/ppermute | solution.py:619
  5.2 6.3 %collective-permute-start.1 = (bf16[48,512]{1,0:T(8,128)(2,1)S(1)}, bf16[48,512]{1,0:T(8,128)(2,1)S(1)}, u32[]{:S(2)}, u32[]{:S(2)}) collective-permute-start(bf16[48,512]{1,0:T(8,128)(2,1)S(1)} %get-tuple-element.26), channel_id=1, source_target_pairs={{0,3},{1,2},{2,1},{3,0},{4,7},{5,6},{6,5},{7,4},{8,11},{9,10},{10,... | collective-permute-start | bytes 147464 | tf_op jit(solution)/shard_map/ppermute | solution.py:619
  7.7 5.6 %collective-permute-start.2 = (bf16[32,512]{1,0:T(8,128)(2,1)S(1)}, bf16[32,512]{1,0:T(8,128)(2,1)S(1)}, u32[]{:S(2)}, u32[]{:S(2)}) collective-permute-start(bf16[32,512]{1,0:T(8,128)(2,1)S(1)} %get-tuple-element.22.refs_4_.refs_0_), channel_id=1, source_target_pairs={{0,2},{1,3},{2,0},{3,1},{4,6},{5,7},{6,4},{7,5},{8,10},{9,11},{10,... | collective-permute-start | bytes 98312 | tf_op jit(solution)/shard_map/ppermute | solution.py:619
  11.6 5.2 %collective-permute-start.3 = (bf16[320,128]{1,0:T(8,128)(2,1)S(1)}, bf16[320,128]{1,0:T(8,128)(2,1)S(1)}, u32[]{:S(2)}, u32[]{:S(2)}) collective-permute-start(bf16[320,128]{1,0:T(8,128)(2,1)S(1)} %get-tuple-element.29), channel_id=1, source_target_pairs={{0,4},{4,0},{8,12},{12,8},{1,5},{5,1},{9,13},{13,9},{2,6},{6,2},{1... | collective-permute-start | bytes 245768 | tf_op jit(solution)/shard_map/ppermute | solution.py:660
  11.7 5.1 %collective-permute-start.4 = (bf16[320,128]{1,0:T(8,128)(2,1)S(1)}, bf16[320,128]{1,0:T(8,128)(2,1)S(1)}, u32[]{:S(2)}, u32[]{:S(2)}) collective-permute-start(bf16[320,128]{1,0:T(8,128)(2,1)S(1)} %get-tuple-element.30), channel_id=1, source_target_pairs={{0,12},{4,8},{8,4},{12,0},{1,13},{5,9},{9,5},{13,1},{2,14},{6,10},... | collective-permute-start | bytes 245768 | tf_op jit(solution)/shard_map/ppermute | solution.py:661
  13.2 3.5 %copy-start.2 = (bf16[64,128]{1,0:T(8,128)(2,1)S(1)}, bf16[64,128]{1,0:T(8,128)(2,1)}, u32[]{:S(2)}) copy-start(bf16[64,128]{1,0:T(8,128)(2,1)} %refs_6_.2) | copy-start | bytes 49156
  14.6 6.9 %collective-permute-start.5 = (f32[16,1280]{1,0:T(8,128)S(1)}, f32[16,1280]{1,0:T(8,128)S(1)}, u32[]{:S(2)}, u32[]{:S(2)}) collective-permute-start(f32[16,1280]{1,0:T(8,128)S(1)} %get-tuple-element.35), channel_id=1, source_target_pairs={{0,4},{4,0},{8,12},{12,8},{1,5},{5,1},{9,13},{13,9},{2,6},{6,2},{1... | collective-permute-start | bytes 245768 | tf_op jit(solution)/shard_map/ppermute | solution.py:673
  14.7 6.8 %collective-permute-start.6 = (f32[16,1280]{1,0:T(8,128)S(1)}, f32[16,1280]{1,0:T(8,128)S(1)}, u32[]{:S(2)}, u32[]{:S(2)}) collective-permute-start(f32[16,1280]{1,0:T(8,128)S(1)} %get-tuple-element.36), channel_id=1, source_target_pairs={{0,12},{4,8},{8,4},{12,0},{1,13},{5,9},{9,5},{13,1},{2,14},{6,10},... | collective-permute-start | bytes 245768 | tf_op jit(solution)/shard_map/ppermute | solution.py:673
  15.8 5.7 %collective-permute-start.7 = (f32[16,1280]{1,0:T(8,128)S(1)}, f32[16,1280]{1,0:T(8,128)S(1)}, u32[]{:S(2)}, u32[]{:S(2)}) collective-permute-start(f32[16,1280]{1,0:T(8,128)S(1)} %get-tuple-element.37), channel_id=1, source_target_pairs={{0,8},{4,12},{8,0},{12,4},{1,9},{5,13},{9,1},{13,5},{2,10},{6,14},... | collective-permute-start | bytes 245768 | tf_op jit(solution)/shard_map/ppermute | solution.py:673
  16.8 4.7 %copy-start = (bf16[128,256]{1,0:T(8,128)(2,1)S(1)}, bf16[128,256]{1,0:T(8,128)(2,1)}, u32[]{:S(2)}) copy-start(bf16[128,256]{1,0:T(8,128)(2,1)} %refs_5_.1) | copy-start | bytes 196612
  16.8 4.7 %copy-start.1 = (bf16[256,128]{1,0:T(8,128)(2,1)S(1)}, bf16[256,128]{1,0:T(8,128)(2,1)}, u32[]{:S(2)}) copy-start(bf16[256,128]{1,0:T(8,128)(2,1)} %refs_6_.3) | copy-start | bytes 196612
  16.8 4.7 %copy-start.3 = (bf16[128]{0:T(256)(128)(2,1)S(1)}, bf16[128]{0:T(256)(128)(2,1)}, u32[]{:S(2)}) copy-start(bf16[128]{0:T(256)(128)(2,1)} %param.27) | copy-start | bytes 772

commit v4 on v3

--- a/solution.py
+++ b/solution.py
@@ -183,63 +183,53 @@
     extra = jnp.concatenate(
         three_parts(coord_x)
         + three_parts(coord_y)
-        + [sub, jnp.zeros((16 - 7, atoms), f32)],
+        + [sub, jnp.zeros((1, atoms), f32)],
         axis=0,
     ).astype(bf16)
     msg_ref[0:channels, :] = charges
-    msg_ref[channels : channels + 16, :] = extra
+    msg_ref[channels : channels + 8, :] = extra
     even = lax.axis_index("xy") % 2 == 0
     right = xcells - 1
     for ref, column in ((even_ref, jnp.where(even, right, 0)), (odd_ref, jnp.where(even, 0, right))):
         ref[0:channels, :] = charges
-        ref[channels : channels + 16, :] = extra
+        ref[channels + 16 : channels + 24, :] = extra
         for z in range(zcells):
             for h in range(slots // 16):
                 begin = pl.multiple_of((z * xcells + column) * slots + 16 * h, 16)
                 lane = (z * (slots // 16) + h) * 128
-                ref[channels + 16 : channels + 32, lane : lane + 128] = hid_ref[
+                ref[channels : channels + 16, lane : lane + 128] = hid_ref[
                     pl.ds(begin, 16), :
                 ]
 
 
 def read_atoms(msg_ref, channels, lanes):
     charges = msg_ref[0:channels, lanes].astype(f32)
-    extra = msg_ref[channels : channels + 16, lanes].astype(f32)
+    extra = msg_ref[msg_ref.shape[0] - 8 :, lanes].astype(f32)
     coord_x = (extra[0:1] + extra[1:2]) + extra[2:3]
     coord_y = (extra[3:4] + extra[4:5]) + extra[5:6]
     return charges, coord_x, coord_y, extra[6:7]
 
 
-def own_kernel(zcells, channels, width_x, slots, near_hbm, dist_hbm, count_hbm, rin_hbm, msg_ref,
-               phase_ref, moment_ref, table_ref, weight_ref, filter_ref, near_ref, dist_ref,
-               count_ref, rin_ref, rad_a, rad_b, sems):
-    moves = [
-        pltpu.make_async_copy(source, target, sems.at[i])
-        for i, (source, target) in enumerate(
-            (
-                (near_hbm, near_ref),
-                (dist_hbm, dist_ref),
-                (count_hbm, count_ref),
-                (rin_hbm, rin_ref),
-            )
-        )
-    ]
-    for move in moves:
-        move.start()
+def pair(table, q):
+    return jnp.concatenate([table[2 * q : 2 * q + 1], table[2 * q + 1 : 2 * q + 2]], axis=1)
+
+
+def own_kernel(zcells, channels, width_x, slots, near_ref, dist_ref, count_ref, rin_ref, rout_ref,
+               msg_ref, phase_ref, moment_ref, table_ref, filter_ref, weight_ref, rad_ref,
+               layer_a, layer_b):
     row_atoms = msg_ref.shape[1] // zcells
     for z in range(zcells):
         lanes = slice(z * row_atoms, (z + 1) * row_atoms)
         charges, coord_x, coord_y, sub = read_atoms(msg_ref, channels, lanes)
         store_phases(phase_ref, lanes, coord_x, coord_y, width_x)
         moment_ref[z] = nt_dot(layer_charges(charges, sub), phase_ref[:, lanes])
-    for move in moves:
-        move.wait()
 
     cells, _, listed = near_ref.shape
     basis = rin_ref.shape[0]
     groups = 128 // slots
     rows = listed // groups
     rin_t = (0.5 * rin_ref[...].astype(f32)).T.astype(bf16)
+    rout_t = rout_ref[...].astype(f32).T.astype(bf16)
     centre = (
         cutoff * lax.broadcasted_iota(jnp.int32, (basis, 128), 0).astype(f32) / (basis - 1)
     )
@@ -253,7 +243,7 @@
             [turned[g * rows : (g + 1) * rows] for g in range(groups)], axis=1
         )
 
-    def spread(cell, rad_ref, slot):
+    def spread(cell, slot):
         near = edge_rows(near_ref[cell].astype(f32)).astype(jnp.int32)
         dist = edge_rows(dist_ref[cell])
         count = jnp.concatenate([count_ref[pl.ds(cell, 1), :]] * groups, axis=1)
@@ -265,22 +255,35 @@
             gap = (dist[q : q + 1] - centre) / basis_width
             rad_ref[slot, :, 128 * q : 128 * q + 128] = jnp.exp(-(gap * gap)).astype(bf16)
 
-    def filtered(cell, rad_ref, slot):
+    def first_layer(slot, layer_ref):
         for q in range(0, rows * 128, 256):
             half = nn_dot(rin_t, rad_ref[slot, :, q : q + 256])
-            filter_ref[cell, :, q : q + 256] = (half + half * jnp.tanh(half)).astype(bf16)
+            layer_ref[slot, :, q : q + 256] = (half + half * jnp.tanh(half)).astype(bf16)
+
+    def second_layer(cell, slot, layer_ref):
+        weight = weight_ref[cell]
+        for q in range(rows // 2):
+            wide = nn_dot(rout_t, layer_ref[slot, :, 256 * q : 256 * q + 256])
+            filter_ref[cell, q] = pair(weight, q) * wide
+
+    def advance(cell, done_ref, next_ref):
+        for slot in range(2):
+            first_layer(slot, next_ref)
+        for slot in range(2):
+            second_layer(cell + slot, slot, done_ref)
+        for slot in range(2):
+            spread(jnp.minimum(cell + 4 + slot, cells - 1), slot)
 
     for slot in range(2):
-        spread(slot, rad_a, slot)
+        spread(slot, slot)
+    for slot in range(2):
+        first_layer(slot, layer_a)
+    for slot in range(2):
+        spread(2 + slot, slot)
 
     def four_cells(turn, carry):
-        cell = 4 * turn
-        for slot in range(2):
-            filtered(cell + slot, rad_a, slot)
-            spread(cell + 2 + slot, rad_b, slot)
-        for slot in range(2):
-            filtered(cell + 2 + slot, rad_b, slot)
-            spread(jnp.minimum(cell + 4 + slot, cells - 1), rad_a, slot)
+        advance(4 * turn, layer_a, layer_b)
+        advance(4 * turn + 2, layer_b, layer_a)
         return carry
 
     lax.fori_loop(0, cells // 4, four_cells, 0)
@@ -344,7 +347,7 @@
     for h in range(slots // 16):
         lane = (z * (slots // 16) + h) * 128
         left, right = sides(
-            even_ref, odd_ref, slice(channels + 16, channels + 32), slice(lane, lane + 128)
+            even_ref, odd_ref, slice(channels, channels + 16), slice(lane, lane + 128)
         )
         ref[16 * h : 16 * h + 16, :] = left
         begin = slots + count + 16 * h
@@ -360,9 +363,8 @@
     second_ref[...] = ext_ref[jnp.where(even, 0, zcells - 1)]
 
 
-def edge_kernel(zcells, xcells, slots, slabs, first_ref, second_ref, own_ref, table_ref, weight_ref,
-                filter_ref, rout_ref, agg_ref, ext_ref, rows_a, rows_b, hot_a, hot_b, both_a,
-                both_b, wide_a, wide_b):
+def edge_kernel(zcells, xcells, slots, slabs, first_ref, second_ref, own_ref, table_ref, filter_ref,
+                agg_ref, ext_ref, rows_a, rows_b, hot_a, hot_b, both_a, both_b):
     features = own_ref.shape[2]
     cells = zcells * xcells
     place = lax.axis_index("gz")
@@ -372,16 +374,12 @@
     ext_ref[0] = jnp.where(place > 0, jnp.where(even, second, first), blank)
     ext_ref[zcells + 1] = jnp.where(place < slabs - 1, jnp.where(even, first, second), blank)
     ext_ref[1 : zcells + 1] = own_ref[...]
-    rout_t = rout_ref[...].astype(f32).T.astype(bf16)
     groups = 128 // slots
     chunks = table_ref.shape[1] // 2
     region = 9 * slots // 2
     row_id = lax.broadcasted_iota(jnp.int32, (16, 256), 0).astype(jnp.int16)
     one, zero = jnp.ones((16, 256), bf16), jnp.zeros((16, 256), bf16)
     group_lane = lax.broadcasted_iota(jnp.int32, (features, 128), 1) // slots
-
-    def pair(table, q):
-        return jnp.concatenate([table[2 * q : 2 * q + 1], table[2 * q + 1 : 2 * q + 2]], axis=1)
 
     def make_hot(cell, hot_ref, rows_ref):
         near = table_ref[cell]
@@ -398,20 +396,18 @@
         rows_ref[:features] = rows[:region].astype(f32).T.astype(bf16)
         rows_ref[features:] = rows[region:].astype(f32).T.astype(bf16)
 
-    def multiply(cell, hot_ref, rows_ref, both_ref, wide_ref):
+    def multiply(hot_ref, rows_ref, both_ref):
         rows_t = rows_ref[...]
         for q in range(chunks):
             both_ref[q] = nn_dot(rows_t, hot_ref[q])
-            wide_ref[q] = nn_dot(rout_t, filter_ref[cell, :, 256 * q : 256 * q + 256])
-
-    def gather_up(cell, both_ref, wide_ref):
+
+    def gather_up(cell, both_ref):
         near = table_ref[cell]
-        weight = weight_ref[cell]
         total = jnp.zeros((features, 128), f32)
         for q in range(chunks):
             upper = pair(near, q) >= region
             picked = jnp.where(upper, both_ref[q, features:], both_ref[q, :features])
-            product = (pair(weight, q) * wide_ref[q]) * picked
+            product = filter_ref[cell, q] * picked
             total = total + (product[:, :128] + product[:, 128:])
         shift = 64
         while shift >= slots:
@@ -422,18 +418,19 @@
 
     make_hot(0, hot_a, rows_a)
 
-    def four_cells(turn, carry):
-        for cell in (4 * turn, 4 * turn + 2):
-            multiply(cell, hot_a, rows_a, both_a, wide_a)
+    def eight_cells(turn, carry):
+        for step in range(4):
+            cell = 8 * turn + 2 * step
+            multiply(hot_a, rows_a, both_a)
             make_hot(cell + 1, hot_b, rows_b)
-            gather_up(jnp.maximum(cell - 1, 0), both_b, wide_b)
-            multiply(cell + 1, hot_b, rows_b, both_b, wide_b)
+            gather_up(jnp.maximum(cell - 1, 0), both_b)
+            multiply(hot_b, rows_b, both_b)
             make_hot(jnp.minimum(cell + 2, cells - 1), hot_a, rows_a)
-            gather_up(cell, both_a, wide_a)
+            gather_up(cell, both_a)
         return carry
 
-    lax.fori_loop(0, cells // 4, four_cells, 0)
-    gather_up(cells - 1, both_b, wide_b)
+    lax.fori_loop(0, cells // 8, eight_cells, 0)
+    gather_up(cells - 1, both_b)
 
 
 def field_kernel(zcells, xcells, slots, channels, width_x, slabs, msg_ref, phase_ref, moment_ref,
@@ -502,7 +499,7 @@
             rows.append(jnp.concatenate([wave_y * sine, -wave_y * cosine], axis=1))
         panel = jnp.concatenate([row.astype(bf16) for row in rows], axis=0)
         evaluated = nn_dot(panel, phase_ref[:, lanes])
-        sub = msg_ref[channels : channels + 16, lanes].astype(f32)[6:7]
+        sub = msg_ref[channels : channels + 8, lanes].astype(f32)[6:7]
         chosen = jnp.where(sub == 0.0, evaluated[: 3 * channels], evaluated[3 * channels :])
         charges = msg_ref[0:channels, lanes].astype(f32)
         long_energy = 0.5 * jnp.sum(charges * chosen[:channels], axis=0, keepdims=True)
@@ -525,17 +522,22 @@
     return pl.BlockSpec(memory_space=pltpu.HBM)
 
 
-def fetching(body, count):
+def fetching(body, count, through):
     def kernel(*refs):
         copies, sems = refs[-count - 1 : -1], refs[-1]
+        given, rest = refs[: count + through], refs[count + through : -count - 1]
+        kept = rest[len(rest) - through :]
         moves = [
-            pltpu.make_async_copy(refs[i], copies[i], sems.at[i]) for i in range(count)
+            pltpu.make_async_copy(source, target, sems.at[i])
+            for i, (source, target) in enumerate(zip(given, copies + kept))
         ]
         for move in moves:
             move.start()
-        for move in moves:
+        for move in moves[:count]:
             move.wait()
-        body(*copies, *refs[count : -count - 1])
+        body(*copies, *rest[: len(rest) - through])
+        for move in moves[count:]:
+            move.wait()
 
     kernel.__name__ = body.__name__
     return kernel
@@ -543,12 +545,6 @@
 
 def held(arrays):
     return [pltpu.with_memory_space_constraint(a, pltpu.HBM) for a in arrays]
-
-
-def fetch_scratch(arrays):
-    return [pltpu.VMEM(a.shape, a.dtype) for a in arrays] + [
-        pltpu.SemaphoreType.DMA((len(arrays),))
-    ]
 
 
 def shards(
@@ -600,54 +596,55 @@
         species_table,
         charge_weight.T,
     )
-    hidden, message, even_message, odd_message = pl.pallas_call(
-        fetching(partial(start_kernel, zcells, xcells, slots), len(inputs)),
-        out_shape=(
-            shape((atoms, width), bf16),
-            shape((channels + 16, atoms), bf16),
-            shape((channels + 32, atoms), bf16),
-            shape((channels + 32, atoms), bf16),
-        ),
-        in_specs=[hbm()] * len(inputs),
-        out_specs=(vmem(),) * 4,
-        scratch_shapes=fetch_scratch(inputs),
-        compiler_params=grant(6),
-    )(*held(inputs))
-
-    paths = routes(strips)
-    payloads = [even_message, odd_message] + [message] * (len(paths) - 2)
-    messages = [lax.ppermute(p, "xy", path) for p, path in zip(payloads, paths)]
-
-    rows = listed * slots // 128
-    chunks = rows // 2
-    basis, hidden_width = radial_in.shape
-    inputs = (
+    through = (
         neighbours.reshape(cells, slots, listed),
         distances.reshape(cells, slots, listed),
         neighbour_count.reshape(cells, slots),
         radial_in,
-    )
-    phases, own_moments, table, weight, filters = pl.pallas_call(
+        radial_out,
+    )
+    hidden, message, even_message, odd_message, *lists = pl.pallas_call(
+        fetching(partial(start_kernel, zcells, xcells, slots), len(inputs), len(through)),
+        out_shape=(
+            shape((atoms, width), bf16),
+            shape((channels + 8, atoms), bf16),
+            shape((channels + 24, atoms), bf16),
+            shape((channels + 24, atoms), bf16),
+        )
+        + tuple(shape(a.shape, a.dtype) for a in through),
+        in_specs=[hbm()] * (len(inputs) + len(through)),
+        out_specs=(vmem(),) * (4 + len(through)),
+        scratch_shapes=[pltpu.VMEM(a.shape, a.dtype) for a in inputs]
+        + [pltpu.SemaphoreType.DMA((len(inputs) + len(through),))],
+        compiler_params=grant(6),
+    )(*held(inputs + through))
+
+    paths = routes(strips)
+    payloads = [even_message, odd_message] + [message] * (len(paths) - 2)
+    messages = [lax.ppermute(p, "xy", path) for p, path in zip(payloads, paths)]
+
+    rows = listed * slots // 128
+    chunks = rows // 2
+    basis, hidden_width = radial_in.shape
+    phases, own_moments, table, filters = pl.pallas_call(
         partial(own_kernel, zcells, channels, width_x, slots),
         out_shape=(
             shape((2 * WAVES, atoms), bf16),
             shape((zcells, 2 * channels, 2 * WAVES), f32),
             shape((cells, rows, 128), jnp.int32),
-            shape((cells, rows, 128), f32),
-            shape((cells, hidden_width, rows * 128), bf16),
+            shape((cells, chunks, width, 256), f32),
         ),
-        in_specs=[hbm()] * len(inputs) + [vmem()],
-        out_specs=(vmem(),) * 5,
-        scratch_shapes=[pltpu.VMEM(a.shape, a.dtype) for a in inputs]
-        + [
+        in_specs=[vmem()] * (len(lists) + 1),
+        out_specs=(vmem(),) * 4,
+        scratch_shapes=[
+            pltpu.VMEM((cells, rows, 128), f32),
             pltpu.VMEM((2, basis, rows * 128), bf16),
-            pltpu.VMEM((2, basis, rows * 128), bf16),
-            pltpu.SemaphoreType.DMA((len(inputs),)),
+            pltpu.VMEM((2, hidden_width, rows * 128), bf16),
+            pltpu.VMEM((2, hidden_width, rows * 128), bf16),
         ],
-        compiler_params=grant(10),
+        compiler_params=grant(16),
         cost_estimate=cost(6_000_000_000, 4_000_000),
-    )(*held(inputs), message)
-
+    )(*lists, message)
     wide = ((xcells + 2) * slots, width)
     first, second, own_rows = pl.pallas_call(
         partial(extend_kernel, zcells, xcells, slots, channels),
@@ -676,16 +673,15 @@
     aggregate = pl.pallas_call(
         partial(edge_kernel, zcells, xcells, slots, slabs),
         out_shape=shape((atoms // 128, width, 128), f32),
-        in_specs=[vmem()] * 7,
+        in_specs=[vmem()] * 5,
         out_specs=vmem(),
         scratch_shapes=[pltpu.VMEM((zcells + 2,) + wide, bf16)]
         + [pltpu.VMEM((2 * width, region), bf16)] * 2
         + [pltpu.VMEM((chunks, region, 256), bf16)] * 2
-        + [pltpu.VMEM((chunks, 2 * width, 256), f32)] * 2
-        + [pltpu.VMEM((chunks, width, 256), f32)] * 2,
-        compiler_params=grant(12),
+        + [pltpu.VMEM((chunks, 2 * width, 256), f32)] * 2,
+        compiler_params=grant(16),
         cost_estimate=cost(12_000_000_000, 4_000_000),
-    )(first, second, own_rows, table, weight, filters, radial_out)
+    )(first, second, own_rows, table, filters)
 
     features_out, energy, forces = pl.pallas_call(
         partial(field_kernel, zcells, xcells, slots, channels, width_x, slabs),

time: 23.2 us -> 22.8 us (0.983)
  Pallas kernels: 12.1 us -> 11.4 us
  waiting for transfers between devices: 0.59 us -> 0.95 us
    pallas_call x1, Pallas kernels: 4.65 us -> 3.89 us  [shards(): pl.pallas_call(partial(edge_kernel, zcells, xcells, slots, slabs), out_sh...]
    ppermute x3, waiting for transfers between devices: 0.01 us -> 0.49 us  [shards(): lax.ppermute(part, 'gz', path)]
  transfers between devices with their start and end apart: 8 -> 8, of which waited for: 1 -> 2; matrix products, arithmetic and copies ran while one was open for 0% -> 0% of each run, Pallas kernels for 40% -> 37%
where the time goes in v4:
time: 22.8 us; the launch traced here: 22.7 us
  Pallas kernels  11.4 us (50%)
  starting transfers between devices  9.58 us (42%)
  waiting for transfers between devices  0.95 us (4%)
  between operations  0.72 us (3%)
    ppermute x3, starting transfers between devices, shards(): messages = [lax.ppermute(p, 'xy', path) for p, path in zip(payloads, paths)]  5.71 us
    pallas_call x1, Pallas kernels, shards(): pl.pallas_call(partial(edge_kernel, zcells, xcells, slots, slabs), out_sh...  3.89 us
    pallas_call x1, Pallas kernels, shards(): pl.pallas_call(partial(own_kernel, zcells, channels, width_x, slots), out...  3.11 us
    ppermute x3, starting transfers between devices, shards(): lax.ppermute(part, 'gz', path)  2.21 us
    ppermute x1, starting transfers between devices, shards(): second = lax.ppermute(second, 'gz', paths[1])  1.59 us
    pallas_call x1, Pallas kernels, shards(): pl.pallas_call(partial(field_kernel, zcells, xcells, slots, channels, wid...  1.55 us
    pallas_call x1, Pallas kernels, shards(): pl.pallas_call(fetching(partial(start_kernel, zcells, xcells, slots), len...  1.5 us
    pallas_call x1, Pallas kernels, shards(): pl.pallas_call(partial(slab_kernel, zcells, channels, width_x, slabs, len...  1.31 us
  transfers between devices with their start and end apart: 8, of which 2 were waited for; matrix products, arithmetic and copies ran while one was open for 0% of the time, Pallas kernels for 37%

profile of v4, /device:TPU:0, one launch (start us, length us, event | category | flops | bytes accessed | tf_op | source)
XLA Modules:
  0.0 22.7 jit_solution(12859604414742294620)
XLA Ops:
  0.6 1.5 %shard_map.157 = (bf16[512,128]{1,0:T(8,128)(2,1)S(1)}, bf16[24,512]{1,0:T(8,128)(2,1)S(1)}, bf16[40,512]{1,0:T(8,128)(2,1)S(1)}, bf16[40,512]{1,0:T(8,128)(2,1)...) custom-call(bf16[512,128]{1,0:T(8,128)(2,1)} %bitcast.15, ...), custom_call_target="tpu_custom_call" | custom-call | tf_op jit(solution)/shard_map/pallas_call | solution.py:606
  2.1 3.1 %collective-permute-start = (bf16[40,512]{1,0:T(8,128)(2,1)S(1)}, bf16[40,512]{1,0:T(8,128)(2,1)S(1)}, u32[]{:S(2)}, u32[]{:S(2)}) collective-permute-start(bf16[40,512]{1,0:T(8,128)(2,1)S(1)} %get-tuple-element.34), channel_id=1, source_target_pairs={{0,1},{1,0},{2,3},{3,2},{4,5},{5,4},{6,7},{7,6},{8,9},{9,8},{10,11... | collective-permute-start | bytes 122888 | tf_op jit(solution)/shard_map/ppermute | solution.py:624
  5.3 2.5 %collective-permute-start.1 = (bf16[40,512]{1,0:T(8,128)(2,1)S(1)}, bf16[40,512]{1,0:T(8,128)(2,1)S(1)}, u32[]{:S(2)}, u32[]{:S(2)}) collective-permute-start(bf16[40,512]{1,0:T(8,128)(2,1)S(1)} %get-tuple-element.35), channel_id=1, source_target_pairs={{0,3},{1,2},{2,1},{3,0},{4,7},{5,6},{6,5},{7,4},{8,11},{9,10},{10,... | collective-permute-start | bytes 122888 | tf_op jit(solution)/shard_map/ppermute | solution.py:624
  7.7 0.1 collective-permute-start.2
  7.9 3.1 %shard_map.158 = (bf16[1280,512]{1,0:T(8,128)(2,1)S(1)}, f32[2,32,1280]{2,1,0:T(8,128)S(1)}, s32[16,8,128]{2,1,0:T(8,128)S(1)}, f32[16,4,128,256]{3,2,1,0:T(8,128)S(1)}) custom-call(s32[16,32,32]{2,1,0:T(8,128)S(1)} %get-tuple-element.27.refs_0_, f32[16,32,32]{2,1,0:T(8,128)S(1)} %get-tuple-element.28.refs_1_, s32[16,32]{1,0:T(8,128)S(1)} %get-tuple-element.29.refs_2_, ...), custom_call_target="tpu_custom_call" | custom-call | flops 6000000000 | bytes 4000000 | tf_op jit(solution)/shard_map/pallas_call | solution.py:629
  11.0 0.0 collective-permute-done.refs_1_
  11.0 0.4 %collective-permute-done.1.refs_2_ = bf16[40,512]{1,0:T(8,128)(2,1)S(1)} collective-permute-done((bf16[40,512]{1,0:T(8,128)(2,1)S(1)}, bf16[40,512]{1,0:T(8,128)(2,1)S(1)}, u32[]{:S(2)}, u32[]{:S(2)}) %collective-permute-start.1) | collective-permute-done | bytes 40992 | tf_op jit(solution)/shard_map/ppermute | solution.py:624
  11.5 0.1 collective-permute-start.3
  11.5 1.6 %collective-permute-start.4 = (bf16[320,128]{1,0:T(8,128)(2,1)S(1)}, bf16[320,128]{1,0:T(8,128)(2,1)S(1)}, u32[]{:S(2)}, u32[]{:S(2)}) collective-permute-start(bf16[320,128]{1,0:T(8,128)(2,1)S(1)} %get-tuple-element.39), channel_id=1, source_target_pairs={{0,12},{4,8},{8,4},{12,0},{1,13},{5,9},{9,5},{13,1},{2,14},{6,10},... | collective-permute-start | bytes 245768 | tf_op jit(solution)/shard_map/ppermute | solution.py:658
  13.1 0.0 collective-permute-done.2.refs_3_
  13.1 1.3 %shard_map.159 = (f32[2,32,1280]{2,1,0:T(8,128)S(1)}, f32[16,1280]{1,0:T(8,128)S(1)}, f32[16,1280]{1,0:T(8,128)S(1)}, f32[16,1280]{1,0:T(8,128)S(1)}) custom-call(f32[2,32,1280]{2,1,0:T(8,128)S(1)} %get-tuple-element.33.refs_0_, bf16[40,512]{1,0:T(8,128)(2,1)S(1)} %collective-permute-done.refs_1_, bf16[40,512]{1,0:T(8,128)(2,1)S(1)} %collective-permute-done.1.refs_2_, ...), custom_call_target="tpu_custom_call" | custom-call | flops 8000000000 | bytes 2000000 | tf_op jit(solution)/shard_map/pallas_call | solution.py:660
  14.5 0.1 collective-permute-start.5
  14.6 1.1 %collective-permute-start.6 = (f32[16,1280]{1,0:T(8,128)S(1)}, f32[16,1280]{1,0:T(8,128)S(1)}, u32[]{:S(2)}, u32[]{:S(2)}) collective-permute-start(f32[16,1280]{1,0:T(8,128)S(1)} %get-tuple-element.44), channel_id=1, source_target_pairs={{0,12},{4,8},{8,4},{12,0},{1,13},{5,9},{9,5},{13,1},{2,14},{6,10},... | collective-permute-start | bytes 245768 | tf_op jit(solution)/shard_map/ppermute | solution.py:670
  15.7 0.9 %collective-permute-start.7 = (f32[16,1280]{1,0:T(8,128)S(1)}, f32[16,1280]{1,0:T(8,128)S(1)}, u32[]{:S(2)}, u32[]{:S(2)}) collective-permute-start(f32[16,1280]{1,0:T(8,128)S(1)} %get-tuple-element.45), channel_id=1, source_target_pairs={{0,8},{4,12},{8,0},{12,4},{1,9},{5,13},{9,1},{13,5},{2,10},{6,14},... | collective-permute-start | bytes 245768 | tf_op jit(solution)/shard_map/ppermute | solution.py:670
  16.7 0.0 collective-permute-done.3.refs_0_
  16.7 0.0 collective-permute-done.4.refs_1_
  16.7 0.0 copy-start
  16.7 0.0 copy-start.1
  16.7 0.0 copy-start.2
  16.7 3.9 %shard_map.161.refs_4_ = f32[4,128,128]{2,1,0:T(8,128)S(1)} custom-call(bf16[320,128]{1,0:T(8,128)(2,1)S(1)} %collective-permute-done.3.refs_0_, bf16[320,128]{1,0:T(8,128)(2,1)S(1)} %collective-permute-done.4.refs_1_, bf16[2,320,128]{2,1,0:T(8,128)(2,1)S(1)} %get-tuple-element.40.refs_2_, s32[16,8,128]{2,1,0:T(8,128)S(1)} %get-tuple-element.41.refs_3_, ...), custom_call_target="tpu_custom_call" | custom-call | flops 12000000000 | bytes 4000000 | tf_op jit(solution)/shard_map/pallas_call | solution.py:673
  20.6 0.0 collective-permute-done.5.refs_8_
  20.6 0.0 collective-permute-done.6.refs_9_
  20.6 0.5 %collective-permute-done.7.refs_10_ = f32[16,1280]{1,0:T(8,128)S(1)} collective-permute-done((f32[16,1280]{1,0:T(8,128)S(1)}, f32[16,1280]{1,0:T(8,128)S(1)}, u32[]{:S(2)}, u32[]{:S(2)}) %collective-permute-start.7) | collective-permute-done | bytes 81952 | tf_op jit(solution)/shard_map/ppermute | solution.py:670
  21.1 0.0 copy-done
  21.1 0.0 copy-done.1
  21.1 0.0 copy-done.2
  21.1 1.5 %shard_map.162 = (bf16[512,128]{1,0:T(8,128)(2,1)}, f32[16,32]{1,0:T(8,128)}, f32[2,16,32]{2,1,0:T(8,128)}) custom-call(bf16[24,512]{1,0:T(8,128)(2,1)S(1)} %get-tuple-element.26.refs_5_.refs_0_, bf16[1280,512]{1,0:T(8,128)(2,1)S(1)} %get-tuple-element.32.refs_1_, f32[2,32,1280]{2,1,0:T(8,128)S(1)} %get-tuple-element.36.refs_2_, ...), custom_call_target="tpu_custom_call" | custom-call | flops 3000000000 | bytes 3000000 | tf_op jit(solution)/shard_map/pallas_call | solution.py:686
  (1 shorter events, 0.0 us)
Async XLA Ops:
  2.1 8.8 %collective-permute-start = (bf16[40,512]{1,0:T(8,128)(2,1)S(1)}, bf16[40,512]{1,0:T(8,128)(2,1)S(1)}, u32[]{:S(2)}, u32[]{:S(2)}) collective-permute-start(bf16[40,512]{1,0:T(8,128)(2,1)S(1)} %get-tuple-element.34), channel_id=1, source_target_pairs={{0,1},{1,0},{2,3},{3,2},{4,5},{5,4},{6,7},{7,6},{8,9},{9,8},{10,11... | collective-permute-start | bytes 122888 | tf_op jit(solution)/shard_map/ppermute | solution.py:624
  5.3 6.2 %collective-permute-start.1 = (bf16[40,512]{1,0:T(8,128)(2,1)S(1)}, bf16[40,512]{1,0:T(8,128)(2,1)S(1)}, u32[]{:S(2)}, u32[]{:S(2)}) collective-permute-start(bf16[40,512]{1,0:T(8,128)(2,1)S(1)} %get-tuple-element.35), channel_id=1, source_target_pairs={{0,3},{1,2},{2,1},{3,0},{4,7},{5,6},{6,5},{7,4},{8,11},{9,10},{10,... | collective-permute-start | bytes 122888 | tf_op jit(solution)/shard_map/ppermute | solution.py:624
  7.7 5.4 %collective-permute-start.2 = (bf16[24,512]{1,0:T(8,128)(2,1)S(1)}, bf16[24,512]{1,0:T(8,128)(2,1)S(1)}, u32[]{:S(2)}, u32[]{:S(2)}) collective-permute-start(bf16[24,512]{1,0:T(8,128)(2,1)S(1)} %get-tuple-element.26.refs_5_.refs_0_), channel_id=1, source_target_pairs={{0,2},{1,3},{2,0},{3,1},{4,6},{5,7},{6,4},{7,5},{8,10},{9,11},{10,... | collective-permute-start | bytes 73736 | tf_op jit(solution)/shard_map/ppermute | solution.py:624
  11.5 5.2 %collective-permute-start.3 = (bf16[320,128]{1,0:T(8,128)(2,1)S(1)}, bf16[320,128]{1,0:T(8,128)(2,1)S(1)}, u32[]{:S(2)}, u32[]{:S(2)}) collective-permute-start(bf16[320,128]{1,0:T(8,128)(2,1)S(1)} %get-tuple-element.38), channel_id=1, source_target_pairs={{0,4},{4,0},{8,12},{12,8},{1,5},{5,1},{9,13},{13,9},{2,6},{6,2},{1... | collective-permute-start | bytes 245768 | tf_op jit(solution)/shard_map/ppermute | solution.py:657
  11.5 5.1 %collective-permute-start.4 = (bf16[320,128]{1,0:T(8,128)(2,1)S(1)}, bf16[320,128]{1,0:T(8,128)(2,1)S(1)}, u32[]{:S(2)}, u32[]{:S(2)}) collective-permute-start(bf16[320,128]{1,0:T(8,128)(2,1)S(1)} %get-tuple-element.39), channel_id=1, source_target_pairs={{0,12},{4,8},{8,4},{12,0},{1,13},{5,9},{9,5},{13,1},{2,14},{6,10},... | collective-permute-start | bytes 245768 | tf_op jit(solution)/shard_map/ppermute | solution.py:658
  14.5 6.1 %collective-permute-start.5 = (f32[16,1280]{1,0:T(8,128)S(1)}, f32[16,1280]{1,0:T(8,128)S(1)}, u32[]{:S(2)}, u32[]{:S(2)}) collective-permute-start(f32[16,1280]{1,0:T(8,128)S(1)} %get-tuple-element.43), channel_id=1, source_target_pairs={{0,4},{4,0},{8,12},{12,8},{1,5},{5,1},{9,13},{13,9},{2,6},{6,2},{1... | collective-permute-start | bytes 245768 | tf_op jit(solution)/shard_map/ppermute | solution.py:670
  14.6 6.0 %collective-permute-start.6 = (f32[16,1280]{1,0:T(8,128)S(1)}, f32[16,1280]{1,0:T(8,128)S(1)}, u32[]{:S(2)}, u32[]{:S(2)}) collective-permute-start(f32[16,1280]{1,0:T(8,128)S(1)} %get-tuple-element.44), channel_id=1, source_target_pairs={{0,12},{4,8},{8,4},{12,0},{1,13},{5,9},{9,5},{13,1},{2,14},{6,10},... | collective-permute-start | bytes 245768 | tf_op jit(solution)/shard_map/ppermute | solution.py:670
  15.7 5.4 %collective-permute-start.7 = (f32[16,1280]{1,0:T(8,128)S(1)}, f32[16,1280]{1,0:T(8,128)S(1)}, u32[]{:S(2)}, u32[]{:S(2)}) collective-permute-start(f32[16,1280]{1,0:T(8,128)S(1)} %get-tuple-element.45), channel_id=1, source_target_pairs={{0,8},{4,12},{8,0},{12,4},{1,9},{5,13},{9,1},{13,5},{2,10},{6,14},... | collective-permute-start | bytes 245768 | tf_op jit(solution)/shard_map/ppermute | solution.py:670
  16.7 4.4 %copy-start = (bf16[128,256]{1,0:T(8,128)(2,1)S(1)}, bf16[128,256]{1,0:T(8,128)(2,1)}, u32[]{:S(2)}) copy-start(bf16[128,256]{1,0:T(8,128)(2,1)} %refs_5_.1) | copy-start | bytes 196612
  16.7 4.4 %copy-start.1 = (bf16[256,128]{1,0:T(8,128)(2,1)S(1)}, bf16[256,128]{1,0:T(8,128)(2,1)}, u32[]{:S(2)}) copy-start(bf16[256,128]{1,0:T(8,128)(2,1)} %refs_6_.1) | copy-start | bytes 196612
  16.7 4.4 %copy-start.2 = (bf16[128]{0:T(256)(128)(2,1)S(1)}, bf16[128]{0:T(256)(128)(2,1)}, u32[]{:S(2)}) copy-start(bf16[128]{0:T(256)(128)(2,1)} %param.27) | copy-start | bytes 772
